TPU v7x, 32 devices: a whole 2x2x4 slice. The times are simulated.
32 devices in a mesh: wave: 8 (over z, x), grp: 4 (over y, core).
Axes of the slice: x: 2, y: 2, z: 4, core: 2. Of those that a mesh axis runs over, the one named last changes fastest.
Arguments:
- spectrum: float32 [1152, 16384], P('grp', 'wave'), may hold values from 0.2 to 2
- edge_vectors: float32 [2, 8, 16384], P(None, None, 'wave'), may hold values from -0.06 to 0.06
- neighbours: int32 [8, 16384], P(None, 'wave'), may hold values from 0 to 2303, as said below
- halo_lists: int32 [2, 8, 128], P(None, 'wave'), may hold values from 0 to 2047, as said below
- group_speed: float32 [32], P('grp'), may hold values from 0.5 to 1.5
- input_coef: float32 [32], P('grp'), may hold values from 0.3 to 1
- dissipation: float32 [32], P('grp'), may hold values from 0.05 to 0.5
- friction: float32 [16384], P('wave'), may hold values from 0.1 to 1
- wind_dir: float32 [16384], P('wave'), may hold values from -3.140625 to 3.140625
- drift_kernel: float32 [40, 1152], P(None, 'grp'), may hold values from -0.1875 to 0.1875
- block_tile: int32 [256], P('wave'), may hold values from 0 to 31, as said below
- block_weights: float32 [256, 64, 512], P('wave'), may hold values from -0.75 to 0.75
Outputs:
- updated: float32 [1152, 16384], P('grp', 'wave')
- drift: float32 [32, 40, 512], P('wave', None, 'grp')
Inputs may be any that keep to these rules, and one draw needn't show every extreme that they name: `neighbours`: entry [n, j] indexes the extended points of point j's partition: below 2048 one of its own points, then the 128 points from the previous partition, then the 128 from the next; a padding entry is the point's own index j % 2048. `halo_lists`: local indices of a partition's own points; repeats are allowed. `block_tile`: block b lies on partition b // 32; tile t belongs to partition t // 4. The 32 blocks of one partition feed the tiles of any one partition at most 8 times, and in every draw one partition receives exactly 8 blocks from every partition.
All inputs are finite; a program needn't handle non-finite values.
Results may differ from a plain program's by a relative error of at most 0.000071.
Values sent between devices are 32-bit elements; how exact they have to be, the bound alone decides.
No kernel may reach another device: no remote copies, remote signals or barrier semaphores. Data moves between devices by JAX's collectives and lax.ppermute only.
A program may use at most 128 MiB of HBM per device.

v0:
```python
import math

import jax
import jax.numpy as jnp
from jax import lax
from jax.sharding import PartitionSpec as P

ND = 36
TPW = 4


def from_behind(value, axis, steps):
    count = lax.axis_size(axis)
    leading, last = (max(0, -steps), min(count, count - steps))
    return lax.ppermute(value, axis, [(source, source + steps) for source in range(leading, last)])


def direction_tables(bins):
    theta = jnp.arange(ND, dtype=jnp.float32) * (2.0 * math.pi / ND)
    repeats = bins // ND
    return (jnp.tile(jnp.cos(theta), repeats), jnp.tile(jnp.sin(theta), repeats))


def advance(
    spectrum,
    extended,
    edge_vectors,
    neighbours,
    speed_bins,
    coef_bins,
    loss_bins,
    friction,
    wind_dir,
    cos_bins,
    sin_bins,
):
    along_x = (speed_bins * cos_bins)[:, None]
    along_y = (speed_bins * sin_bins)[:, None]
    inflow_sum = jnp.zeros(spectrum.shape, jnp.float32)
    for column in range(neighbours.shape[0]):
        projected = (
            along_x * edge_vectors[0, column][None, :] + along_y * edge_vectors[1, column][None, :]
        )
        inflow = jnp.maximum(-projected, 0.0)
        upwind = jnp.take(extended, neighbours[column], axis=1)
        inflow_sum = inflow_sum + inflow * (upwind - spectrum)
    advected = spectrum + inflow_sum
    facing = jnp.maximum(
        cos_bins[:, None] * jnp.cos(wind_dir)[None, :]
        + sin_bins[:, None] * jnp.sin(wind_dir)[None, :],
        0.0,
    )
    growth = coef_bins[:, None] * friction[None, :] * facing - loss_bins[:, None]
    return advected * jnp.exp(growth)


def body(
    spectrum,
    edge_vectors,
    neighbours,
    halo_lists,
    group_speed,
    input_coef,
    dissipation,
    friction,
    wind_dir,
    drift_kernel,
    block_tile,
    block_weights,
):
    bins = spectrum.shape[0]
    cos_bins, sin_bins = direction_tables(bins)
    speed_bins = jnp.repeat(group_speed, ND)
    coef_bins = jnp.repeat(input_coef, ND)
    loss_bins = jnp.repeat(dissipation, ND)
    to_next = jnp.take(spectrum, halo_lists[0, 0], axis=1)
    to_prev = jnp.take(spectrum, halo_lists[1, 0], axis=1)
    from_prev = from_behind(to_next, "wave", 1)
    from_next = from_behind(to_prev, "wave", -1)
    extended = jnp.concatenate([spectrum, from_prev, from_next], axis=1)
    updated = advance(
        spectrum,
        extended,
        edge_vectors,
        neighbours,
        speed_bins,
        coef_bins,
        loss_bins,
        friction,
        wind_dir,
        cos_bins,
        sin_bins,
    )
    drift_part = jnp.dot(
        drift_kernel, updated, precision=lax.Precision.HIGHEST, preferred_element_type=jnp.float32
    )
    n_wave = lax.axis_size("wave")
    n_group = lax.axis_size("grp")
    blocks = block_tile.shape[0]
    block_rows = block_weights.shape[1]
    tile_cells = block_weights.shape[2]
    depth_rows = drift_kernel.shape[0]
    group_cells = tile_cells // n_group
    local_tile = block_tile % TPW
    owner = block_tile // TPW
    per_block = drift_part.reshape(depth_rows, blocks, block_rows)
    shaped = block_weights.reshape(blocks, block_rows, n_group, group_cells)
    terms = jnp.einsum("zbj,bjgc->bgzc", per_block, shaped, precision=lax.Precision.HIGHEST)
    arranged = (
        jnp.zeros((n_wave, n_group, TPW, depth_rows, group_cells), jnp.float32)
        .at[owner, :, local_tile]
        .add(terms)
    )
    arranged = arranged.reshape(n_wave * n_group * TPW, depth_rows, group_cells)
    drift = lax.psum_scatter(arranged, ("wave", "grp"), scatter_dimension=0, tiled=True)
    return (updated, drift)


def solution(mesh):
    in_specs = (
        P("grp", "wave"),
        P(None, None, "wave"),
        P(None, "wave"),
        P(None, "wave", None),
        P("grp"),
        P("grp"),
        P("grp"),
        P("wave"),
        P("wave"),
        P(None, "grp"),
        P("wave"),
        P("wave", None, None),
    )
    out_specs = (P("grp", "wave"), P("wave", None, "grp"))
    return jax.shard_map(body, mesh=mesh, in_specs=in_specs, out_specs=out_specs, check_vma=False)
```

profile of v0, /device:TPU:0, one launch (start us, length us, event | category | flops | bytes accessed | tf_op | source)
XLA Modules:
  0.0 302.9 jit_solution(71335819527606106)
XLA Ops:
  7.2 0.7 compare_and_fusion.9
  7.9 2.2 copy.31
  10.2 0.8 gather_fusion
  10.9 0.8 select_bitcast_fusion.1
  11.7 5.5 %collective-permute-start = (f32[288,128]{0,1:T(8,128)}, f32[288,128]{0,1:T(8,128)}, u32[]{:S(2)}, u32[]{:S(2)}) collective-permute-start(f32[288,128]{0,1:T(8,128)} %select_bitcast_fusion.1), channel_id=1, source_target_pairs={{0,4},{4,8},{8,12},{12,16},{16,20},{20,24},{24,28},{1,5},{5,9},{9,... | collective-permute-start | bytes 442376 | tf_op jit(solution)/shard_map/ppermute | solution.py:15
  17.2 0.8 gather_fusion.1
  18.0 0.8 select_bitcast_fusion
  18.7 1.3 collective-permute-start.1
  20.0 1.3 fusion.39
  21.3 0.6 compare_and_fusion
  22.0 0.6 fusion.28
  22.6 0.6 fusion.29
  23.7 0.6 fusion.26
  24.9 0.6 compare_and_fusion.4
  26.1 0.6 fusion.25
  26.8 0.6 compare_and_fusion.6
  27.4 0.6 fusion.36
  28.0 0.7 fusion.38
  28.9 0.7 tile.28
  29.6 0.7 broadcast_in_dim.41
  30.4 0.7 fusion.40
  31.2 0.7 broadcast_in_dim.42
  32.0 0.7 broadcast_in_dim.43
  32.8 0.7 fusion.35
  33.5 2.9 pad_maximum_fusion
  36.4 9.2 %gather_fusion.2 = f32[2048,288]{1,0:T(8,128)S(1)} fusion(f32[288,2304]{0,1:T(8,128)} %pad_maximum_fusion, s32[2048]{0:T(1024)S(1)} %copy-done.9), kind=kCustom, calls=%fused_computation.1.clone | custom fusion | bytes 4726784 | tf_op jit(solution)/shard_map/jit(_take)/gather | solution.py:45
  45.6 2.2 copy.32
  47.8 9.2 %gather_fusion.3 = f32[2048,288]{1,0:T(8,128)S(1)} fusion(f32[288,2304]{0,1:T(8,128)} %pad_maximum_fusion, s32[2048]{0:T(1024)S(1)} %copy-done.8), kind=kCustom, calls=%fused_computation.3.clone | custom fusion | bytes 4726784 | tf_op jit(solution)/shard_map/jit(_take)/gather | solution.py:45
  57.0 2.2 copy.33
  59.2 9.2 %gather_fusion.4 = f32[2048,288]{1,0:T(8,128)S(1)} fusion(f32[288,2304]{0,1:T(8,128)} %pad_maximum_fusion, s32[2048]{0:T(1024)S(1)} %copy-done.7), kind=kCustom, calls=%fused_computation.4.clone | custom fusion | bytes 4726784 | tf_op jit(solution)/shard_map/jit(_take)/gather | solution.py:45
  68.4 2.2 copy.34
  70.6 9.2 %gather_fusion.5 = f32[2048,288]{1,0:T(8,128)S(1)} fusion(f32[288,2304]{0,1:T(8,128)} %pad_maximum_fusion, s32[2048]{0:T(1024)S(1)} %copy-done.6), kind=kCustom, calls=%fused_computation.5.clone | custom fusion | bytes 4726784 | tf_op jit(solution)/shard_map/jit(_take)/gather | solution.py:45
  79.8 2.2 copy.35
  82.0 9.2 %gather_fusion.6 = f32[2048,288]{1,0:T(8,128)S(1)} fusion(f32[288,2304]{0,1:T(8,128)} %pad_maximum_fusion, s32[2048]{0:T(1024)S(1)} %copy-done.5), kind=kCustom, calls=%fused_computation.6.clone | custom fusion | bytes 4726784 | tf_op jit(solution)/shard_map/jit(_take)/gather | solution.py:45
  91.2 2.2 copy.36
  93.4 9.2 %gather_fusion.7 = f32[2048,288]{1,0:T(8,128)S(1)} fusion(f32[288,2304]{0,1:T(8,128)} %pad_maximum_fusion, s32[2048]{0:T(1024)S(1)} %copy-done.4), kind=kCustom, calls=%fused_computation.7.clone | custom fusion | bytes 4726784 | tf_op jit(solution)/shard_map/jit(_take)/gather | solution.py:45
  102.6 2.1 copy.37
  104.7 9.2 %gather_fusion.8 = f32[2048,288]{1,0:T(8,128)S(1)} fusion(f32[288,2304]{0,1:T(8,128)} %pad_maximum_fusion, s32[2048]{0:T(1024)S(1)} %fusion.30), kind=kCustom, calls=%fused_computation.8.clone | custom fusion | bytes 4726784 | tf_op jit(solution)/shard_map/jit(_take)/gather | solution.py:45
  114.0 2.1 copy.38
  116.1 9.2 %gather_fusion.9 = f32[2048,288]{1,0:T(8,128)S(1)} fusion(f32[288,2304]{0,1:T(8,128)} %pad_maximum_fusion, s32[2048]{0:T(1024)S(1)} %fusion.31), kind=kCustom, calls=%fused_computation.9.clone | custom fusion | bytes 4726784 | tf_op jit(solution)/shard_map/jit(_take)/gather | solution.py:45
  125.5 2.1 copy.39
  127.9 10.8 %fusion.6 = f32[288,2048]{1,0:T(8,128)S(1)} fusion(f32[288,2048]{1,0:T(8,128)} %param.16, f32[2048,288]{0,1:T(8,128)} %copy.39, f32[2048,288]{0,1:T(8,128)} %copy.38, f32[2048,288]{0,1:T(8,128)} %copy.37, f32[2048,288]{0,1:T(8,128)} %copy.36, f32[2048,288]{0,1:T(8,128)} %copy.35, f32[2048,288]{0,1:T(8,128)} %copy.34, f32[2048,288]{0,1:T(8,128)} %copy.33, ...), kind=kLoop, calls=%fused_computation.19 | loop fusion | flops 47185920 | bytes 23771904 | tf_op jit(solution)/shard_map/mul | solution.py:54
  138.7 1.4 copy-done.2
  140.1 1.7 convolution_bitcast_fusion
  142.1 6.5 %fusion.20 = f32[32,4,40,128]{3,2,1,0:T(8,128)} fusion(f32[40,32,64,1]{2,1,0,3:T(8,128)S(1)} %bitcast.130, f32[32,64,512]{2,1,0:T(8,128)} %param.27), kind=kOutput, calls=%fused_computation.41 | convolution fusion | flops 503316480 | bytes 7143424 | tf_op jit(solution)/shard_map/zbj,bjgc->bgzc/dot_general | solution.py:108
  148.9 5.9 %scatter_fusion = f32[8,4,4,40,128]{4,3,2,1,0:T(8,128)S(1)} fusion(f32[8,4,4,40,128]{4,3,2,1,0:T(8,128)S(1)} %broadcast_in_dim.44, s32[32]{0:T(128)S(1)} %fusion.35, f32[32,4,40,128]{3,2,1,0:T(8,128)} %fusion.20), kind=kCustom, calls=%fused_computation.10 | custom fusion | flops 655360 | bytes 7864576 | tf_op jit(solution)/shard_map/scatter-add | solution.py:112
  154.9 1.5 copy-done.1
  156.3 139.7 %reduce-scatter.2.cloned.1.call-done = f32[4,40,128]{2,1,0:T(8,128)} async-done(((f32[128,40,128]{2,1,0:T(8,128)}), f32[4,40,128]{2,1,0:T(8,128)}) %reduce-scatter.2.cloned.1.call-update) | async-done | bytes 81936 | tf_op jit(solution)/shard_map/reduce_scatter | solution.py:115
  (89 shorter events, 3.0 us)
Async XLA Ops:
  7.2 132.9 %copy-start = (f32[40,288]{1,0:T(8,128)S(1)}, f32[40,288]{1,0:T(8,128)}, u32[]{:S(2)}) copy-start(f32[40,288]{1,0:T(8,128)} %param.25) | copy-start | bytes 138244
  7.2 288.9 %reduce-scatter.2.cloned.1.call-start = ((), (), s32[]{:S(2)}) async-start(), calls=%async_computation.1 | async-start | bytes 2703360 | tf_op jit(solution)/shard_map/reduce_scatter | solution.py:115
  10.2 17.9 %copy-start.3 = (f32[2,8,2048]{2,1,0:T(8,128)S(1)}, f32[2,8,2048]{2,1,0:T(8,128)}, u32[]{:S(2)}) copy-start(f32[2,8,2048]{2,1,0:T(8,128)} %param.17) | copy-start | bytes 393220
  11.7 21.8 %collective-permute-start = (f32[288,128]{0,1:T(8,128)}, f32[288,128]{0,1:T(8,128)}, u32[]{:S(2)}, u32[]{:S(2)}) collective-permute-start(f32[288,128]{0,1:T(8,128)} %select_bitcast_fusion.1), channel_id=1, source_target_pairs={{0,4},{4,8},{8,12},{12,16},{16,20},{20,24},{24,28},{1,5},{5,9},{9,... | collective-permute-start | bytes 442376 | tf_op jit(solution)/shard_map/ppermute | solution.py:15
  18.7 14.8 %collective-permute-start.1 = (f32[288,128]{0,1:T(8,128)}, f32[288,128]{0,1:T(8,128)S(1)}, u32[]{:S(2)}, u32[]{:S(2)}) collective-permute-start(f32[288,128]{0,1:T(8,128)} %select_bitcast_fusion), channel_id=1, source_target_pairs={{4,0},{8,4},{12,8},{16,12},{20,16},{24,20},{28,24},{5,1},{9,5},{13... | collective-permute-start | bytes 442376 | tf_op jit(solution)/shard_map/ppermute | solution.py:15
  33.5 2.9 copy-start.9
  45.6 2.2 copy-start.8
  57.0 2.2 copy-start.7
  68.4 2.2 copy-start.6
  79.8 2.2 copy-start.5
  91.2 2.2 copy-start.4
  125.3 2.4 copy-start.10
  125.3 2.4 copy-start.11
  125.3 2.4 copy-start.12
  125.3 2.4 copy-start.13
  125.3 2.4 copy-start.14
  125.3 2.4 copy-start.15
  125.4 2.4 copy-start.16
  125.4 2.4 copy-start.17
  125.4 2.4 copy-start.18
  125.4 2.4 copy-start.19
  125.4 2.4 copy-start.20
  125.4 2.4 copy-start.21
  125.4 2.4 copy-start.22
  125.4 2.4 copy-start.23
  125.4 2.4 copy-start.24
  125.4 2.4 copy-start.25
  125.5 2.4 copy-start.26
  125.5 2.4 copy-start.27
  125.5 2.4 copy-start.28
  125.5 2.4 copy-start.29
  125.5 2.4 copy-start.30
  125.5 2.4 copy-start.31
  125.5 2.4 copy-start.32
  125.5 2.4 copy-start.33
  125.5 2.4 copy-start.34
  138.7 1.4 copy-start.2
  154.8 1.5 copy-start.1
Sparse Core Ops, SparseCore 0:
  156.5 139.5 reduce-scatter.1
where the time goes:
time: 304 us; the launch traced here: 303 us
  waiting for transfers between devices  140 us (46%)
  local copies, waits for them, and re-layouts  104 us (34%)
  other arithmetic  29.2 us (10%)
  between operations  14.7 us (5%)
  matrix products  8.25 us (3%)
  starting transfers between devices  6.82 us (2%)
    reduce_scatter x1, waiting for transfers between devices, body(): lax.psum_scatter(arranged, ('wave', 'grp'), scatter_dimension=0, tiled=True)  140 us
    gather x16, local copies, waits for them, and re-layouts, advance(): upwind = jnp.take(extended, neighbours[column], axis=1)  90.9 us
    mul x1, other arithmetic, advance(): return advected * jnp.exp(growth)  10.8 us
    ppermute x2, starting transfers between devices, from_behind(): lax.ppermute(value, axis, [(source, source + steps) for source in range(l...  6.79 us
    dot_general x1, matrix products, body(): jnp.einsum('zbj,bjgc->bgzc', per_block, shaped, precision=lax.Precision.H...  6.51 us
  transfers between devices with their start and end apart: 3, of which 1 were waited for; matrix products, arithmetic and copies ran while one was open for 5% of the time, Pallas kernels for 0%

commit v1 on v0

v1 whole, which is shorter than its diff:
```python
import functools
import math

import jax
import jax.numpy as jnp
import ml_dtypes
import numpy as np
from jax import lax
from jax.experimental import pallas as pl
from jax.experimental.pallas import tpu as pltpu
from jax.sharding import PartitionSpec as P

ND = 36
TPW = 4
LANES = 128
PAIR = 2 * ND
BF = jnp.bfloat16
F32 = jnp.float32
VMEM = pl.BlockSpec(memory_space=pltpu.VMEM)
SMEM = pl.BlockSpec(memory_space=pltpu.SMEM)
ANY = pl.BlockSpec(memory_space=pl.ANY)


def params(mib):
    return pltpu.CompilerParams(vmem_limit_bytes=mib << 20)


def split2(x):
    high = x.astype(BF)
    return high, (x - high.astype(F32)).astype(BF)


def dot(a, b):
    return jnp.dot(a, b, preferred_element_type=F32)


def direction_constants(slots):
    theta = np.arange(ND) * (2.0 * math.pi / ND)
    cosine, sine = np.cos(theta), np.sin(theta)
    table = np.zeros((2, slots, slots, LANES), np.float32)
    for slot in range(slots):
        for half in range(2):
            table[0, slot, slot, half * ND : (half + 1) * ND] = -cosine
            table[1, slot, slot, half * ND : (half + 1) * ND] = -sine
    table = table.reshape(2 * slots, slots * LANES)
    high = table.astype(ml_dtypes.bfloat16)
    low = (table - high.astype(np.float32)).astype(ml_dtypes.bfloat16)
    rows = np.stack([np.tile(cosine, 2), np.tile(sine, 2)]).astype(np.float32)
    facing = np.broadcast_to(rows[:, :, None], (2, PAIR, LANES))
    return np.concatenate([high, low, high], 0), np.ascontiguousarray(facing)


def halo_kernel(lists_ref, spec_ref, next_ref, prev_ref):
    points = spec_ref.shape[1]
    step = 256
    totals = [None, None]
    for start in range(0, points, step):
        high, rest = spec_ref[:, start : start + step], None
        first = high.astype(BF)
        rest = high - first.astype(F32)
        second = rest.astype(BF)
        third = (rest - second.astype(F32)).astype(BF)
        ids = lax.broadcasted_iota(jnp.int32, (step, LANES), 0) + start
        for side in range(2):
            chosen = jnp.where(ids == lists_ref[side], 1.0, 0.0).astype(BF)
            part = dot(first, chosen) + dot(second, chosen) + dot(third, chosen)
            totals[side] = part if totals[side] is None else totals[side] + part
    next_ref[...] = totals[0]
    prev_ref[...] = totals[1]


def pick_halo(spectrum, lists):
    bins = spectrum.shape[0]
    shape = jax.ShapeDtypeStruct((bins, lists.shape[-1]), F32)
    return pl.pallas_call(
        halo_kernel,
        in_specs=[VMEM, VMEM],
        out_specs=[VMEM, VMEM],
        out_shape=[shape, shape],
        compiler_params=params(40),
    )(lists, spectrum)


def advance_kernel(
    index_ref,
    speed_ref,
    coef_ref,
    loss_ref,
    spec_ref,
    prev_ref,
    next_ref,
    edge_ref,
    air_ref,
    weight_ref,
    facing_ref,
    kernel_ref,
    updated_ref,
    stokes_ref,
    table,
    inflow,
    gathered,
    result,
    sems,
    *,
    unroll,
):
    bins, points = spec_ref.shape
    groups = bins // PAIR
    slots = edge_ref.shape[0] // 2
    halo = prev_ref.shape[1]
    blocks = points // LANES
    filler = jnp.zeros((LANES - PAIR, LANES), F32)

    def place(x, group, block):
        rows = pl.ds(block * (LANES * groups) + group, LANES, stride=groups)
        table[rows, :] = jnp.concatenate([x, filler], 0).T

    @pl.loop(0, blocks)
    def _(block):
        columns = pl.ds(pl.multiple_of(block * LANES, LANES), LANES)
        for group in range(groups):
            place(spec_ref[group * PAIR : (group + 1) * PAIR, columns], group, block)

    for group in range(groups):
        rows = slice(group * PAIR, (group + 1) * PAIR)
        place(prev_ref[rows, :], group, blocks)
        place(next_ref[rows, :], group, blocks + halo // LANES)

    kernel_high, kernel_low = split2(kernel_ref[...])
    kernel_both = jnp.concatenate([kernel_high, kernel_low], 0)
    depth = kernel_ref.shape[0]

    def copy_out(block):
        columns = pl.ds(pl.multiple_of(block * LANES, LANES), LANES)
        return pltpu.make_async_copy(
            result.at[block], updated_ref.at[:, columns], sems.at[block]
        )

    @pl.loop(0, blocks)
    def _(block):
        base = pl.multiple_of(block * LANES, LANES)
        columns = pl.ds(base, LANES)
        edge_high, edge_low = split2(edge_ref[:, columns])
        left = jnp.concatenate([edge_high, edge_high, edge_low], 0)
        weights = lax.dot_general(
            left, weight_ref[...], (((0,), (0,)), ((), ())), preferred_element_type=F32
        )
        for slot in range(slots):
            inflow[slot, :LANES, :] = jnp.maximum(weights[:, slot * LANES : (slot + 1) * LANES], 0.0)

        @pl.loop(0, LANES // unroll)
        def _(chunk):
            first = pl.multiple_of(chunk * unroll, unroll)
            for u in range(unroll):
                point = first + u
                picks = index_ref.at[pl.ds((base + point) * slots, slots)]
                own = table[pl.ds((base + point) * groups, groups), :]
                terms = []
                for slot in range(slots):
                    upwind = table[pl.ds(picks[slot], groups), :]
                    factor = inflow[slot, pl.ds(point, groups, stride=0), :]
                    terms.append(factor * (upwind - own))
                while len(terms) > 1:
                    terms = [a + b for a, b in zip(terms[::2], terms[1::2])]
                gathered[pl.ds(point * groups, groups), :] = terms[0]

        cos_wind = air_ref[0:1, columns]
        sin_wind = air_ref[1:2, columns]
        friction = air_ref[2:3, columns]
        facing = jnp.maximum(facing_ref[0] * cos_wind + facing_ref[1] * sin_wind, 0.0)
        pushed = facing * friction
        lower = lax.broadcasted_iota(jnp.int32, (PAIR, LANES), 0) < ND

        def per_bin(ref, group):
            return jnp.where(lower, ref[2 * group], ref[2 * group + 1])

        for group in range(groups):
            rows = slice(group * PAIR, (group + 1) * PAIR)
            change = gathered[pl.ds(group, LANES, stride=groups), :].T[:PAIR]
            advected = spec_ref[rows, columns] + per_bin(speed_ref, group) * change
            growth = per_bin(coef_ref, group) * pushed - per_bin(loss_ref, group)
            result[block, rows, :] = advected * jnp.exp(growth)
        copy_out(block).start()
        high, low = split2(result[block])
        both = dot(kernel_both, high)
        stokes_ref[:, columns] = both[:depth] + both[depth:] + dot(kernel_high, low)

    @pl.loop(0, blocks)
    def _(block):
        copy_out(block).wait()


def advance(index, speed, coef, loss, spectrum, prev, nxt, edges, air, kernel):
    bins, points = spectrum.shape
    slots = edges.shape[0] // 2
    groups = bins // PAIR
    weight, facing = direction_constants(slots)
    rows = (points + prev.shape[1] + nxt.shape[1]) * groups
    return pl.pallas_call(
        functools.partial(advance_kernel, unroll=16),
        in_specs=[SMEM] * 4 + [VMEM] * 8,
        out_specs=[ANY, VMEM],
        out_shape=[
            jax.ShapeDtypeStruct((bins, points), F32),
            jax.ShapeDtypeStruct((kernel.shape[0], points), F32),
        ],
        scratch_shapes=[
            pltpu.VMEM((rows + 8, LANES), F32),
            pltpu.VMEM((slots, LANES + 8, LANES), F32),
            pltpu.VMEM((LANES * groups, LANES), F32),
            pltpu.VMEM((points // LANES, bins, LANES), F32),
            pltpu.SemaphoreType.DMA((points // LANES,)),
        ],
        compiler_params=params(40),
    )(index, speed, coef, loss, spectrum, prev, nxt, edges, air, weight, facing, kernel)


def regrid_kernel(slot_ref, stokes_ref, high_ref, low_ref, out_ref, *, block_rows):
    depth = stokes_ref.shape[0]
    out_ref[...] = jnp.zeros(out_ref.shape, F32)
    lower = lax.broadcasted_iota(jnp.int32, (depth, LANES), 1) < block_rows
    for pair in range(stokes_ref.shape[1] // LANES):
        columns = slice(pair * LANES, (pair + 1) * LANES)
        part = stokes_ref[:, columns]
        both = jnp.concatenate([jnp.where(lower, part, 0.0), jnp.where(lower, 0.0, part)], 0)
        high, low = split2(both)
        terms = (
            dot(high, high_ref[columns, :])
            + dot(low, high_ref[columns, :])
            + dot(high, low_ref[columns, :])
        )
        for half in range(2):
            slot = slot_ref[2 * pair + half]
            out_ref[slot] = out_ref[slot] + terms[half * depth : (half + 1) * depth]


def regrid(slots, stokes, high, low, count, block_rows):
    depth = stokes.shape[0]
    return pl.pallas_call(
        functools.partial(regrid_kernel, block_rows=block_rows),
        in_specs=[SMEM, VMEM, VMEM, VMEM],
        out_specs=VMEM,
        out_shape=jax.ShapeDtypeStruct((count, depth, LANES), F32),
        compiler_params=params(30),
    )(slots, stokes, high, low)


def swap(value, axis, bit):
    count = lax.axis_size(axis)
    return lax.ppermute(value, axis, [(i, i ^ bit) for i in range(count)])


def sum_over(value, axis):
    count = lax.axis_size(axis)
    me = lax.axis_index(axis)
    half = value.shape[1] // 2
    odd = (me & 1) == 1
    left, right = value[:, :half], value[:, half:]
    mine = jnp.where(odd, right, left) + swap(jnp.where(odd, left, right), axis, 1)
    bit = 2
    while bit < count:
        mine = mine + swap(mine, axis, bit)
        bit *= 2
    other = swap(mine, axis, 1)
    return jnp.concatenate([jnp.where(odd, other, mine), jnp.where(odd, mine, other)], 1)


def scatter_sum(parts, axis, bits):
    count = parts.shape[0]
    rest = parts.reshape((2,) * len(bits) + parts.shape[1:])
    for position, bit in enumerate(bits):
        live = sorted(bits[position:], reverse=True)
        dimension = live.index(bit)
        keep = lax.index_in_dim(rest, 0, dimension, keepdims=False)
        send = lax.index_in_dim(rest, 1, dimension, keepdims=False)
        rest = keep + swap(send, axis, bit)
    return rest


def shift(value, axis, steps):
    count = lax.axis_size(axis)
    leading, last = (max(0, -steps), min(count, count - steps))
    return lax.ppermute(value, axis, [(source, source + steps) for source in range(leading, last)])


def body(
    spectrum,
    edge_vectors,
    neighbours,
    halo_lists,
    group_speed,
    input_coef,
    dissipation,
    friction,
    wind_dir,
    drift_kernel,
    block_tile,
    block_weights,
):
    n_wave = lax.axis_size("wave")
    n_group = lax.axis_size("grp")
    to_next, to_prev = pick_halo(spectrum, halo_lists)
    from_prev = shift(to_next, "wave", 1)
    from_next = shift(to_prev, "wave", -1)
    slots = neighbours.shape[0]
    groups = spectrum.shape[0] // PAIR
    index = (neighbours * groups).T.reshape(-1)
    air = jnp.stack([jnp.cos(wind_dir), jnp.sin(wind_dir), friction])
    edges = edge_vectors.reshape(2 * slots, -1)
    updated, stokes = advance(
        index, group_speed, input_coef, dissipation, spectrum, from_prev, from_next, edges, air, drift_kernel
    )
    stokes = sum_over(stokes, "grp")
    blocks, block_rows, tile_cells = block_weights.shape
    cells = tile_cells // n_group
    mine = lax.dynamic_slice_in_dim(block_weights, lax.axis_index("grp") * cells, cells, 2)
    mine = mine.reshape(blocks * block_rows, cells)
    rounded = lax.reduce_precision(mine, 8, 7)
    high, low = rounded.astype(BF), (mine - rounded).astype(BF)
    relative = (block_tile // TPW) ^ lax.axis_index("wave")
    depth = drift_kernel.shape[0]
    parts = regrid(relative * TPW + block_tile % TPW, stokes, high, low, n_wave * TPW, block_rows)
    bits = [1 << b for b in range(n_wave.bit_length() - 1)]
    drift = scatter_sum(parts.reshape(n_wave, TPW, depth, cells), "wave", bits)
    return updated, drift


def solution(mesh):
    in_specs = (
        P("grp", "wave"),
        P(None, None, "wave"),
        P(None, "wave"),
        P(None, "wave", None),
        P("grp"),
        P("grp"),
        P("grp"),
        P("wave"),
        P("wave"),
        P(None, "grp"),
        P("wave"),
        P("wave", None, None),
    )
    out_specs = (P("grp", "wave"), P("wave", None, "grp"))
    return jax.shard_map(body, mesh=mesh, in_specs=in_specs, out_specs=out_specs, check_vma=False)
```

time: 304 us -> 77.7 us (0.26)
  waiting for transfers between devices: 140 us -> 22.4 us
  local copies, waits for them, and re-layouts: 104 us -> 7.47 us
  Pallas kernels: 0 us -> 29.9 us
  other arithmetic: 29.2 us -> 1.88 us
  between operations: 14.7 us -> 0.92 us
  matrix products: 8.25 us -> 0 us
  starting transfers between devices: 6.82 us -> 14.8 us
    reduce_scatter x1 -> x0, waiting for transfers between devices: 140 us -> none  [body(): lax.psum_scatter(arranged, ('wave', 'grp'), scatter_dimension=0, tiled=True)]
    gather x18 -> x0, local copies, waits for them, and re-layouts: 92.4 us -> none  [the longest x16 90.9 us: advance(): upwind = jnp.take(extended, neighbours[column], axis=1)]
    pallas_call x0 -> x3, Pallas kernels: none -> 29.9 us  [the longest x1 26.7 us: advance(): pl.pallas_call(functools.partial(advance_kernel, unroll=16), in_specs=[SM...]
    ppermute x2 -> x8, waiting for transfers between devices: 0.01 us -> 22.4 us  [the longest x6 21.1 us: swap(): return lax.ppermute(value, axis, [(i, i ^ bit) for i in range(count)])]
    mul x2 -> x0, other arithmetic: 10.8 us -> none  [the longest x1 10.8 us: advance(): return advected * jnp.exp(growth)]
    dot_general x2 -> x0, matrix products: 8.25 us -> none  [the longest x1 6.51 us: body(): jnp.einsum('zbj,bjgc->bgzc', per_block, shaped, precision=lax.Precision.H...]
    ppermute x2 -> x8, starting transfers between devices: 6.79 us -> 14.8 us  [the longest x6 8.66 us: swap(): return lax.ppermute(value, axis, [(i, i ^ bit) for i in range(count)])]
    scatter-add x1 -> x0, other arithmetic: 5.92 us -> none  [body(): arranged = jnp.zeros((n_wave, n_group, TPW, depth_rows, group_cells), jnp...]
  transfers between devices with their start and end apart: 3 -> 8, of which waited for: 1 -> 7; matrix products, arithmetic and copies ran while one was open for 5% -> 8% of each run, Pallas kernels for 0% -> 0%
where the time goes in v1:
time: 77.7 us; the launch traced here: 77.4 us
  Pallas kernels  29.9 us (38%)
  waiting for transfers between devices  22.4 us (29%)
  starting transfers between devices  14.8 us (19%)
  local copies, waits for them, and re-layouts  7.47 us (10%)
  other arithmetic  1.88 us (2%)
  between operations  0.92 us (1%)
    pallas_call x1, Pallas kernels, advance(): pl.pallas_call(functools.partial(advance_kernel, unroll=16), in_specs=[SM...  26.7 us
    ppermute x6, waiting for transfers between devices, swap(): return lax.ppermute(value, axis, [(i, i ^ bit) for i in range(count)])  21.1 us
    ppermute x6, starting transfers between devices, swap(): return lax.ppermute(value, axis, [(i, i ^ bit) for i in range(count)])  8.66 us
    ppermute x2, starting transfers between devices, shift(): lax.ppermute(value, axis, [(source, source + steps) for source in range(l...  6.15 us
    unnamed x25, local copies, waits for them, and re-layouts  2.4 us
    pallas_call x1, Pallas kernels, pick_halo(): pl.pallas_call(halo_kernel, in_specs=[VMEM, VMEM], out_specs=[VMEM, VMEM]...  2.04 us
    reshape x1, local copies, waits for them, and re-layouts, body(): index = (neighbours * groups).T.reshape(-1)  1.65 us
  transfers between devices with their start and end apart: 8, of which 7 were waited for; matrix products, arithmetic and copies ran while one was open for 8% of the time, Pallas kernels for 0%

profile of v1, /device:TPU:0, one launch (start us, length us, event | category | flops | bytes accessed | tf_op | source)
XLA Modules:
  0.0 77.4 jit_solution(17753205454248356345)
XLA Ops:
  0.6 0.0 copy-start
  0.6 1.7 %copy-done = f32[288,2048]{1,0:T(8,128)S(1)} copy-done((f32[288,2048]{1,0:T(8,128)S(1)}, f32[288,2048]{1,0:T(8,128)}, u32[]{:S(2)}) %copy-start) | copy-done | bytes 2359320
  2.3 0.0 copy-start.6
  2.3 0.7 copy-done.6
  3.0 0.0 copy-start.10
  3.0 0.0 copy-start.2
  3.0 0.0 copy-start.4
  3.0 0.0 copy-start.5
  3.0 0.0 copy-start.7
  3.0 0.0 copy-start.8
  3.0 0.0 copy-start.9
  3.0 2.0 %shard_map.149 = (f32[288,128]{1,0:T(8,128)S(1)}, f32[288,128]{1,0:T(8,128)S(1)}) custom-call(s32[2,1,128]{2,1,0:T(1,128)S(1)} %copy-done.6, f32[288,2048]{1,0:T(8,128)S(1)} %copy-done), custom_call_target="tpu_custom_call" | custom-call | tf_op jit(solution)/shard_map/pallas_call | solution.py:75
  5.1 4.9 %collective-permute-start = (f32[288,128]{1,0:T(8,128)S(1)}, f32[288,128]{1,0:T(8,128)S(1)}, u32[]{:S(2)}, u32[]{:S(2)}) collective-permute-start(f32[288,128]{1,0:T(8,128)S(1)} %get-tuple-element.6), channel_id=1, source_target_pairs={{0,4},{4,8},{8,12},{12,16},{16,20},{20,24},{24,28},{1,5},{5,9},{9,... | collective-permute-start | bytes 442376 | tf_op jit(solution)/shard_map/ppermute | solution.py:283
  10.0 1.3 %collective-permute-start.1 = (f32[288,128]{1,0:T(8,128)S(1)}, f32[288,128]{1,0:T(8,128)S(1)}, u32[]{:S(2)}, u32[]{:S(2)}) collective-permute-start(f32[288,128]{1,0:T(8,128)S(1)} %get-tuple-element.7), channel_id=1, source_target_pairs={{4,0},{8,4},{12,8},{16,12},{20,16},{24,20},{28,24},{5,1},{9,5},{13... | collective-permute-start | bytes 442376 | tf_op jit(solution)/shard_map/ppermute | solution.py:283
  11.3 0.7 fusion.6
  12.0 0.8 %multiply_bitcast_fusion = s32[2048,8]{0,1:T(8,128)S(1)} fusion(s32[8,2048]{1,0:T(8,128)} %param.16), kind=kLoop, calls=%fused_computation.17 | loop fusion | flops 16384 | bytes 131072 | tf_op jit(solution)/shard_map/transpose | solution.py:307
  12.9 1.3 %copy.18 = s32[2048,8]{1,0:T(8,128)} copy(s32[2048,8]{0,1:T(8,128)S(1)} %multiply_bitcast_fusion) | data formatting | bytes 131072 | tf_op jit(solution)/shard_map/transpose | solution.py:307
  14.2 1.6 %reshape.13.index_ref = s32[16384]{0:T(1024)S(1)} reshape(s32[2048,8]{1,0:T(8,128)} %copy.18) | data formatting | bytes 131072 | tf_op jit(solution)/shard_map/reshape | solution.py:307
  15.8 0.0 copy-done.10
  15.9 0.0 collective-permute-done.prev_ref
  15.9 1.3 %collective-permute-done.1.next_ref = f32[288,128]{1,0:T(8,128)S(1)} collective-permute-done((f32[288,128]{1,0:T(8,128)S(1)}, f32[288,128]{1,0:T(8,128)S(1)}, u32[]{:S(2)}, u32[]{:S(2)}) %collective-permute-start.1) | collective-permute-done | bytes 147488 | tf_op jit(solution)/shard_map/ppermute | solution.py:283
  17.1 0.0 copy-done.1
  17.1 0.0 copy-done.2
  17.2 0.0 copy-done.3
  17.2 0.0 copy-done.4
  17.2 0.0 copy-done.5
  17.2 0.0 copy-done.7
  17.2 0.0 copy-done.8
  17.2 0.0 copy-done.9
  17.2 0.0 copy-start.11
  17.2 26.7 %shard_map.150 = (f32[288,2048]{1,0:T(8,128)}, f32[40,2048]{1,0:T(8,128)S(1)}) custom-call(s32[16384]{0:T(1024)S(1)} %reshape.13.index_ref, f32[8]{0:T(128)S(1)} %copy-done.7, f32[8]{0:T(128)S(1)} %copy-done.8, f32[8]{0:T(128)S(1)} %copy-done.9, f32[288,2048]{1,0:T(8,128)S(1)} %copy-done.1, f32[288,128]{1,0:T(8,128)S(1)} %collective-permute-done.prev_ref, ...), custom_call_target="tpu_custom_call" | custom-call | tf_op jit(solution)/shard_map/pallas_call | solution.py:199
  43.9 0.1 collective-permute-start.2
  44.0 1.3 %constant_dynamic-slice_fusion = f32[32,64,128]{2,1,0:T(8,128)S(1)} fusion(f32[32,64,512]{2,1,0:T(8,128)} %param.25, s32[]{:T(128)S(6)} %select_n.42), kind=kLoop, calls=%fused_computation.25 | loop fusion | bytes 2097156 | tf_op jit(solution)/shard_map/dynamic_slice | solution.py:316
  45.3 0.1 collective-permute-done.2
  45.4 1.6 %collective-permute-start.3 = (f32[40,1024]{1,0:T(8,128)S(1)}, f32[40,1024]{1,0:T(8,128)S(1)}, u32[]{:S(2)}, u32[]{:S(2)}) collective-permute-start(f32[40,1024]{1,0:T(8,128)S(1)} %select_add_fusion), channel_id=1, source_target_pairs={{0,2},{1,3},{2,0},{3,1},{4,6},{5,7},{6,4},{7,5},{8,10},{9,11},{10,... | collective-permute-start | bytes 491528 | tf_op jit(solution)/shard_map/ppermute | solution.py:250
  47.0 0.2 fusion
  47.2 4.8 %collective-permute-done.3 = f32[40,1024]{1,0:T(8,128)S(1)} collective-permute-done((f32[40,1024]{1,0:T(8,128)S(1)}, f32[40,1024]{1,0:T(8,128)S(1)}, u32[]{:S(2)}, u32[]{:S(2)}) %collective-permute-start.3) | collective-permute-done | bytes 163872 | tf_op jit(solution)/shard_map/ppermute | solution.py:250
  52.1 0.1 collective-permute-start.4
  52.1 0.0 copy-done.11
  52.2 1.4 %collective-permute-done.4 = f32[40,1024]{1,0:T(8,128)S(1)} collective-permute-done((f32[40,1024]{1,0:T(8,128)S(1)}, f32[40,1024]{1,0:T(8,128)S(1)}, u32[]{:S(2)}, u32[]{:S(2)}) %collective-permute-start.4) | collective-permute-done | bytes 163872 | tf_op jit(solution)/shard_map/ppermute | solution.py:250
  53.6 1.2 %shard_map.151 = f32[32,40,128]{2,1,0:T(8,128)S(1)} custom-call(s32[32]{0:T(128)S(1)} %fusion.4.slot_ref, f32[40,2048]{1,0:T(8,128)S(1)} %pad_maximum_fusion.stokes_ref, bf16[2048,128]{1,0:T(8,128)(2,1)S(1)} %get-tuple-element.11.high_ref, bf16[2048,128]{1,0:T(8,128)(2,1)S(1)} %get-tuple-element.10.low_ref), custom_call_target="tpu_custom_call" | custom-call | tf_op jit(solution)/shard_map/pallas_call | solution.py:239
  54.9 2.5 %collective-permute-start.5 = (f32[2,2,4,40,128]{4,3,2,0,1:T(8,128)S(1)}, f32[2,2,4,40,128]{4,3,2,0,1:T(8,128)S(1)}, u32[]{:S(2)}, u32[]{:S(2)}) collective-permute-start(f32[2,2,4,40,128]{4,3,2,0,1:T(8,128)S(1)} %bitcast.31), channel_id=1, source_target_pairs={{0,4},{4,0},{8,12},{12,8},{16,20},{20,16},{24,28},{28,24},{1,5},{5... | collective-permute-start | bytes 983048 | tf_op jit(solution)/shard_map/ppermute | solution.py:250
  57.4 8.0 %collective-permute-done.5 = f32[2,2,4,40,128]{4,3,2,0,1:T(8,128)S(1)} collective-permute-done((f32[2,2,4,40,128]{4,3,2,0,1:T(8,128)S(1)}, f32[2,2,4,40,128]{4,3,2,0,1:T(8,128)S(1)}, u32[]{:S(2)}, u32[]{:S(2)}) %collective-permute-start.5) | collective-permute-done | bytes 327712 | tf_op jit(solution)/shard_map/ppermute | solution.py:250
  65.5 1.8 %collective-permute-start.6 = (f32[2,4,40,128]{3,2,1,0:T(8,128)S(1)}, f32[2,4,40,128]{3,2,1,0:T(8,128)S(1)}, u32[]{:S(2)}, u32[]{:S(2)}) collective-permute-start(f32[2,4,40,128]{3,2,1,0:T(8,128)S(1)} %slice_bitcast_fusion), channel_id=1, source_target_pairs={{0,8},{4,12},{8,0},{12,4},{16,24},{20,28},{24,16},{28,20},{1,9},{5... | collective-permute-start | bytes 491528 | tf_op jit(solution)/shard_map/ppermute | solution.py:250
  67.3 4.0 %collective-permute-done.6 = f32[2,4,40,128]{3,2,1,0:T(8,128)S(1)} collective-permute-done((f32[2,4,40,128]{3,2,1,0:T(8,128)S(1)}, f32[2,4,40,128]{3,2,1,0:T(8,128)S(1)}, u32[]{:S(2)}, u32[]{:S(2)}) %collective-permute-start.6) | collective-permute-done | bytes 163872 | tf_op jit(solution)/shard_map/ppermute | solution.py:250
  71.3 2.6 %collective-permute-start.7 = (f32[4,40,128]{2,1,0:T(8,128)S(1)}, f32[4,40,128]{2,1,0:T(8,128)S(1)}, u32[]{:S(2)}, u32[]{:S(2)}) collective-permute-start(f32[4,40,128]{2,1,0:T(8,128)S(1)} %slice_bitcast_fusion.2), channel_id=1, source_target_pairs={{0,16},{4,20},{8,24},{12,28},{16,0},{20,4},{24,8},{28,12},{1,17},{... | collective-permute-start | bytes 245768 | tf_op jit(solution)/shard_map/ppermute | solution.py:250
  73.9 2.8 %collective-permute-done.7 = f32[4,40,128]{2,1,0:T(8,128)S(1)} collective-permute-done((f32[4,40,128]{2,1,0:T(8,128)S(1)}, f32[4,40,128]{2,1,0:T(8,128)S(1)}, u32[]{:S(2)}, u32[]{:S(2)}) %collective-permute-start.7) | collective-permute-done | bytes 81952 | tf_op jit(solution)/shard_map/ppermute | solution.py:250
  76.7 0.6 fusion.3
  (15 shorter events, 0.3 us)
Async XLA Ops:
  0.6 1.7 %copy-start = (f32[288,2048]{1,0:T(8,128)S(1)}, f32[288,2048]{1,0:T(8,128)}, u32[]{:S(2)}) copy-start(f32[288,2048]{1,0:T(8,128)} %spec_ref.3) | copy-start | bytes 7077892
  2.3 0.7 copy-start.6
  3.0 12.8 %copy-start.10 = (f32[2048]{0:T(1024)S(1)}, f32[2048]{0:T(1024)}, u32[]{:S(2)}) copy-start(f32[2048]{0:T(1024)} %param.21) | copy-start | bytes 24580
  3.0 14.2 %copy-start.1 = (f32[288,2048]{1,0:T(8,128)S(1)}, f32[288,2048]{1,0:T(8,128)}, u32[]{:S(2)}) copy-start(f32[288,2048]{1,0:T(8,128)} %spec_ref.3) | copy-start | bytes 7077892
  3.0 14.2 %copy-start.2 = (f32[2,8,2048]{2,1,0:T(8,128)S(1)}, f32[2,8,2048]{2,1,0:T(8,128)}, u32[]{:S(2)}) copy-start(f32[2,8,2048]{2,1,0:T(8,128)} %param.15) | copy-start | bytes 393220
  3.0 14.2 %copy-start.3 = (bf16[48,1024]{1,0:T(8,128)(2,1)S(1)}, bf16[48,1024]{1,0:T(8,128)(2,1)}, u32[]{:S(2)}) copy-start(bf16[48,1024]{1,0:T(8,128)(2,1)} %constant.49.clone.weight_ref) | copy-start | bytes 294916
  3.0 14.2 %copy-start.4 = (f32[2,72,128]{2,1,0:T(8,128)S(1)}, f32[2,72,128]{2,1,0:T(8,128)}, u32[]{:S(2)}) copy-start(f32[2,72,128]{2,1,0:T(8,128)} %constant.50.clone.facing_ref) | copy-start | bytes 221188
  3.0 14.2 %copy-start.5 = (f32[40,288]{1,0:T(8,128)S(1)}, f32[40,288]{1,0:T(8,128)}, u32[]{:S(2)}) copy-start(f32[40,288]{1,0:T(8,128)} %kernel_ref.1) | copy-start | bytes 138244
  3.0 14.2 %copy-start.7 = (f32[8]{0:T(128)S(1)}, f32[8]{0:T(128)}, u32[]{:S(2)}) copy-start(f32[8]{0:T(128)} %speed_ref.1) | copy-start | bytes 100
  3.0 14.2 %copy-start.8 = (f32[8]{0:T(128)S(1)}, f32[8]{0:T(128)}, u32[]{:S(2)}) copy-start(f32[8]{0:T(128)} %coef_ref.1) | copy-start | bytes 100
  3.0 14.2 %copy-start.9 = (f32[8]{0:T(128)S(1)}, f32[8]{0:T(128)}, u32[]{:S(2)}) copy-start(f32[8]{0:T(128)} %loss_ref.1) | copy-start | bytes 100
  5.1 10.8 %collective-permute-start = (f32[288,128]{1,0:T(8,128)S(1)}, f32[288,128]{1,0:T(8,128)S(1)}, u32[]{:S(2)}, u32[]{:S(2)}) collective-permute-start(f32[288,128]{1,0:T(8,128)S(1)} %get-tuple-element.6), channel_id=1, source_target_pairs={{0,4},{4,8},{8,12},{12,16},{16,20},{20,24},{24,28},{1,5},{5,9},{9,... | collective-permute-start | bytes 442376 | tf_op jit(solution)/shard_map/ppermute | solution.py:283
  10.0 7.2 %collective-permute-start.1 = (f32[288,128]{1,0:T(8,128)S(1)}, f32[288,128]{1,0:T(8,128)S(1)}, u32[]{:S(2)}, u32[]{:S(2)}) collective-permute-start(f32[288,128]{1,0:T(8,128)S(1)} %get-tuple-element.7), channel_id=1, source_target_pairs={{4,0},{8,4},{12,8},{16,12},{20,16},{24,20},{28,24},{5,1},{9,5},{13... | collective-permute-start | bytes 442376 | tf_op jit(solution)/shard_map/ppermute | solution.py:283
  17.2 34.9 %copy-start.11 = (s32[32]{0:T(128)S(1)}, s32[32]{0:T(128)}, u32[]{:S(2)}) copy-start(s32[32]{0:T(128)} %param.24) | copy-start | bytes 388
  43.9 1.5 %collective-permute-start.2 = (f32[40,1024]{1,0:T(8,128)S(1)}, f32[40,1024]{1,0:T(8,128)S(1)}, u32[]{:S(2)}, u32[]{:S(2)}) collective-permute-start(f32[40,1024]{1,0:T(8,128)S(1)} %slice_select_fusion), channel_id=1, source_target_pairs={{0,1},{1,0},{2,3},{3,2},{4,5},{5,4},{6,7},{7,6},{8,9},{9,8},{10,11... | collective-permute-start | bytes 491528 | tf_op jit(solution)/shard_map/ppermute | solution.py:250
  45.4 6.6 %collective-permute-start.3 = (f32[40,1024]{1,0:T(8,128)S(1)}, f32[40,1024]{1,0:T(8,128)S(1)}, u32[]{:S(2)}, u32[]{:S(2)}) collective-permute-start(f32[40,1024]{1,0:T(8,128)S(1)} %select_add_fusion), channel_id=1, source_target_pairs={{0,2},{1,3},{2,0},{3,1},{4,6},{5,7},{6,4},{7,5},{8,10},{9,11},{10,... | collective-permute-start | bytes 491528 | tf_op jit(solution)/shard_map/ppermute | solution.py:250
  52.1 1.5 %collective-permute-start.4 = (f32[40,1024]{1,0:T(8,128)S(1)}, f32[40,1024]{1,0:T(8,128)S(1)}, u32[]{:S(2)}, u32[]{:S(2)}) collective-permute-start(f32[40,1024]{1,0:T(8,128)S(1)} %add.31), channel_id=1, source_target_pairs={{0,1},{1,0},{2,3},{3,2},{4,5},{5,4},{6,7},{7,6},{8,9},{9,8},{10,11... | collective-permute-start | bytes 491528 | tf_op jit(solution)/shard_map/ppermute | solution.py:250
  54.9 10.5 %collective-permute-start.5 = (f32[2,2,4,40,128]{4,3,2,0,1:T(8,128)S(1)}, f32[2,2,4,40,128]{4,3,2,0,1:T(8,128)S(1)}, u32[]{:S(2)}, u32[]{:S(2)}) collective-permute-start(f32[2,2,4,40,128]{4,3,2,0,1:T(8,128)S(1)} %bitcast.31), channel_id=1, source_target_pairs={{0,4},{4,0},{8,12},{12,8},{16,20},{20,16},{24,28},{28,24},{1,5},{5... | collective-permute-start | bytes 983048 | tf_op jit(solution)/shard_map/ppermute | solution.py:250
  65.5 5.8 %collective-permute-start.6 = (f32[2,4,40,128]{3,2,1,0:T(8,128)S(1)}, f32[2,4,40,128]{3,2,1,0:T(8,128)S(1)}, u32[]{:S(2)}, u32[]{:S(2)}) collective-permute-start(f32[2,4,40,128]{3,2,1,0:T(8,128)S(1)} %slice_bitcast_fusion), channel_id=1, source_target_pairs={{0,8},{4,12},{8,0},{12,4},{16,24},{20,28},{24,16},{28,20},{1,9},{5... | collective-permute-start | bytes 491528 | tf_op jit(solution)/shard_map/ppermute | solution.py:250
  71.3 5.4 %collective-permute-start.7 = (f32[4,40,128]{2,1,0:T(8,128)S(1)}, f32[4,40,128]{2,1,0:T(8,128)S(1)}, u32[]{:S(2)}, u32[]{:S(2)}) collective-permute-start(f32[4,40,128]{2,1,0:T(8,128)S(1)} %slice_bitcast_fusion.2), channel_id=1, source_target_pairs={{0,16},{4,20},{8,24},{12,28},{16,0},{20,4},{24,8},{28,12},{1,17},{... | collective-permute-start | bytes 245768 | tf_op jit(solution)/shard_map/ppermute | solution.py:250

commit v2 on v1

v2 whole, which is shorter than its diff:
```python
import functools
import math

import jax
import jax.numpy as jnp
import ml_dtypes
import numpy as np
from jax import lax
from jax.experimental import pallas as pl
from jax.experimental.pallas import tpu as pltpu
from jax.sharding import PartitionSpec as P

ND = 36
TPW = 4
LANES = 128
UNROLL = 16
PAIR = 2 * ND
BF = jnp.bfloat16
F32 = jnp.float32
VMEM = pl.BlockSpec(memory_space=pltpu.VMEM)
SMEM = pl.BlockSpec(memory_space=pltpu.SMEM)
ANY = pl.BlockSpec(memory_space=pl.ANY)


def params(mib):
    return pltpu.CompilerParams(vmem_limit_bytes=mib << 20)


def split2(x):
    high = x.astype(BF)
    return high, (x - high.astype(F32)).astype(BF)


def dot(a, b):
    return jnp.dot(a, b, preferred_element_type=F32)


def direction_constants(slots):
    theta = np.arange(ND) * (2.0 * math.pi / ND)
    cosine, sine = np.cos(theta), np.sin(theta)
    table = np.zeros((2, slots, slots, LANES), np.float32)
    for slot in range(slots):
        for half in range(2):
            table[0, slot, slot, half * ND : (half + 1) * ND] = -cosine
            table[1, slot, slot, half * ND : (half + 1) * ND] = -sine
    table = table.reshape(2 * slots, slots * LANES)
    high = table.astype(ml_dtypes.bfloat16)
    low = (table - high.astype(np.float32)).astype(ml_dtypes.bfloat16)
    rows = np.stack([np.tile(cosine, 2), np.tile(sine, 2)]).astype(np.float32)
    facing = np.broadcast_to(rows[:, :, None], (2, PAIR, LANES))
    return np.concatenate([high, low, high], 0), np.ascontiguousarray(facing)


def vmem(shape, dtype=F32):
    return pltpu.VMEM(shape, dtype)


def in_hbm(*arrays):
    return [pltpu.with_memory_space_constraint(array, pltpu.HBM) for array in arrays]


def start_all(sources, targets, sems):
    copies = [
        pltpu.make_async_copy(source, target, sems.at[number])
        for number, (source, target) in enumerate(zip(sources, targets))
    ]
    for copy in copies:
        copy.start()
    return copies


def pick_kernel(lists_hbm, spec_hbm, spec_ref, next_ref, prev_ref, lists_ref, sems, small_sems):
    points = spec_ref.shape[1]
    chunks = sems.shape[0]
    width = points // chunks
    copies = []
    for chunk in range(chunks):
        columns = pl.ds(chunk * width, width)
        copies.append(
            pltpu.make_async_copy(
                spec_hbm.at[:, columns], spec_ref.at[:, columns], sems.at[chunk]
            )
        )
    (lists_copy,) = start_all([lists_hbm], [lists_ref], small_sems)
    for copy in copies:
        copy.start()
    lists_copy.wait()
    count = next_ref.shape[1]
    lists = jnp.concatenate([lists_ref[0], lists_ref[1]], 1)
    total = None
    for chunk in range(chunks):
        copies[chunk].wait()
        part = spec_ref[:, chunk * width : (chunk + 1) * width]
        first = part.astype(BF)
        rest = part - first.astype(F32)
        second = rest.astype(BF)
        third = (rest - second.astype(F32)).astype(BF)
        ids = lax.broadcasted_iota(jnp.int32, (width, 2 * count), 0) + chunk * width
        chosen = jnp.where(ids == lists, 1.0, 0.0).astype(BF)
        found = dot(first, chosen) + (dot(second, chosen) + dot(third, chosen))
        total = found if total is None else total + found
    next_ref[...] = total[:, :count]
    prev_ref[...] = total[:, count:]


def pick_halo(spectrum, lists):
    bins, points = spectrum.shape
    halo = jax.ShapeDtypeStruct((bins, lists.shape[-1]), F32)
    return pl.pallas_call(
        pick_kernel,
        in_specs=[ANY, ANY],
        out_specs=[VMEM] * 3,
        out_shape=[vmem((bins, points)), halo, halo],
        scratch_shapes=[
            pltpu.VMEM(lists.shape, jnp.int32),
            pltpu.SemaphoreType.DMA((8,)),
            pltpu.SemaphoreType.DMA((1,)),
        ],
        compiler_params=params(8),
    )(*in_hbm(lists, spectrum))


def prepare_kernel(*refs):
    spec_ref, operands = refs[0], refs[1:9]
    table, inflow, gain, index_out = refs[9:13]
    scratch, (turn, sems, index_sem) = refs[13:21], refs[21:]
    copies = start_all(operands, scratch, sems)
    coef_ref, loss_ref, edge_ref, wind_ref, friction_ref, weight_ref, facing_ref, index_ref = scratch
    bins, points = gain.shape
    groups = bins // PAIR
    slots = inflow.shape[0]
    filler = jnp.zeros((LANES - PAIR, LANES), F32)

    @pl.loop(0, points // LANES)
    def _(block):
        columns = pl.ds(pl.multiple_of(block * LANES, LANES), LANES)
        for group in range(groups):
            part = spec_ref[group * PAIR : (group + 1) * PAIR, columns]
            rows = pl.ds(block * (LANES * groups) + group, LANES, stride=groups)
            table[rows, :] = jnp.concatenate([part, filler], 0).T

    for copy in copies:
        copy.wait()
    index_ref[...] = index_ref[...] * groups
    index_copy = pltpu.make_async_copy(index_ref, index_out, index_sem)
    index_copy.start()
    lower = lax.broadcasted_iota(jnp.int32, (PAIR, LANES), 0) < ND

    def per_bin(ref, group):
        return jnp.where(lower, ref[2 * group], ref[2 * group + 1])

    coef = [per_bin(coef_ref, group) for group in range(groups)]
    loss = [per_bin(loss_ref, group) for group in range(groups)]
    turn[0] = jnp.cos(wind_ref[...])
    turn[1] = jnp.sin(wind_ref[...])

    @pl.loop(0, points // LANES)
    def _(block):
        base = pl.multiple_of(block * LANES, LANES)
        columns = pl.ds(base, LANES)
        edge_high, edge_low = split2(edge_ref[:, columns])
        left = jnp.concatenate([edge_high, edge_high, edge_low], 0)
        weights = lax.dot_general(
            left, weight_ref[...], (((0,), (0,)), ((), ())), preferred_element_type=F32
        )
        for slot in range(slots):
            factor = jnp.maximum(weights[:, slot * LANES : (slot + 1) * LANES], 0.0)
            inflow[slot, pl.ds(base, LANES), :] = factor
        row = pl.ds(block, 1)
        facing = facing_ref[0] * turn[0, row, :] + facing_ref[1] * turn[1, row, :]
        pushed = jnp.maximum(facing, 0.0) * friction_ref[row, :]
        for group in range(groups):
            gain[group * PAIR : (group + 1) * PAIR, columns] = jnp.exp(
                coef[group] * pushed - loss[group]
            )

    index_copy.wait()


def prepare(spectrum, coef, loss, edges, wind, friction, index, rows):
    bins, points = spectrum.shape
    slots = edges.shape[0] // 2
    weight, facing = direction_constants(slots)
    shape = (points // LANES, LANES)
    operands = [edges, wind.reshape(shape), friction.reshape(shape), weight, facing, index]
    operands = [jnp.asarray(operand) for operand in operands]
    return pl.pallas_call(
        prepare_kernel,
        in_specs=[VMEM] + [ANY] * 8,
        out_specs=[VMEM, VMEM, VMEM, ANY],
        out_shape=[
            vmem((rows, LANES)),
            vmem((slots, points + 8, LANES)),
            vmem((bins, points)),
            pltpu.HBM(index.shape, index.dtype),
        ],
        scratch_shapes=[
            pltpu.SMEM(coef.shape, F32),
            pltpu.SMEM(loss.shape, F32),
            *[pltpu.VMEM(operand.shape, operand.dtype) for operand in operands],
            pltpu.VMEM((2, *shape), F32),
            pltpu.SemaphoreType.DMA((8,)),
            pltpu.SemaphoreType.DMA(()),
        ],
        compiler_params=params(6),
    )(spectrum, *in_hbm(coef, loss, *operands))


def advance_kernel(
    speed_hbm,
    index_hbm,
    kernel_hbm,
    table_in,
    inflow,
    spec_ref,
    gain_ref,
    prev_ref,
    next_ref,
    updated_ref,
    stokes_ref,
    table,
    speed_ref,
    kernel_ref,
    index_ref,
    gathered,
    result,
    sems,
    index_sems,
    small_sems,
    *,
    unroll,
):
    bins, points = spec_ref.shape
    groups = bins // PAIR
    slots = inflow.shape[0]
    halo = prev_ref.shape[1]
    blocks = points // LANES
    filler = jnp.zeros((LANES - PAIR, LANES), F32)

    def fetch(block):
        return pltpu.make_async_copy(index_hbm.at[block], index_ref.at[block], index_sems.at[block])

    @pl.loop(0, blocks)
    def _(block):
        fetch(block).start()

    small = start_all([speed_hbm, kernel_hbm], [speed_ref, kernel_ref], small_sems)

    for number, ref in enumerate((prev_ref, next_ref)):
        for group in range(groups):
            part = jnp.concatenate([ref[group * PAIR : (group + 1) * PAIR, :], filler], 0).T
            start = (points + number * halo) * groups + group
            table[pl.ds(start, halo, stride=groups), :] = part

    for copy in small:
        copy.wait()
    kernel_high, kernel_low = split2(kernel_ref[...])
    kernel_both = jnp.concatenate([kernel_high, kernel_low], 0)
    depth = kernel_ref.shape[0]
    lower = lax.broadcasted_iota(jnp.int32, (PAIR, LANES), 0) < ND

    def copy_out(block):
        columns = pl.ds(pl.multiple_of(block * LANES, LANES), LANES)
        return pltpu.make_async_copy(
            result.at[block], updated_ref.at[:, columns], sems.at[block]
        )

    @pl.loop(0, blocks)
    def _(block):
        base = pl.multiple_of(block * LANES, LANES)
        columns = pl.ds(base, LANES)
        fetch(block).wait()

        @pl.loop(0, LANES // unroll)
        def _(chunk):
            first = pl.multiple_of(chunk * unroll, unroll)
            picks = [
                index_ref.at[block, slot, pl.ds(first, unroll)]
                for slot in range(slots)
            ]
            for u in range(unroll):
                point = base + first + u
                own = table[pl.ds(point * groups, groups), :]
                terms = []
                for slot in range(slots):
                    upwind = table[pl.ds(picks[slot][u], groups), :]
                    factor = inflow[slot, pl.ds(point, groups, stride=0), :]
                    terms.append(factor * (upwind - own))
                while len(terms) > 1:
                    terms = [a + b for a, b in zip(terms[::2], terms[1::2])]
                gathered[pl.ds((first + u) * groups, groups), :] = terms[0]

        for group in range(groups):
            rows = slice(group * PAIR, (group + 1) * PAIR)
            change = gathered[pl.ds(group, LANES, stride=groups), :].T[:PAIR]
            speed = jnp.where(lower, speed_ref[2 * group], speed_ref[2 * group + 1])
            advected = spec_ref[rows, columns] + speed * change
            result[block, rows, :] = advected * gain_ref[rows, columns]
        copy_out(block).start()
        high, low = split2(result[block])
        both = dot(kernel_both, high)
        stokes_ref[:, columns] = both[:depth] + both[depth:] + dot(kernel_high, low)

    @pl.loop(0, blocks)
    def _(block):
        copy_out(block).wait()


def advance(speed, index, table, inflow, spectrum, gain, prev, nxt, kernel):
    bins, points = spectrum.shape
    groups = bins // PAIR
    blocks = points // LANES
    return pl.pallas_call(
        functools.partial(advance_kernel, unroll=UNROLL),
        in_specs=[ANY] * 3 + [VMEM] * 6,
        out_specs=[ANY, VMEM, VMEM],
        out_shape=[
            jax.ShapeDtypeStruct((bins, points), F32),
            jax.ShapeDtypeStruct((kernel.shape[0], points), F32),
            vmem(table.shape),
        ],
        input_output_aliases={3: 2},
        scratch_shapes=[
            pltpu.SMEM(speed.shape, F32),
            pltpu.VMEM(kernel.shape, F32),
            pltpu.SMEM(index.shape, jnp.int32),
            pltpu.VMEM((LANES * groups, LANES), F32),
            pltpu.VMEM((blocks, bins, LANES), F32),
            pltpu.SemaphoreType.DMA((blocks,)),
            pltpu.SemaphoreType.DMA((blocks,)),
            pltpu.SemaphoreType.DMA((2,)),
        ],
        compiler_params=params(10),
    )(*in_hbm(speed, index, kernel), table, inflow, spectrum, gain, prev, nxt)


def regrid_kernel(slot_ref, stokes_ref, high_ref, low_ref, out_ref, *, block_rows):
    depth = stokes_ref.shape[0]
    out_ref[...] = jnp.zeros(out_ref.shape, F32)
    lower = lax.broadcasted_iota(jnp.int32, (depth, LANES), 1) < block_rows
    for pair in range(stokes_ref.shape[1] // LANES):
        columns = slice(pair * LANES, (pair + 1) * LANES)
        part = stokes_ref[:, columns]
        both = jnp.concatenate([jnp.where(lower, part, 0.0), jnp.where(lower, 0.0, part)], 0)
        high, low = split2(both)
        terms = (
            dot(high, high_ref[columns, :])
            + dot(low, high_ref[columns, :])
            + dot(high, low_ref[columns, :])
        )
        for half in range(2):
            slot = slot_ref[2 * pair + half]
            out_ref[slot] = out_ref[slot] + terms[half * depth : (half + 1) * depth]


def regrid(slots, stokes, high, low, count, block_rows):
    depth = stokes.shape[0]
    return pl.pallas_call(
        functools.partial(regrid_kernel, block_rows=block_rows),
        in_specs=[SMEM, VMEM, VMEM, VMEM],
        out_specs=VMEM,
        out_shape=jax.ShapeDtypeStruct((count, depth, LANES), F32),
        compiler_params=params(4),
    )(slots, stokes, high, low)


def swap(value, axis, bit):
    count = lax.axis_size(axis)
    return lax.ppermute(value, axis, [(i, i ^ bit) for i in range(count)])


def sum_over(value, axis):
    count = lax.axis_size(axis)
    me = lax.axis_index(axis)
    half = value.shape[1] // 2
    odd = (me & 1) == 1
    left, right = value[:, :half], value[:, half:]
    mine = jnp.where(odd, right, left) + swap(jnp.where(odd, left, right), axis, 1)
    bit = 2
    while bit < count:
        mine = mine + swap(mine, axis, bit)
        bit *= 2
    other = swap(mine, axis, 1)
    return jnp.concatenate([jnp.where(odd, other, mine), jnp.where(odd, mine, other)], 1)


def places(relative, bits):
    total = jnp.zeros_like(relative)
    for bit in bits:
        total = 2 * total + jnp.where((relative & bit) != 0, 1, 0)
    return total


def exchange(value, even_bit, odd_bit):
    waves, groups = lax.axis_size("wave"), lax.axis_size("grp")
    pairs = [
        (w * groups + g, (w ^ (odd_bit if g % 2 else even_bit)) * groups + g)
        for w in range(waves)
        for g in range(groups)
    ]
    return lax.ppermute(value, ("wave", "grp"), pairs)


def scatter_sum(parts, bits, other_bits):
    for bit, other in zip(bits, other_bits):
        half = parts.shape[0] // 2
        parts = parts[:half] + exchange(parts[half:], bit, other)
    return parts[0]


def shift(value, axis, steps):
    count = lax.axis_size(axis)
    leading, last = (max(0, -steps), min(count, count - steps))
    return lax.ppermute(value, axis, [(source, source + steps) for source in range(leading, last)])


def body(
    spectrum,
    edge_vectors,
    neighbours,
    halo_lists,
    group_speed,
    input_coef,
    dissipation,
    friction,
    wind_dir,
    drift_kernel,
    block_tile,
    block_weights,
):
    n_wave = lax.axis_size("wave")
    n_group = lax.axis_size("grp")
    bins, points = spectrum.shape
    groups = bins // PAIR
    slots = neighbours.shape[0]
    rows = (points + 2 * halo_lists.shape[-1]) * groups
    spectrum, to_next, to_prev = pick_halo(spectrum, halo_lists)
    from_prev = shift(to_next, "wave", 1)
    from_next = shift(to_prev, "wave", -1)
    index = neighbours.reshape(slots, points // LANES, LANES).transpose(1, 0, 2)
    edges = edge_vectors.reshape(2 * slots, points)
    table, inflow, gain, index = prepare(
        spectrum, input_coef, dissipation, edges, wind_dir, friction, index, rows
    )
    updated, stokes, _ = advance(
        group_speed, index, table, inflow, spectrum, gain, from_prev, from_next, drift_kernel
    )
    stokes = sum_over(stokes, "grp")
    blocks, block_rows, tile_cells = block_weights.shape
    cells = tile_cells // n_group
    mine = lax.dynamic_slice_in_dim(block_weights, lax.axis_index("grp") * cells, cells, 2)
    mine = mine.reshape(blocks * block_rows, cells)
    rounded = lax.reduce_precision(mine, 8, 7)
    high, low = rounded.astype(BF), (mine - rounded).astype(BF)
    relative = (block_tile // TPW) ^ lax.axis_index("wave")
    tile = block_tile % TPW
    depth = drift_kernel.shape[0]
    bits = [1 << b for b in range(n_wave.bit_length() - 1)]
    other_bits = bits[1::-1] + bits[2:]
    odd = lax.axis_index("grp") % 2 == 1
    place = jnp.where(odd, places(relative, other_bits), places(relative, bits))
    parts = regrid(place * TPW + tile, stokes, high, low, n_wave * TPW, block_rows)
    drift = scatter_sum(parts.reshape(n_wave, TPW, depth, cells), bits, other_bits)
    return updated, drift


def solution(mesh):
    in_specs = (
        P("grp", "wave"),
        P(None, None, "wave"),
        P(None, "wave"),
        P(None, "wave", None),
        P("grp"),
        P("grp"),
        P("grp"),
        P("wave"),
        P("wave"),
        P(None, "grp"),
        P("wave"),
        P("wave", None, None),
    )
    out_specs = (P("grp", "wave"), P("wave", None, "grp"))
    return jax.shard_map(body, mesh=mesh, in_specs=in_specs, out_specs=out_specs, check_vma=False)
```

time: 77.7 us -> 69.4 us (0.89)
  local copies, waits for them, and re-layouts: 7.47 us -> 1.37 us
  waiting for transfers between devices: 22.4 us -> 17 us
  Pallas kernels: 29.9 us -> 32.2 us
  starting transfers between devices: 14.8 us -> 16.8 us
  other arithmetic: 1.88 us -> 1.01 us
    ppermute x6 -> x3, waiting for transfers between devices: 21.1 us -> 6.27 us  [swap(): return lax.ppermute(value, axis, [(i, i ^ bit) for i in range(count)])]
    ppermute x0 -> x3, waiting for transfers between devices: none -> 10.8 us  [exchange(): return lax.ppermute(value, ('wave', 'grp'), pairs)]
    ppermute x0 -> x3, starting transfers between devices: none -> 8.88 us  [exchange(): return lax.ppermute(value, ('wave', 'grp'), pairs)]
    ppermute x6 -> x3, starting transfers between devices: 8.66 us -> 1.73 us  [swap(): return lax.ppermute(value, axis, [(i, i ^ bit) for i in range(count)])]
    unnamed x25 -> x2, local copies, waits for them, and re-layouts: 2.4 us -> 0.01 us
    pallas_call x2 -> x3, Pallas kernels: 28.7 us -> 30.9 us  [the longest x1 20.2 us: advance(): pl.pallas_call(functools.partial(advance_kernel, unroll=UNROLL), in_specs...]
    reshape x1 -> x0, local copies, waits for them, and re-layouts: 1.65 us -> none  [body(): index = (neighbours * groups).T.reshape(-1)]
    transpose x1 -> x0, local copies, waits for them, and re-layouts: 1.31 us -> none  [body(): index = (neighbours * groups).T.reshape(-1)]
  transfers between devices with their start and end apart: 8 -> 8, of which waited for: 7 -> 6; matrix products, arithmetic and copies ran while one was open for 8% -> 2% of each run, Pallas kernels for 0% -> 10%
where the time goes in v2:
time: 69.4 us; the launch traced here: 69.1 us
  Pallas kernels  32.2 us (46%)
  waiting for transfers between devices  17 us (24%)
  starting transfers between devices  16.8 us (24%)
  local copies, waits for them, and re-layouts  1.37 us (2%)
  other arithmetic  1.01 us (1%)
  between operations  0.82 us (1%)
    pallas_call x1, Pallas kernels, advance(): pl.pallas_call(functools.partial(advance_kernel, unroll=UNROLL), in_specs...  20.2 us
    ppermute x3, waiting for transfers between devices, exchange(): return lax.ppermute(value, ('wave', 'grp'), pairs)  10.8 us
    ppermute x3, starting transfers between devices, exchange(): return lax.ppermute(value, ('wave', 'grp'), pairs)  8.88 us
    pallas_call x1, Pallas kernels, prepare(): pl.pallas_call(prepare_kernel, in_specs=[VMEM] + [ANY] * 8, out_specs=[VM...  6.78 us
    ppermute x3, waiting for transfers between devices, swap(): return lax.ppermute(value, axis, [(i, i ^ bit) for i in range(count)])  6.27 us
    ppermute x2, starting transfers between devices, shift(): lax.ppermute(value, axis, [(source, source + steps) for source in range(l...  6.14 us
    pallas_call x1, Pallas kernels, pick_halo(): pl.pallas_call(pick_kernel, in_specs=[ANY, ANY], out_specs=[VMEM] * 3, ou...  3.91 us
    ppermute x3, starting transfers between devices, swap(): return lax.ppermute(value, axis, [(i, i ^ bit) for i in range(count)])  1.73 us
  transfers between devices with their start and end apart: 8, of which 6 were waited for; matrix products, arithmetic and copies ran while one was open for 2% of the time, Pallas kernels for 10%

profile of v2, /device:TPU:0, one launch (start us, length us, event | category | flops | bytes accessed | tf_op | source)
XLA Modules:
  0.0 69.1 jit_solution(14497270096564582316)
XLA Ops:
  0.6 3.9 %shard_map.149 = (f32[288,2048]{1,0:T(8,128)S(1)}, f32[288,128]{1,0:T(8,128)S(1)}, f32[288,128]{1,0:T(8,128)S(1)}) custom-call(s32[2,1,128]{2,1,0:T(1,128)} %lists_hbm.1, f32[288,2048]{1,0:T(8,128)} %spec_hbm.1), custom_call_target="tpu_custom_call" | custom-call | tf_op jit(solution)/shard_map/pallas_call | solution.py:109
  4.5 4.8 %collective-permute-start = (f32[288,128]{1,0:T(8,128)S(1)}, f32[288,128]{1,0:T(8,128)S(1)}, u32[]{:S(2)}, u32[]{:S(2)}) collective-permute-start(f32[288,128]{1,0:T(8,128)S(1)} %get-tuple-element.16), channel_id=1, source_target_pairs={{0,4},{4,8},{8,12},{12,16},{16,20},{20,24},{24,28},{1,5},{5,9},{9,... | collective-permute-start | bytes 442376 | tf_op jit(solution)/shard_map/ppermute | solution.py:414
  9.4 1.3 %collective-permute-start.1 = (f32[288,128]{1,0:T(8,128)S(1)}, f32[288,128]{1,0:T(8,128)S(1)}, u32[]{:S(2)}, u32[]{:S(2)}) collective-permute-start(f32[288,128]{1,0:T(8,128)S(1)} %get-tuple-element.17), channel_id=1, source_target_pairs={{4,0},{8,4},{12,8},{16,12},{20,16},{24,20},{28,24},{5,1},{9,5},{13... | collective-permute-start | bytes 442376 | tf_op jit(solution)/shard_map/ppermute | solution.py:414
  10.7 6.8 %shard_map.150 = (f32[9216,128]{1,0:T(8,128)S(1)}, f32[8,2056,128]{2,1,0:T(8,128)S(1)}, f32[288,2048]{1,0:T(8,128)S(1)}, s32[16,8,128]{2,1,0:T(8,128)}) custom-call(f32[288,2048]{1,0:T(8,128)S(1)} %get-tuple-element.11.refs_0_.spec_ref, f32[8]{0:T(128)} %refs_1_.1, f32[8]{0:T(128)} %refs_2_.1, f32[16,2048]{1,0:T(8,128)} %bitcast.15, f32[16,128]{1,0:T(8,128)} %bitcast.17, ...), custom_call_target="tpu_custom_call" | custom-call | tf_op jit(solution)/shard_map/pallas_call | solution.py:187
  17.5 0.0 collective-permute-done.prev_ref
  17.5 0.0 collective-permute-done.1.next_ref
  17.5 20.2 %shard_map.151 = (f32[288,2048]{1,0:T(8,128)}, f32[40,2048]{1,0:T(8,128)S(1)}, f32[9216,128]{1,0:T(8,128)S(1)}) custom-call(f32[8]{0:T(128)} %speed_hbm.1, s32[16,8,128]{2,1,0:T(8,128)} %get-tuple-element.12.index_hbm, f32[40,288]{1,0:T(8,128)} %kernel_hbm.1, f32[9216,128]{1,0:T(8,128)S(1)} %get-tuple-element.13.table_in, ...), custom_call_target="tpu_custom_call", output_to_operand_aliasing={{2}: (3, {})} | custom-call | tf_op jit(solution)/shard_map/pallas_call | solution.py:313
  37.8 0.0 copy-start
  37.8 0.1 collective-permute-start.2
  37.9 1.3 %constant_dynamic-slice_fusion = f32[32,64,128]{2,1,0:T(8,128)S(1)} fusion(f32[32,64,512]{2,1,0:T(8,128)} %param.25, s32[]{:T(128)S(6)} %select_n.75), kind=kLoop, calls=%fused_computation.22 | loop fusion | bytes 2097156 | tf_op jit(solution)/shard_map/dynamic_slice | solution.py:451
  39.2 0.1 collective-permute-done.2
  39.3 1.6 %collective-permute-start.3 = (f32[40,1024]{1,0:T(8,128)S(1)}, f32[40,1024]{1,0:T(8,128)S(1)}, u32[]{:S(2)}, u32[]{:S(2)}) collective-permute-start(f32[40,1024]{1,0:T(8,128)S(1)} %select_add_fusion), channel_id=1, source_target_pairs={{0,2},{1,3},{2,0},{3,1},{4,6},{5,7},{6,4},{7,5},{8,10},{9,11},{10,... | collective-permute-start | bytes 491528 | tf_op jit(solution)/shard_map/ppermute | solution.py:369
  40.9 0.2 fusion
  41.1 4.8 %collective-permute-done.3 = f32[40,1024]{1,0:T(8,128)S(1)} collective-permute-done((f32[40,1024]{1,0:T(8,128)S(1)}, f32[40,1024]{1,0:T(8,128)S(1)}, u32[]{:S(2)}, u32[]{:S(2)}) %collective-permute-start.3) | collective-permute-done | bytes 163872 | tf_op jit(solution)/shard_map/ppermute | solution.py:369
  45.9 0.1 collective-permute-start.4
  46.0 0.0 copy-done
  46.0 1.3 %collective-permute-done.4 = f32[40,1024]{1,0:T(8,128)S(1)} collective-permute-done((f32[40,1024]{1,0:T(8,128)S(1)}, f32[40,1024]{1,0:T(8,128)S(1)}, u32[]{:S(2)}, u32[]{:S(2)}) %collective-permute-start.4) | collective-permute-done | bytes 163872 | tf_op jit(solution)/shard_map/ppermute | solution.py:369
  47.5 1.2 %shard_map.152 = f32[32,40,128]{2,1,0:T(8,128)S(1)} custom-call(s32[32]{0:T(128)S(1)} %fusion.2.slot_ref, f32[40,2048]{1,0:T(8,128)S(1)} %pad_maximum_fusion.stokes_ref, bf16[2048,128]{1,0:T(8,128)(2,1)S(1)} %get-tuple-element.21.high_ref, bf16[2048,128]{1,0:T(8,128)(2,1)S(1)} %get-tuple-element.20.low_ref), custom_call_target="tpu_custom_call" | custom-call | tf_op jit(solution)/shard_map/pallas_call | solution.py:358
  48.7 2.7 %collective-permute-start.5 = (f32[4,4,40,128]{3,2,1,0:T(8,128)S(1)}, f32[4,4,40,128]{3,2,1,0:T(8,128)S(1)}, u32[]{:S(2)}, u32[]{:S(2)}) collective-permute-start(f32[4,4,40,128]{3,2,1,0:T(8,128)S(1)} %bitcast.14), channel_id=1, source_target_pairs={{0,4},{1,9},{2,6},{3,11},{4,0},{5,13},{6,2},{7,15},{8,12},{9,1},{1... | collective-permute-start | bytes 983048 | tf_op jit(solution)/shard_map/ppermute | solution.py:401
  51.5 5.1 %collective-permute-done.5 = f32[4,4,40,128]{3,2,1,0:T(8,128)S(1)} collective-permute-done((f32[4,4,40,128]{3,2,1,0:T(8,128)S(1)}, f32[4,4,40,128]{3,2,1,0:T(8,128)S(1)}, u32[]{:S(2)}, u32[]{:S(2)}) %collective-permute-start.5) | collective-permute-done | bytes 327712 | tf_op jit(solution)/shard_map/ppermute | solution.py:401
  56.6 3.0 %collective-permute-start.6 = (f32[2,4,40,128]{3,2,1,0:T(8,128)S(1)}, f32[2,4,40,128]{3,2,1,0:T(8,128)S(1)}, u32[]{:S(2)}, u32[]{:S(2)}) collective-permute-start(f32[2,4,40,128]{3,2,1,0:T(8,128)S(1)} %slice.43), channel_id=1, source_target_pairs={{0,8},{1,5},{2,10},{3,7},{4,12},{5,1},{6,14},{7,3},{8,0},{9,13},{1... | collective-permute-start | bytes 491528 | tf_op jit(solution)/shard_map/ppermute | solution.py:401
  59.6 3.3 %collective-permute-done.6 = f32[2,4,40,128]{3,2,1,0:T(8,128)S(1)} collective-permute-done((f32[2,4,40,128]{3,2,1,0:T(8,128)S(1)}, f32[2,4,40,128]{3,2,1,0:T(8,128)S(1)}, u32[]{:S(2)}, u32[]{:S(2)}) %collective-permute-start.6) | collective-permute-done | bytes 163872 | tf_op jit(solution)/shard_map/ppermute | solution.py:401
  63.0 3.1 %collective-permute-start.7 = (f32[1,4,40,128]{3,2,1,0:T(8,128)S(1)}, f32[1,4,40,128]{3,2,1,0:T(8,128)S(1)}, u32[]{:S(2)}, u32[]{:S(2)}) collective-permute-start(f32[1,4,40,128]{3,2,1,0:T(8,128)S(1)} %slice.45), channel_id=1, source_target_pairs={{0,16},{1,17},{2,18},{3,19},{4,20},{5,21},{6,22},{7,23},{8,24},{9,... | collective-permute-start | bytes 245768 | tf_op jit(solution)/shard_map/ppermute | solution.py:401
  66.1 2.4 %collective-permute-done.7 = f32[1,4,40,128]{3,2,1,0:T(8,128)S(1)} collective-permute-done((f32[1,4,40,128]{3,2,1,0:T(8,128)S(1)}, f32[1,4,40,128]{3,2,1,0:T(8,128)S(1)}, u32[]{:S(2)}, u32[]{:S(2)}) %collective-permute-start.7) | collective-permute-done | bytes 81952 | tf_op jit(solution)/shard_map/ppermute | solution.py:401
  68.5 0.6 fusion.1
  (11 shorter events, 0.3 us)
Async XLA Ops:
  4.5 12.9 %collective-permute-start = (f32[288,128]{1,0:T(8,128)S(1)}, f32[288,128]{1,0:T(8,128)S(1)}, u32[]{:S(2)}, u32[]{:S(2)}) collective-permute-start(f32[288,128]{1,0:T(8,128)S(1)} %get-tuple-element.16), channel_id=1, source_target_pairs={{0,4},{4,8},{8,12},{12,16},{16,20},{20,24},{24,28},{1,5},{5,9},{9,... | collective-permute-start | bytes 442376 | tf_op jit(solution)/shard_map/ppermute | solution.py:414
  9.4 8.1 %collective-permute-start.1 = (f32[288,128]{1,0:T(8,128)S(1)}, f32[288,128]{1,0:T(8,128)S(1)}, u32[]{:S(2)}, u32[]{:S(2)}) collective-permute-start(f32[288,128]{1,0:T(8,128)S(1)} %get-tuple-element.17), channel_id=1, source_target_pairs={{4,0},{8,4},{12,8},{16,12},{20,16},{24,20},{28,24},{5,1},{9,5},{13... | collective-permute-start | bytes 442376 | tf_op jit(solution)/shard_map/ppermute | solution.py:414
  37.8 8.2 %copy-start = (s32[32]{0:T(128)S(1)}, s32[32]{0:T(128)}, u32[]{:S(2)}) copy-start(s32[32]{0:T(128)} %param.24) | copy-start | bytes 388
  37.8 1.5 %collective-permute-start.2 = (f32[40,1024]{1,0:T(8,128)S(1)}, f32[40,1024]{1,0:T(8,128)S(1)}, u32[]{:S(2)}, u32[]{:S(2)}) collective-permute-start(f32[40,1024]{1,0:T(8,128)S(1)} %slice_select_fusion), channel_id=1, source_target_pairs={{0,1},{1,0},{2,3},{3,2},{4,5},{5,4},{6,7},{7,6},{8,9},{9,8},{10,11... | collective-permute-start | bytes 491528 | tf_op jit(solution)/shard_map/ppermute | solution.py:369
  39.3 6.6 %collective-permute-start.3 = (f32[40,1024]{1,0:T(8,128)S(1)}, f32[40,1024]{1,0:T(8,128)S(1)}, u32[]{:S(2)}, u32[]{:S(2)}) collective-permute-start(f32[40,1024]{1,0:T(8,128)S(1)} %select_add_fusion), channel_id=1, source_target_pairs={{0,2},{1,3},{2,0},{3,1},{4,6},{5,7},{6,4},{7,5},{8,10},{9,11},{10,... | collective-permute-start | bytes 491528 | tf_op jit(solution)/shard_map/ppermute | solution.py:369
  45.9 1.5 %collective-permute-start.4 = (f32[40,1024]{1,0:T(8,128)S(1)}, f32[40,1024]{1,0:T(8,128)S(1)}, u32[]{:S(2)}, u32[]{:S(2)}) collective-permute-start(f32[40,1024]{1,0:T(8,128)S(1)} %add.52), channel_id=1, source_target_pairs={{0,1},{1,0},{2,3},{3,2},{4,5},{5,4},{6,7},{7,6},{8,9},{9,8},{10,11... | collective-permute-start | bytes 491528 | tf_op jit(solution)/shard_map/ppermute | solution.py:369
  48.7 7.8 %collective-permute-start.5 = (f32[4,4,40,128]{3,2,1,0:T(8,128)S(1)}, f32[4,4,40,128]{3,2,1,0:T(8,128)S(1)}, u32[]{:S(2)}, u32[]{:S(2)}) collective-permute-start(f32[4,4,40,128]{3,2,1,0:T(8,128)S(1)} %bitcast.14), channel_id=1, source_target_pairs={{0,4},{1,9},{2,6},{3,11},{4,0},{5,13},{6,2},{7,15},{8,12},{9,1},{1... | collective-permute-start | bytes 983048 | tf_op jit(solution)/shard_map/ppermute | solution.py:401
  56.6 6.3 %collective-permute-start.6 = (f32[2,4,40,128]{3,2,1,0:T(8,128)S(1)}, f32[2,4,40,128]{3,2,1,0:T(8,128)S(1)}, u32[]{:S(2)}, u32[]{:S(2)}) collective-permute-start(f32[2,4,40,128]{3,2,1,0:T(8,128)S(1)} %slice.43), channel_id=1, source_target_pairs={{0,8},{1,5},{2,10},{3,7},{4,12},{5,1},{6,14},{7,3},{8,0},{9,13},{1... | collective-permute-start | bytes 491528 | tf_op jit(solution)/shard_map/ppermute | solution.py:401
  63.0 5.5 %collective-permute-start.7 = (f32[1,4,40,128]{3,2,1,0:T(8,128)S(1)}, f32[1,4,40,128]{3,2,1,0:T(8,128)S(1)}, u32[]{:S(2)}, u32[]{:S(2)}) collective-permute-start(f32[1,4,40,128]{3,2,1,0:T(8,128)S(1)} %slice.45), channel_id=1, source_target_pairs={{0,16},{1,17},{2,18},{3,19},{4,20},{5,21},{6,22},{7,23},{8,24},{9,... | collective-permute-start | bytes 245768 | tf_op jit(solution)/shard_map/ppermute | solution.py:401

commit v3 on v2

--- a/solution.py
+++ b/solution.py
@@ -13,7 +13,8 @@
 ND = 36
 TPW = 4
 LANES = 128
-UNROLL = 16
+UNROLL = 128
+WIDTH = 512
 PAIR = 2 * ND
 BF = jnp.bfloat16
 F32 = jnp.float32
@@ -91,13 +92,10 @@
     for chunk in range(chunks):
         copies[chunk].wait()
         part = spec_ref[:, chunk * width : (chunk + 1) * width]
-        first = part.astype(BF)
-        rest = part - first.astype(F32)
-        second = rest.astype(BF)
-        third = (rest - second.astype(F32)).astype(BF)
+        first, second = split2(part)
         ids = lax.broadcasted_iota(jnp.int32, (width, 2 * count), 0) + chunk * width
         chosen = jnp.where(ids == lists, 1.0, 0.0).astype(BF)
-        found = dot(first, chosen) + (dot(second, chosen) + dot(third, chosen))
+        found = dot(first, chosen) + dot(second, chosen)
         total = found if total is None else total + found
     next_ref[...] = total[:, :count]
     prev_ref[...] = total[:, count:]
@@ -113,7 +111,7 @@
         out_shape=[vmem((bins, points)), halo, halo],
         scratch_shapes=[
             pltpu.VMEM(lists.shape, jnp.int32),
-            pltpu.SemaphoreType.DMA((8,)),
+            pltpu.SemaphoreType.DMA((4,)),
             pltpu.SemaphoreType.DMA((1,)),
         ],
         compiler_params=params(8),
@@ -131,7 +129,7 @@
     slots = inflow.shape[0]
     filler = jnp.zeros((LANES - PAIR, LANES), F32)
 
-    @pl.loop(0, points // LANES)
+    @pl.loop(0, points // LANES, unroll=8)
     def _(block):
         columns = pl.ds(pl.multiple_of(block * LANES, LANES), LANES)
         for group in range(groups):
@@ -154,7 +152,7 @@
     turn[0] = jnp.cos(wind_ref[...])
     turn[1] = jnp.sin(wind_ref[...])
 
-    @pl.loop(0, points // LANES)
+    @pl.loop(0, points // LANES, unroll=8)
     def _(block):
         base = pl.multiple_of(block * LANES, LANES)
         columns = pl.ds(base, LANES)
@@ -259,25 +257,23 @@
     depth = kernel_ref.shape[0]
     lower = lax.broadcasted_iota(jnp.int32, (PAIR, LANES), 0) < ND
 
-    def copy_out(block):
-        columns = pl.ds(pl.multiple_of(block * LANES, LANES), LANES)
+    width = result.shape[2]
+
+    def copy_out(part, group):
+        columns = pl.ds(pl.multiple_of(part * width, width), width)
+        rows = pl.ds(group * PAIR, PAIR)
         return pltpu.make_async_copy(
-            result.at[block], updated_ref.at[:, columns], sems.at[block]
+            result.at[part, rows], updated_ref.at[rows, columns], sems.at[part, group]
         )
 
-    @pl.loop(0, blocks)
-    def _(block):
+    def gather(block, start):
+        fetch(block).wait()
         base = pl.multiple_of(block * LANES, LANES)
-        columns = pl.ds(base, LANES)
-        fetch(block).wait()
 
         @pl.loop(0, LANES // unroll)
         def _(chunk):
             first = pl.multiple_of(chunk * unroll, unroll)
-            picks = [
-                index_ref.at[block, slot, pl.ds(first, unroll)]
-                for slot in range(slots)
-            ]
+            picks = [index_ref.at[block, slot, pl.ds(first, unroll)] for slot in range(slots)]
             for u in range(unroll):
                 point = base + first + u
                 own = table[pl.ds(point * groups, groups), :]
@@ -288,22 +284,35 @@
                     terms.append(factor * (upwind - own))
                 while len(terms) > 1:
                     terms = [a + b for a, b in zip(terms[::2], terms[1::2])]
-                gathered[pl.ds((first + u) * groups, groups), :] = terms[0]
+                gathered[pl.ds((start + first + u) * groups, groups), :] = terms[0]
+
+    @pl.loop(0, points // width)
+    def _(part):
+        columns = pl.ds(pl.multiple_of(part * width, width), width)
+        several = width // LANES
+
+        @pl.loop(0, several)
+        def _(step):
+            gather(part * several + step, pl.multiple_of(step * LANES, LANES))
 
         for group in range(groups):
             rows = slice(group * PAIR, (group + 1) * PAIR)
-            change = gathered[pl.ds(group, LANES, stride=groups), :].T[:PAIR]
             speed = jnp.where(lower, speed_ref[2 * group], speed_ref[2 * group + 1])
-            advected = spec_ref[rows, columns] + speed * change
-            result[block, rows, :] = advected * gain_ref[rows, columns]
-        copy_out(block).start()
-        high, low = split2(result[block])
+            for step in range(several):
+                inner = slice(step * LANES, (step + 1) * LANES)
+                outer = pl.ds(pl.multiple_of(part * width + step * LANES, LANES), LANES)
+                picked = gathered[pl.ds(step * LANES * groups + group, LANES, stride=groups), :]
+                advected = spec_ref[rows, outer] + speed * picked.T[:PAIR]
+                result[part, rows, inner] = advected * gain_ref[rows, outer]
+            copy_out(part, group).start()
+        high, low = split2(result[part])
         both = dot(kernel_both, high)
         stokes_ref[:, columns] = both[:depth] + both[depth:] + dot(kernel_high, low)
 
-    @pl.loop(0, blocks)
-    def _(block):
-        copy_out(block).wait()
+    @pl.loop(0, points // width)
+    def _(part):
+        for group in range(groups):
+            copy_out(part, group).wait()
 
 
 def advance(speed, index, table, inflow, spectrum, gain, prev, nxt, kernel):
@@ -324,9 +333,9 @@
             pltpu.SMEM(speed.shape, F32),
             pltpu.VMEM(kernel.shape, F32),
             pltpu.SMEM(index.shape, jnp.int32),
-            pltpu.VMEM((LANES * groups, LANES), F32),
-            pltpu.VMEM((blocks, bins, LANES), F32),
-            pltpu.SemaphoreType.DMA((blocks,)),
+            pltpu.VMEM((WIDTH * groups, LANES), F32),
+            pltpu.VMEM((points // WIDTH, bins, WIDTH), F32),
+            pltpu.SemaphoreType.DMA((points // WIDTH, groups)),
             pltpu.SemaphoreType.DMA((blocks,)),
             pltpu.SemaphoreType.DMA((2,)),
         ],

time: 69.4 us -> 62.1 us (0.89)
  Pallas kernels: 32.2 us -> 23.1 us
  waiting for transfers between devices: 17 us -> 19.9 us
  starting transfers between devices: 16.8 us -> 15.6 us
    pallas_call x1, Pallas kernels: 20.2 us -> 15.8 us  [advance(): pl.pallas_call(functools.partial(advance_kernel, unroll=UNROLL), in_specs...]
    pallas_call x1, Pallas kernels: 6.78 us -> 3.05 us  [prepare(): pl.pallas_call(prepare_kernel, in_specs=[VMEM] + [ANY] * 8, out_specs=[VM...]
    ppermute x2, waiting for transfers between devices: 0.01 us -> 2.83 us  [shift(): lax.ppermute(value, axis, [(source, source + steps) for source in range(l...]
    ppermute x3, starting transfers between devices: 8.88 us -> 7.76 us  [exchange(): return lax.ppermute(value, ('wave', 'grp'), pairs)]
    pallas_call x1, Pallas kernels: 3.91 us -> 3.02 us  [pick_halo(): pl.pallas_call(pick_kernel, in_specs=[ANY, ANY], out_specs=[VMEM] * 3, ou...]
  transfers between devices with their start and end apart: 8 -> 8, of which waited for: 6 -> 7; matrix products, arithmetic and copies ran while one was open for 2% -> 2% of each run, Pallas kernels for 10% -> 5%
where the time goes in v3:
time: 62.1 us; the launch traced here: 61.8 us
  Pallas kernels  23.1 us (37%)
  waiting for transfers between devices  19.9 us (32%)
  starting transfers between devices  15.6 us (25%)
  local copies, waits for them, and re-layouts  1.37 us (2%)
  other arithmetic  1.01 us (2%)
  between operations  0.81 us (1%)
    pallas_call x1, Pallas kernels, advance(): pl.pallas_call(functools.partial(advance_kernel, unroll=UNROLL), in_specs...  15.8 us
    ppermute x3, waiting for transfers between devices, exchange(): return lax.ppermute(value, ('wave', 'grp'), pairs)  10.8 us
    ppermute x3, starting transfers between devices, exchange(): return lax.ppermute(value, ('wave', 'grp'), pairs)  7.76 us
    ppermute x3, waiting for transfers between devices, swap(): return lax.ppermute(value, axis, [(i, i ^ bit) for i in range(count)])  6.27 us
    ppermute x2, starting transfers between devices, shift(): lax.ppermute(value, axis, [(source, source + steps) for source in range(l...  6.14 us
    pallas_call x1, Pallas kernels, prepare(): pl.pallas_call(prepare_kernel, in_specs=[VMEM] + [ANY] * 8, out_specs=[VM...  3.05 us
    pallas_call x1, Pallas kernels, pick_halo(): pl.pallas_call(pick_kernel, in_specs=[ANY, ANY], out_specs=[VMEM] * 3, ou...  3.02 us
    ppermute x2, waiting for transfers between devices, shift(): lax.ppermute(value, axis, [(source, source + steps) for source in range(l...  2.83 us
  transfers between devices with their start and end apart: 8, of which 7 were waited for; matrix products, arithmetic and copies ran while one was open for 2% of the time, Pallas kernels for 5%

profile of v3, /device:TPU:0, one launch (start us, length us, event | category | flops | bytes accessed | tf_op | source)
XLA Modules:
  0.0 61.8 jit_solution(3293540267010500392)
XLA Ops:
  0.6 3.0 %shard_map.149 = (f32[288,2048]{1,0:T(8,128)S(1)}, f32[288,128]{1,0:T(8,128)S(1)}, f32[288,128]{1,0:T(8,128)S(1)}) custom-call(s32[2,1,128]{2,1,0:T(1,128)} %lists_hbm.1, f32[288,2048]{1,0:T(8,128)} %spec_hbm.1), custom_call_target="tpu_custom_call" | custom-call | tf_op jit(solution)/shard_map/pallas_call | solution.py:107
  3.7 4.9 %collective-permute-start = (f32[288,128]{1,0:T(8,128)S(1)}, f32[288,128]{1,0:T(8,128)S(1)}, u32[]{:S(2)}, u32[]{:S(2)}) collective-permute-start(f32[288,128]{1,0:T(8,128)S(1)} %get-tuple-element.16), channel_id=1, source_target_pairs={{0,4},{4,8},{8,12},{12,16},{16,20},{20,24},{24,28},{1,5},{5,9},{9,... | collective-permute-start | bytes 442376 | tf_op jit(solution)/shard_map/ppermute | solution.py:423
  8.5 1.3 %collective-permute-start.1 = (f32[288,128]{1,0:T(8,128)S(1)}, f32[288,128]{1,0:T(8,128)S(1)}, u32[]{:S(2)}, u32[]{:S(2)}) collective-permute-start(f32[288,128]{1,0:T(8,128)S(1)} %get-tuple-element.17), channel_id=1, source_target_pairs={{4,0},{8,4},{12,8},{16,12},{20,16},{24,20},{28,24},{5,1},{9,5},{13... | collective-permute-start | bytes 442376 | tf_op jit(solution)/shard_map/ppermute | solution.py:423
  9.8 3.0 %shard_map.150 = (f32[9216,128]{1,0:T(8,128)S(1)}, f32[8,2056,128]{2,1,0:T(8,128)S(1)}, f32[288,2048]{1,0:T(8,128)S(1)}, s32[16,8,128]{2,1,0:T(8,128)}) custom-call(f32[288,2048]{1,0:T(8,128)S(1)} %get-tuple-element.11.refs_0_.spec_ref, f32[8]{0:T(128)} %refs_1_.1, f32[8]{0:T(128)} %refs_2_.1, f32[16,2048]{1,0:T(8,128)} %bitcast.15, f32[16,128]{1,0:T(8,128)} %bitcast.17, ...), custom_call_target="tpu_custom_call" | custom-call | tf_op jit(solution)/shard_map/pallas_call | solution.py:185
  12.9 0.0 collective-permute-done.prev_ref
  12.9 2.8 %collective-permute-done.1.next_ref = f32[288,128]{1,0:T(8,128)S(1)} collective-permute-done((f32[288,128]{1,0:T(8,128)S(1)}, f32[288,128]{1,0:T(8,128)S(1)}, u32[]{:S(2)}, u32[]{:S(2)}) %collective-permute-start.1) | collective-permute-done | bytes 147488 | tf_op jit(solution)/shard_map/ppermute | solution.py:423
  15.7 15.8 %shard_map.151 = (f32[288,2048]{1,0:T(8,128)}, f32[40,2048]{1,0:T(8,128)S(1)}, f32[9216,128]{1,0:T(8,128)S(1)}) custom-call(f32[8]{0:T(128)} %speed_hbm.1, s32[16,8,128]{2,1,0:T(8,128)} %get-tuple-element.12.index_hbm, f32[40,288]{1,0:T(8,128)} %kernel_hbm.1, f32[9216,128]{1,0:T(8,128)S(1)} %get-tuple-element.13.table_in, ...), custom_call_target="tpu_custom_call", output_to_operand_aliasing={{2}: (3, {})} | custom-call | tf_op jit(solution)/shard_map/pallas_call | solution.py:322
  31.6 0.0 copy-start
  31.6 0.1 collective-permute-start.2
  31.7 1.3 %constant_dynamic-slice_fusion = f32[32,64,128]{2,1,0:T(8,128)S(1)} fusion(f32[32,64,512]{2,1,0:T(8,128)} %param.25, s32[]{:T(128)S(6)} %select_n.75), kind=kLoop, calls=%fused_computation.22 | loop fusion | bytes 2097156 | tf_op jit(solution)/shard_map/dynamic_slice | solution.py:460
  33.0 0.1 collective-permute-done.2
  33.1 1.6 %collective-permute-start.3 = (f32[40,1024]{1,0:T(8,128)S(1)}, f32[40,1024]{1,0:T(8,128)S(1)}, u32[]{:S(2)}, u32[]{:S(2)}) collective-permute-start(f32[40,1024]{1,0:T(8,128)S(1)} %select_add_fusion), channel_id=1, source_target_pairs={{0,2},{1,3},{2,0},{3,1},{4,6},{5,7},{6,4},{7,5},{8,10},{9,11},{10,... | collective-permute-start | bytes 491528 | tf_op jit(solution)/shard_map/ppermute | solution.py:378
  34.7 0.2 fusion
  34.9 4.8 %collective-permute-done.3 = f32[40,1024]{1,0:T(8,128)S(1)} collective-permute-done((f32[40,1024]{1,0:T(8,128)S(1)}, f32[40,1024]{1,0:T(8,128)S(1)}, u32[]{:S(2)}, u32[]{:S(2)}) %collective-permute-start.3) | collective-permute-done | bytes 163872 | tf_op jit(solution)/shard_map/ppermute | solution.py:378
  39.7 0.1 collective-permute-start.4
  39.8 0.0 copy-done
  39.9 1.3 %collective-permute-done.4 = f32[40,1024]{1,0:T(8,128)S(1)} collective-permute-done((f32[40,1024]{1,0:T(8,128)S(1)}, f32[40,1024]{1,0:T(8,128)S(1)}, u32[]{:S(2)}, u32[]{:S(2)}) %collective-permute-start.4) | collective-permute-done | bytes 163872 | tf_op jit(solution)/shard_map/ppermute | solution.py:378
  41.3 1.2 %shard_map.152 = f32[32,40,128]{2,1,0:T(8,128)S(1)} custom-call(s32[32]{0:T(128)S(1)} %fusion.2.slot_ref, f32[40,2048]{1,0:T(8,128)S(1)} %pad_maximum_fusion.stokes_ref, bf16[2048,128]{1,0:T(8,128)(2,1)S(1)} %get-tuple-element.21.high_ref, bf16[2048,128]{1,0:T(8,128)(2,1)S(1)} %get-tuple-element.20.low_ref), custom_call_target="tpu_custom_call" | custom-call | tf_op jit(solution)/shard_map/pallas_call | solution.py:367
  42.5 2.5 %collective-permute-start.5 = (f32[4,4,40,128]{3,2,1,0:T(8,128)S(1)}, f32[4,4,40,128]{3,2,1,0:T(8,128)S(1)}, u32[]{:S(2)}, u32[]{:S(2)}) collective-permute-start(f32[4,4,40,128]{3,2,1,0:T(8,128)S(1)} %bitcast.14), channel_id=1, source_target_pairs={{0,4},{1,9},{2,6},{3,11},{4,0},{5,13},{6,2},{7,15},{8,12},{9,1},{1... | collective-permute-start | bytes 983048 | tf_op jit(solution)/shard_map/ppermute | solution.py:410
  45.0 5.1 %collective-permute-done.5 = f32[4,4,40,128]{3,2,1,0:T(8,128)S(1)} collective-permute-done((f32[4,4,40,128]{3,2,1,0:T(8,128)S(1)}, f32[4,4,40,128]{3,2,1,0:T(8,128)S(1)}, u32[]{:S(2)}, u32[]{:S(2)}) %collective-permute-start.5) | collective-permute-done | bytes 327712 | tf_op jit(solution)/shard_map/ppermute | solution.py:410
  50.2 2.2 %collective-permute-start.6 = (f32[2,4,40,128]{3,2,1,0:T(8,128)S(1)}, f32[2,4,40,128]{3,2,1,0:T(8,128)S(1)}, u32[]{:S(2)}, u32[]{:S(2)}) collective-permute-start(f32[2,4,40,128]{3,2,1,0:T(8,128)S(1)} %slice.43), channel_id=1, source_target_pairs={{0,8},{1,5},{2,10},{3,7},{4,12},{5,1},{6,14},{7,3},{8,0},{9,13},{1... | collective-permute-start | bytes 491528 | tf_op jit(solution)/shard_map/ppermute | solution.py:410
  52.3 3.3 %collective-permute-done.6 = f32[2,4,40,128]{3,2,1,0:T(8,128)S(1)} collective-permute-done((f32[2,4,40,128]{3,2,1,0:T(8,128)S(1)}, f32[2,4,40,128]{3,2,1,0:T(8,128)S(1)}, u32[]{:S(2)}, u32[]{:S(2)}) %collective-permute-start.6) | collective-permute-done | bytes 163872 | tf_op jit(solution)/shard_map/ppermute | solution.py:410
  55.7 3.1 %collective-permute-start.7 = (f32[1,4,40,128]{3,2,1,0:T(8,128)S(1)}, f32[1,4,40,128]{3,2,1,0:T(8,128)S(1)}, u32[]{:S(2)}, u32[]{:S(2)}) collective-permute-start(f32[1,4,40,128]{3,2,1,0:T(8,128)S(1)} %slice.45), channel_id=1, source_target_pairs={{0,16},{1,17},{2,18},{3,19},{4,20},{5,21},{6,22},{7,23},{8,24},{9,... | collective-permute-start | bytes 245768 | tf_op jit(solution)/shard_map/ppermute | solution.py:410
  58.8 2.4 %collective-permute-done.7 = f32[1,4,40,128]{3,2,1,0:T(8,128)S(1)} collective-permute-done((f32[1,4,40,128]{3,2,1,0:T(8,128)S(1)}, f32[1,4,40,128]{3,2,1,0:T(8,128)S(1)}, u32[]{:S(2)}, u32[]{:S(2)}) %collective-permute-start.7) | collective-permute-done | bytes 81952 | tf_op jit(solution)/shard_map/ppermute | solution.py:410
  61.2 0.6 %fusion.1 = f32[4,40,128]{2,1,0:T(8,128)} fusion(f32[1,4,40,128]{3,2,1,0:T(8,128)S(1)} %collective-permute-done.7, f32[2,4,40,128]{3,2,1,0:T(8,128)S(1)} %slice_add_fusion), kind=kLoop, calls=%fused_computation.8 | loop fusion | flops 20480 | bytes 245760 | tf_op jit(solution)/shard_map/squeeze | solution.py:417
  (11 shorter events, 0.3 us)
Async XLA Ops:
  3.7 9.2 %collective-permute-start = (f32[288,128]{1,0:T(8,128)S(1)}, f32[288,128]{1,0:T(8,128)S(1)}, u32[]{:S(2)}, u32[]{:S(2)}) collective-permute-start(f32[288,128]{1,0:T(8,128)S(1)} %get-tuple-element.16), channel_id=1, source_target_pairs={{0,4},{4,8},{8,12},{12,16},{16,20},{20,24},{24,28},{1,5},{5,9},{9,... | collective-permute-start | bytes 442376 | tf_op jit(solution)/shard_map/ppermute | solution.py:423
  8.5 7.2 %collective-permute-start.1 = (f32[288,128]{1,0:T(8,128)S(1)}, f32[288,128]{1,0:T(8,128)S(1)}, u32[]{:S(2)}, u32[]{:S(2)}) collective-permute-start(f32[288,128]{1,0:T(8,128)S(1)} %get-tuple-element.17), channel_id=1, source_target_pairs={{4,0},{8,4},{12,8},{16,12},{20,16},{24,20},{28,24},{5,1},{9,5},{13... | collective-permute-start | bytes 442376 | tf_op jit(solution)/shard_map/ppermute | solution.py:423
  31.6 8.2 %copy-start = (s32[32]{0:T(128)S(1)}, s32[32]{0:T(128)}, u32[]{:S(2)}) copy-start(s32[32]{0:T(128)} %param.24) | copy-start | bytes 388
  31.6 1.5 %collective-permute-start.2 = (f32[40,1024]{1,0:T(8,128)S(1)}, f32[40,1024]{1,0:T(8,128)S(1)}, u32[]{:S(2)}, u32[]{:S(2)}) collective-permute-start(f32[40,1024]{1,0:T(8,128)S(1)} %slice_select_fusion), channel_id=1, source_target_pairs={{0,1},{1,0},{2,3},{3,2},{4,5},{5,4},{6,7},{7,6},{8,9},{9,8},{10,11... | collective-permute-start | bytes 491528 | tf_op jit(solution)/shard_map/ppermute | solution.py:378
  33.1 6.6 %collective-permute-start.3 = (f32[40,1024]{1,0:T(8,128)S(1)}, f32[40,1024]{1,0:T(8,128)S(1)}, u32[]{:S(2)}, u32[]{:S(2)}) collective-permute-start(f32[40,1024]{1,0:T(8,128)S(1)} %select_add_fusion), channel_id=1, source_target_pairs={{0,2},{1,3},{2,0},{3,1},{4,6},{5,7},{6,4},{7,5},{8,10},{9,11},{10,... | collective-permute-start | bytes 491528 | tf_op jit(solution)/shard_map/ppermute | solution.py:378
  39.7 1.5 %collective-permute-start.4 = (f32[40,1024]{1,0:T(8,128)S(1)}, f32[40,1024]{1,0:T(8,128)S(1)}, u32[]{:S(2)}, u32[]{:S(2)}) collective-permute-start(f32[40,1024]{1,0:T(8,128)S(1)} %add.52), channel_id=1, source_target_pairs={{0,1},{1,0},{2,3},{3,2},{4,5},{5,4},{6,7},{7,6},{8,9},{9,8},{10,11... | collective-permute-start | bytes 491528 | tf_op jit(solution)/shard_map/ppermute | solution.py:378
  42.5 7.6 %collective-permute-start.5 = (f32[4,4,40,128]{3,2,1,0:T(8,128)S(1)}, f32[4,4,40,128]{3,2,1,0:T(8,128)S(1)}, u32[]{:S(2)}, u32[]{:S(2)}) collective-permute-start(f32[4,4,40,128]{3,2,1,0:T(8,128)S(1)} %bitcast.14), channel_id=1, source_target_pairs={{0,4},{1,9},{2,6},{3,11},{4,0},{5,13},{6,2},{7,15},{8,12},{9,1},{1... | collective-permute-start | bytes 983048 | tf_op jit(solution)/shard_map/ppermute | solution.py:410
  50.2 5.5 %collective-permute-start.6 = (f32[2,4,40,128]{3,2,1,0:T(8,128)S(1)}, f32[2,4,40,128]{3,2,1,0:T(8,128)S(1)}, u32[]{:S(2)}, u32[]{:S(2)}) collective-permute-start(f32[2,4,40,128]{3,2,1,0:T(8,128)S(1)} %slice.43), channel_id=1, source_target_pairs={{0,8},{1,5},{2,10},{3,7},{4,12},{5,1},{6,14},{7,3},{8,0},{9,13},{1... | collective-permute-start | bytes 491528 | tf_op jit(solution)/shard_map/ppermute | solution.py:410
  55.7 5.5 %collective-permute-start.7 = (f32[1,4,40,128]{3,2,1,0:T(8,128)S(1)}, f32[1,4,40,128]{3,2,1,0:T(8,128)S(1)}, u32[]{:S(2)}, u32[]{:S(2)}) collective-permute-start(f32[1,4,40,128]{3,2,1,0:T(8,128)S(1)} %slice.45), channel_id=1, source_target_pairs={{0,16},{1,17},{2,18},{3,19},{4,20},{5,21},{6,22},{7,23},{8,24},{9,... | collective-permute-start | bytes 245768 | tf_op jit(solution)/shard_map/ppermute | solution.py:410

commit v4 on v3

--- a/solution.py
+++ b/solution.py
@@ -14,7 +14,7 @@
 TPW = 4
 LANES = 128
 UNROLL = 128
-WIDTH = 512
+WIDTH = 1024
 PAIR = 2 * ND
 BF = jnp.bfloat16
 F32 = jnp.float32
@@ -70,7 +70,9 @@
     return copies
 
 
-def pick_kernel(lists_hbm, spec_hbm, spec_ref, next_ref, prev_ref, lists_ref, sems, small_sems):
+def pick_kernel(
+    lists_hbm, spec_hbm, spec_ref, first_ref, second_ref, lists_ref, chosen, sems, small_sems
+):
     points = spec_ref.shape[1]
     chunks = sems.shape[0]
     width = points // chunks
@@ -86,19 +88,23 @@
     for copy in copies:
         copy.start()
     lists_copy.wait()
-    count = next_ref.shape[1]
-    lists = jnp.concatenate([lists_ref[0], lists_ref[1]], 1)
+    count = first_ref.shape[1]
+    odd = lax.axis_index("wave") % 2
+    lists = jnp.concatenate([lists_ref[odd], lists_ref[1 - odd]], 1)
+    for start in range(0, points, LANES):
+        ids = lax.broadcasted_iota(jnp.int32, (LANES, 2 * count), 0) + start
+        chosen[start : start + LANES, :] = jnp.where(ids == lists, 1.0, 0.0).astype(BF)
     total = None
     for chunk in range(chunks):
         copies[chunk].wait()
-        part = spec_ref[:, chunk * width : (chunk + 1) * width]
-        first, second = split2(part)
-        ids = lax.broadcasted_iota(jnp.int32, (width, 2 * count), 0) + chunk * width
-        chosen = jnp.where(ids == lists, 1.0, 0.0).astype(BF)
-        found = dot(first, chosen) + dot(second, chosen)
+        part = slice(chunk * width, (chunk + 1) * width)
+        high, low = split2(spec_ref[:, part])
+        found = dot(jnp.concatenate([high, low], 0), chosen[part, :])
         total = found if total is None else total + found
-    next_ref[...] = total[:, :count]
-    prev_ref[...] = total[:, count:]
+    bins = spec_ref.shape[0]
+    total = total[:bins] + total[bins:]
+    first_ref[...] = total[:, :count]
+    second_ref[...] = total[:, count:]
 
 
 def pick_halo(spectrum, lists):
@@ -111,7 +117,8 @@
         out_shape=[vmem((bins, points)), halo, halo],
         scratch_shapes=[
             pltpu.VMEM(lists.shape, jnp.int32),
-            pltpu.SemaphoreType.DMA((4,)),
+            pltpu.VMEM((points, 2 * lists.shape[-1]), BF),
+            pltpu.SemaphoreType.DMA((2,)),
             pltpu.SemaphoreType.DMA((1,)),
         ],
         compiler_params=params(8),
@@ -119,11 +126,16 @@
 
 
 def prepare_kernel(*refs):
-    spec_ref, operands = refs[0], refs[1:9]
-    table, inflow, gain, index_out = refs[9:13]
-    scratch, (turn, sems, index_sem) = refs[13:21], refs[21:]
-    copies = start_all(operands, scratch, sems)
-    coef_ref, loss_ref, edge_ref, wind_ref, friction_ref, weight_ref, facing_ref, index_ref = scratch
+    spec_ref, operands, blocks_hbm = refs[0], refs[1:11], refs[11]
+    table, inflow, gain, index_ref, speed_rows, kernel_both, high_ref, low_ref = refs[12:20]
+    scratch, (weights_ref, turn, sems, weights_sem) = refs[20:29], refs[29:]
+    copies = start_all(operands, (*scratch, index_ref), sems)
+    cells = high_ref.shape[1]
+    mine = pl.ds(pl.multiple_of(lax.axis_index("grp") * cells, LANES), cells)
+    weights_copy = pltpu.make_async_copy(blocks_hbm.at[:, :, mine], weights_ref, weights_sem)
+    weights_copy.start()
+    coef_ref, loss_ref, speed_ref, edge_ref, wind_ref, friction_ref = scratch[:6]
+    weight_ref, facing_ref, kernel_ref = scratch[6:]
     bins, points = gain.shape
     groups = bins // PAIR
     slots = inflow.shape[0]
@@ -140,13 +152,15 @@
     for copy in copies:
         copy.wait()
     index_ref[...] = index_ref[...] * groups
-    index_copy = pltpu.make_async_copy(index_ref, index_out, index_sem)
-    index_copy.start()
+    kernel_high, kernel_low = split2(kernel_ref[...])
+    kernel_both[...] = jnp.concatenate([kernel_high, kernel_low], 0)
     lower = lax.broadcasted_iota(jnp.int32, (PAIR, LANES), 0) < ND
 
     def per_bin(ref, group):
         return jnp.where(lower, ref[2 * group], ref[2 * group + 1])
 
+    for group in range(groups):
+        speed_rows[group * PAIR : (group + 1) * PAIR, :] = per_bin(speed_ref, group)
     coef = [per_bin(coef_ref, group) for group in range(groups)]
     loss = [per_bin(loss_ref, group) for group in range(groups)]
     turn[0] = jnp.cos(wind_ref[...])
@@ -172,91 +186,99 @@
                 coef[group] * pushed - loss[group]
             )
 
-    index_copy.wait()
-
-
-def prepare(spectrum, coef, loss, edges, wind, friction, index, rows):
+    weights_copy.wait()
+    count, block_rows, _ = weights_ref.shape
+
+    @pl.loop(0, count, unroll=8)
+    def _(block):
+        high, low = split2(weights_ref[block])
+        rows = pl.ds(pl.multiple_of(block * block_rows, block_rows), block_rows)
+        high_ref[rows, :] = high
+        low_ref[rows, :] = low
+
+
+def prepare(spectrum, coef, loss, speed, edges, wind, friction, kernel, index, blocks, rows):
     bins, points = spectrum.shape
     slots = edges.shape[0] // 2
     weight, facing = direction_constants(slots)
     shape = (points // LANES, LANES)
-    operands = [edges, wind.reshape(shape), friction.reshape(shape), weight, facing, index]
+    operands = [edges, wind.reshape(shape), friction.reshape(shape), weight, facing, kernel]
     operands = [jnp.asarray(operand) for operand in operands]
+    count, block_rows, tile_cells = blocks.shape
+    cells = tile_cells // lax.axis_size("grp")
     return pl.pallas_call(
         prepare_kernel,
-        in_specs=[VMEM] + [ANY] * 8,
-        out_specs=[VMEM, VMEM, VMEM, ANY],
+        in_specs=[VMEM] + [ANY] * 11,
+        out_specs=[VMEM] * 8,
         out_shape=[
             vmem((rows, LANES)),
             vmem((slots, points + 8, LANES)),
             vmem((bins, points)),
-            pltpu.HBM(index.shape, index.dtype),
+            vmem(index.shape, jnp.int32),
+            vmem((bins, LANES)),
+            vmem((2 * kernel.shape[0], bins), BF),
+            vmem((count * block_rows, cells), BF),
+            vmem((count * block_rows, cells), BF),
         ],
         scratch_shapes=[
-            pltpu.SMEM(coef.shape, F32),
-            pltpu.SMEM(loss.shape, F32),
+            *[pltpu.SMEM(operand.shape, F32) for operand in (coef, loss, speed)],
             *[pltpu.VMEM(operand.shape, operand.dtype) for operand in operands],
+            pltpu.VMEM((count, block_rows, cells), F32),
             pltpu.VMEM((2, *shape), F32),
-            pltpu.SemaphoreType.DMA((8,)),
+            pltpu.SemaphoreType.DMA((10,)),
             pltpu.SemaphoreType.DMA(()),
         ],
-        compiler_params=params(6),
-    )(spectrum, *in_hbm(coef, loss, *operands))
+        compiler_params=params(8),
+    )(spectrum, *in_hbm(coef, loss, speed, *operands, index, blocks))
 
 
 def advance_kernel(
-    speed_hbm,
-    index_hbm,
-    kernel_hbm,
+    index_vmem,
     table_in,
     inflow,
     spec_ref,
     gain_ref,
-    prev_ref,
-    next_ref,
+    speed_rows,
+    kernel_both,
+    first_ref,
+    second_ref,
     updated_ref,
-    stokes_ref,
+    keep_ref,
+    send_ref,
     table,
-    speed_ref,
-    kernel_ref,
     index_ref,
     gathered,
     result,
     sems,
     index_sems,
-    small_sems,
     *,
     unroll,
 ):
     bins, points = spec_ref.shape
     groups = bins // PAIR
     slots = inflow.shape[0]
-    halo = prev_ref.shape[1]
+    halo = first_ref.shape[1]
     blocks = points // LANES
+    depth = keep_ref.shape[0]
     filler = jnp.zeros((LANES - PAIR, LANES), F32)
 
     def fetch(block):
-        return pltpu.make_async_copy(index_hbm.at[block], index_ref.at[block], index_sems.at[block])
+        return pltpu.make_async_copy(
+            index_vmem.at[block], index_ref.at[block], index_sems.at[block]
+        )
 
     @pl.loop(0, blocks)
     def _(block):
         fetch(block).start()
 
-    small = start_all([speed_hbm, kernel_hbm], [speed_ref, kernel_ref], small_sems)
-
-    for number, ref in enumerate((prev_ref, next_ref)):
+    right = lax.axis_index("wave") % 2
+    for number, ref in ((1 - right, first_ref), (right, second_ref)):
         for group in range(groups):
             part = jnp.concatenate([ref[group * PAIR : (group + 1) * PAIR, :], filler], 0).T
             start = (points + number * halo) * groups + group
             table[pl.ds(start, halo, stride=groups), :] = part
 
-    for copy in small:
-        copy.wait()
-    kernel_high, kernel_low = split2(kernel_ref[...])
-    kernel_both = jnp.concatenate([kernel_high, kernel_low], 0)
-    depth = kernel_ref.shape[0]
-    lower = lax.broadcasted_iota(jnp.int32, (PAIR, LANES), 0) < ND
-
+    odd = lax.axis_index("grp") % 2
     width = result.shape[2]
 
     def copy_out(part, group):
@@ -288,7 +310,6 @@
 
     @pl.loop(0, points // width)
     def _(part):
-        columns = pl.ds(pl.multiple_of(part * width, width), width)
         several = width // LANES
 
         @pl.loop(0, several)
@@ -297,7 +318,7 @@
 
         for group in range(groups):
             rows = slice(group * PAIR, (group + 1) * PAIR)
-            speed = jnp.where(lower, speed_ref[2 * group], speed_ref[2 * group + 1])
+            speed = speed_rows[rows, :]
             for step in range(several):
                 inner = slice(step * LANES, (step + 1) * LANES)
                 outer = pl.ds(pl.multiple_of(part * width + step * LANES, LANES), LANES)
@@ -306,8 +327,19 @@
                 result[part, rows, inner] = advected * gain_ref[rows, outer]
             copy_out(part, group).start()
         high, low = split2(result[part])
-        both = dot(kernel_both, high)
-        stokes_ref[:, columns] = both[:depth] + both[depth:] + dot(kernel_high, low)
+        both = dot(kernel_both[...], high)
+        stokes = both[:depth] + both[depth:] + dot(kernel_both[:depth, :], low)
+        half_parts = points // width // 2
+        local = pl.ds(pl.multiple_of(lax.rem(part, half_parts) * width, width), width)
+        kept = (part >= half_parts) == (odd == 1)
+
+        @pl.when(kept)
+        def _():
+            keep_ref[:, local] = stokes
+
+        @pl.when(jnp.logical_not(kept))
+        def _():
+            send_ref[:, local] = stokes
 
     @pl.loop(0, points // width)
     def _(part):
@@ -315,62 +347,57 @@
             copy_out(part, group).wait()
 
 
-def advance(speed, index, table, inflow, spectrum, gain, prev, nxt, kernel):
+def advance(index, table, inflow, spectrum, gain, speed_rows, kernel_both, first, second):
     bins, points = spectrum.shape
     groups = bins // PAIR
     blocks = points // LANES
+    half = jax.ShapeDtypeStruct((kernel_both.shape[0] // 2, points // 2), F32)
     return pl.pallas_call(
         functools.partial(advance_kernel, unroll=UNROLL),
-        in_specs=[ANY] * 3 + [VMEM] * 6,
-        out_specs=[ANY, VMEM, VMEM],
-        out_shape=[
-            jax.ShapeDtypeStruct((bins, points), F32),
-            jax.ShapeDtypeStruct((kernel.shape[0], points), F32),
-            vmem(table.shape),
-        ],
-        input_output_aliases={3: 2},
+        in_specs=[VMEM] * 9,
+        out_specs=[ANY, VMEM, VMEM, VMEM],
+        out_shape=[jax.ShapeDtypeStruct((bins, points), F32), half, half, vmem(table.shape)],
+        input_output_aliases={1: 3},
         scratch_shapes=[
-            pltpu.SMEM(speed.shape, F32),
-            pltpu.VMEM(kernel.shape, F32),
             pltpu.SMEM(index.shape, jnp.int32),
             pltpu.VMEM((WIDTH * groups, LANES), F32),
             pltpu.VMEM((points // WIDTH, bins, WIDTH), F32),
             pltpu.SemaphoreType.DMA((points // WIDTH, groups)),
             pltpu.SemaphoreType.DMA((blocks,)),
-            pltpu.SemaphoreType.DMA((2,)),
         ],
-        compiler_params=params(10),
-    )(*in_hbm(speed, index, kernel), table, inflow, spectrum, gain, prev, nxt)
-
-
-def regrid_kernel(slot_ref, stokes_ref, high_ref, low_ref, out_ref, *, block_rows):
-    depth = stokes_ref.shape[0]
+        compiler_params=params(12),
+    )(index, table, inflow, spectrum, gain, speed_rows, kernel_both, first, second)
+
+
+def regrid_kernel(slot_ref, mine_ref, other_ref, high_ref, low_ref, out_ref, *, block_rows):
+    depth, points = mine_ref.shape
+    pairs = points // LANES
+    odd = lax.axis_index("grp") % 2
     out_ref[...] = jnp.zeros(out_ref.shape, F32)
     lower = lax.broadcasted_iota(jnp.int32, (depth, LANES), 1) < block_rows
-    for pair in range(stokes_ref.shape[1] // LANES):
-        columns = slice(pair * LANES, (pair + 1) * LANES)
-        part = stokes_ref[:, columns]
-        both = jnp.concatenate([jnp.where(lower, part, 0.0), jnp.where(lower, 0.0, part)], 0)
-        high, low = split2(both)
-        terms = (
-            dot(high, high_ref[columns, :])
-            + dot(low, high_ref[columns, :])
-            + dot(high, low_ref[columns, :])
-        )
-        for half in range(2):
-            slot = slot_ref[2 * pair + half]
-            out_ref[slot] = out_ref[slot] + terms[half * depth : (half + 1) * depth]
-
-
-def regrid(slots, stokes, high, low, count, block_rows):
-    depth = stokes.shape[0]
+    for ref, half in ((mine_ref, odd), (other_ref, 1 - odd)):
+        for pair in range(pairs):
+            part = ref[:, pair * LANES : (pair + 1) * LANES]
+            both = jnp.concatenate([jnp.where(lower, part, 0.0), jnp.where(lower, 0.0, part)], 0)
+            high, low = split2(both)
+            place = half * pairs + pair
+            rows = pl.ds(pl.multiple_of(place * LANES, LANES), LANES)
+            terms = (
+                dot(high, high_ref[rows, :]) + dot(low, high_ref[rows, :]) + dot(high, low_ref[rows, :])
+            )
+            for side in range(2):
+                slot = slot_ref[2 * place + side]
+                out_ref[slot] = out_ref[slot] + terms[side * depth : (side + 1) * depth]
+
+
+def regrid(slots, mine, other, high, low, count, block_rows):
     return pl.pallas_call(
         functools.partial(regrid_kernel, block_rows=block_rows),
-        in_specs=[SMEM, VMEM, VMEM, VMEM],
+        in_specs=[SMEM] + [VMEM] * 4,
         out_specs=VMEM,
-        out_shape=jax.ShapeDtypeStruct((count, depth, LANES), F32),
+        out_shape=jax.ShapeDtypeStruct((count, mine.shape[0], LANES), F32),
         compiler_params=params(4),
-    )(slots, stokes, high, low)
+    )(slots, mine, other, high, low)
 
 
 def swap(value, axis, bit):
@@ -378,19 +405,13 @@
     return lax.ppermute(value, axis, [(i, i ^ bit) for i in range(count)])
 
 
-def sum_over(value, axis):
-    count = lax.axis_size(axis)
-    me = lax.axis_index(axis)
-    half = value.shape[1] // 2
-    odd = (me & 1) == 1
-    left, right = value[:, :half], value[:, half:]
-    mine = jnp.where(odd, right, left) + swap(jnp.where(odd, left, right), axis, 1)
+def sum_over(keep, send, axis):
+    mine = keep + swap(send, axis, 1)
     bit = 2
-    while bit < count:
+    while bit < lax.axis_size(axis):
         mine = mine + swap(mine, axis, bit)
         bit *= 2
-    other = swap(mine, axis, 1)
-    return jnp.concatenate([jnp.where(odd, other, mine), jnp.where(odd, mine, other)], 1)
+    return mine, swap(mine, axis, 1)
 
 
 def places(relative, bits):
@@ -417,10 +438,11 @@
     return parts[0]
 
 
-def shift(value, axis, steps):
-    count = lax.axis_size(axis)
-    leading, last = (max(0, -steps), min(count, count - steps))
-    return lax.ppermute(value, axis, [(source, source + steps) for source in range(leading, last)])
+def swap_halo(first, second):
+    count = lax.axis_size("wave")
+    first = swap(first, "wave", 1)
+    inner = [(i, i + 1 if i % 2 else i - 1) for i in range(1, count - 1)]
+    return first, lax.ppermute(second, "wave", inner)
 
 
 def body(
@@ -438,38 +460,41 @@
     block_weights,
 ):
     n_wave = lax.axis_size("wave")
-    n_group = lax.axis_size("grp")
     bins, points = spectrum.shape
     groups = bins // PAIR
     slots = neighbours.shape[0]
     rows = (points + 2 * halo_lists.shape[-1]) * groups
-    spectrum, to_next, to_prev = pick_halo(spectrum, halo_lists)
-    from_prev = shift(to_next, "wave", 1)
-    from_next = shift(to_prev, "wave", -1)
+    spectrum, first, second = pick_halo(spectrum, halo_lists)
+    first, second = swap_halo(first, second)
     index = neighbours.reshape(slots, points // LANES, LANES).transpose(1, 0, 2)
     edges = edge_vectors.reshape(2 * slots, points)
-    table, inflow, gain, index = prepare(
-        spectrum, input_coef, dissipation, edges, wind_dir, friction, index, rows
+    table, inflow, gain, index, speed_rows, kernel_both, high, low = prepare(
+        spectrum,
+        input_coef,
+        dissipation,
+        group_speed,
+        edges,
+        wind_dir,
+        friction,
+        drift_kernel,
+        index,
+        block_weights,
+        rows,
     )
-    updated, stokes, _ = advance(
-        group_speed, index, table, inflow, spectrum, gain, from_prev, from_next, drift_kernel
+    updated, keep, send, _ = advance(
+        index, table, inflow, spectrum, gain, speed_rows, kernel_both, first, second
     )
-    stokes = sum_over(stokes, "grp")
-    blocks, block_rows, tile_cells = block_weights.shape
-    cells = tile_cells // n_group
-    mine = lax.dynamic_slice_in_dim(block_weights, lax.axis_index("grp") * cells, cells, 2)
-    mine = mine.reshape(blocks * block_rows, cells)
-    rounded = lax.reduce_precision(mine, 8, 7)
-    high, low = rounded.astype(BF), (mine - rounded).astype(BF)
+    mine, other = sum_over(keep, send, "grp")
     relative = (block_tile // TPW) ^ lax.axis_index("wave")
     tile = block_tile % TPW
-    depth = drift_kernel.shape[0]
     bits = [1 << b for b in range(n_wave.bit_length() - 1)]
     other_bits = bits[1::-1] + bits[2:]
     odd = lax.axis_index("grp") % 2 == 1
     place = jnp.where(odd, places(relative, other_bits), places(relative, bits))
-    parts = regrid(place * TPW + tile, stokes, high, low, n_wave * TPW, block_rows)
-    drift = scatter_sum(parts.reshape(n_wave, TPW, depth, cells), bits, other_bits)
+    block_rows = block_weights.shape[1]
+    parts = regrid(place * TPW + tile, mine, other, high, low, n_wave * TPW, block_rows)
+    parts = parts.reshape(n_wave, TPW, *parts.shape[1:])
+    drift = scatter_sum(parts, bits, other_bits)
     return updated, drift
 
 

time: 62.1 us -> 57.5 us (0.926)
  Pallas kernels: 23.1 us -> 21.2 us
  waiting for transfers between devices: 19.9 us -> 18.1 us
  local copies, waits for them, and re-layouts: 1.37 us -> 0.07 us
  starting transfers between devices: 15.6 us -> 16.5 us
    ppermute x2 -> x1, starting transfers between devices: 6.14 us -> 0.66 us  [swap_halo(): return (first, lax.ppermute(second, 'wave', inner))]
    ppermute x3, starting transfers between devices: 7.76 us -> 11 us  [exchange(): return lax.ppermute(value, ('wave', 'grp'), pairs)]
    ppermute x3 -> x4, starting transfers between devices: 1.72 us -> 4.9 us  [swap(): return lax.ppermute(value, axis, [(i, i ^ bit) for i in range(count)])]
    ppermute x2 -> x1, waiting for transfers between devices: 2.83 us -> 0.01 us  [swap_halo(): return (first, lax.ppermute(second, 'wave', inner))]
    pallas_call x1, Pallas kernels: 15.8 us -> 14.3 us  [advance(): pl.pallas_call(functools.partial(advance_kernel, unroll=UNROLL), in_specs...]
    dynamic_slice x1 -> x0, local copies, waits for them, and re-layouts: 1.3 us -> none  [body(): lax.dynamic_slice_in_dim(block_weights, lax.axis_index('grp') * cells, ce...]
    ppermute x3 -> x4, waiting for transfers between devices: 6.27 us -> 7.29 us  [swap(): return lax.ppermute(value, axis, [(i, i ^ bit) for i in range(count)])]
  transfers between devices with their start and end apart: 8 -> 8, of which waited for: 7 -> 6; matrix products, arithmetic and copies ran while one was open for 2% -> 0% of each run, Pallas kernels for 5% -> 6%
where the time goes in v4:
time: 57.5 us; the launch traced here: 57.3 us
  Pallas kernels  21.2 us (37%)
  waiting for transfers between devices  18.1 us (31%)
  starting transfers between devices  16.5 us (29%)
  other arithmetic  0.77 us (1%)
  between operations  0.76 us (1%)
    pallas_call x1, Pallas kernels, advance(): pl.pallas_call(functools.partial(advance_kernel, unroll=UNROLL), in_specs...  14.3 us
    ppermute x3, starting transfers between devices, exchange(): return lax.ppermute(value, ('wave', 'grp'), pairs)  11 us
    ppermute x3, waiting for transfers between devices, exchange(): return lax.ppermute(value, ('wave', 'grp'), pairs)  10.8 us
    ppermute x4, waiting for transfers between devices, swap(): return lax.ppermute(value, axis, [(i, i ^ bit) for i in range(count)])  7.29 us
    ppermute x4, starting transfers between devices, swap(): return lax.ppermute(value, axis, [(i, i ^ bit) for i in range(count)])  4.9 us
    pallas_call x1, Pallas kernels, prepare(): pl.pallas_call(prepare_kernel, in_specs=[VMEM] + [ANY] * 11, out_specs=[V...  3.22 us
    pallas_call x1, Pallas kernels, pick_halo(): pl.pallas_call(pick_kernel, in_specs=[ANY, ANY], out_specs=[VMEM] * 3, ou...  2.43 us
    pallas_call x1, Pallas kernels, regrid(): pl.pallas_call(functools.partial(regrid_kernel, block_rows=block_rows), i...  1.22 us
  transfers between devices with their start and end apart: 8, of which 6 were waited for; matrix products, arithmetic and copies ran while one was open for 0% of the time, Pallas kernels for 6%

profile of v4, /device:TPU:0, one launch (start us, length us, event | category | flops | bytes accessed | tf_op | source)
XLA Modules:
  0.0 57.3 jit_solution(17183448473247584358)
XLA Ops:
  0.6 2.4 %shard_map.149 = (f32[288,2048]{1,0:T(8,128)S(1)}, f32[288,128]{1,0:T(8,128)S(1)}, f32[288,128]{1,0:T(8,128)S(1)}) custom-call(s32[2,1,128]{2,1,0:T(1,128)} %lists_hbm.1, f32[288,2048]{1,0:T(8,128)} %spec_hbm.1), custom_call_target="tpu_custom_call" | custom-call | tf_op jit(solution)/shard_map/pallas_call | solution.py:113
  3.1 3.0 %collective-permute-start = (f32[288,128]{1,0:T(8,128)S(1)}, f32[288,128]{1,0:T(8,128)S(1)}, u32[]{:S(2)}, u32[]{:S(2)}) collective-permute-start(f32[288,128]{1,0:T(8,128)S(1)} %get-tuple-element.23), channel_id=1, source_target_pairs={{0,4},{4,0},{8,12},{12,8},{16,20},{20,16},{24,28},{28,24},{1,5},{5... | collective-permute-start | bytes 442376 | tf_op jit(solution)/shard_map/ppermute | solution.py:405
  6.1 0.7 %collective-permute-start.1 = (f32[288,128]{1,0:T(8,128)S(1)}, f32[288,128]{1,0:T(8,128)S(1)}, u32[]{:S(2)}, u32[]{:S(2)}) collective-permute-start(f32[288,128]{1,0:T(8,128)S(1)} %get-tuple-element.24), channel_id=1, source_target_pairs={{4,8},{8,4},{12,16},{16,12},{20,24},{24,20},{5,9},{9,5},{13,17},{1... | collective-permute-start | bytes 442376 | tf_op jit(solution)/shard_map/ppermute | solution.py:445
  6.7 3.2 %shard_map.150 = (f32[9216,128]{1,0:T(8,128)S(1)}, f32[8,2056,128]{2,1,0:T(8,128)S(1)}, f32[288,2048]{1,0:T(8,128)S(1)}, s32[16,8,128]{2,1,0:T(8,128)S(1)}, f32[...) custom-call(f32[288,2048]{1,0:T(8,128)S(1)} %get-tuple-element.16.re, ...), custom_call_target="tpu_custom_call" | custom-call | tf_op jit(solution)/shard_map/pallas_call | solution.py:209
  10.0 0.0 collective-permute-done.first_ref
  10.0 0.0 collective-permute-done.1.second_ref
  10.0 0.0 copy-start
  10.0 14.3 %shard_map.151 = (f32[288,2048]{1,0:T(8,128)}, f32[40,1024]{1,0:T(8,128)S(1)}, f32[40,1024]{1,0:T(8,128)S(1)}, f32[9216,128]{1,0:T(8,128)S(1)}) custom-call(s32[16,8,128]{2,1,0:T(8,128)S(1)} %get-tuple-element.17.index_vmem, f32[9216,128]{1,0:T(8,128)S(1)} %get-tuple-element.18.table_in, ...), custom_call_target="tpu_custom_call", output_to_operand_aliasing={{3}: (1, {})} | custom-call | tf_op jit(solution)/shard_map/pallas_call | solution.py:355
  24.3 0.1 collective-permute-start.2
  24.4 1.4 %collective-permute-done.2 = f32[40,1024]{1,0:T(8,128)S(1)} collective-permute-done((f32[40,1024]{1,0:T(8,128)S(1)}, f32[40,1024]{1,0:T(8,128)S(1)}, u32[]{:S(2)}, u32[]{:S(2)}) %collective-permute-start.2) | collective-permute-done | bytes 163872 | tf_op jit(solution)/shard_map/ppermute | solution.py:405
  25.8 1.8 %collective-permute-start.3 = (f32[40,1024]{1,0:T(8,128)S(1)}, f32[40,1024]{1,0:T(8,128)S(1)}, u32[]{:S(2)}, u32[]{:S(2)}) collective-permute-start(f32[40,1024]{1,0:T(8,128)S(1)} %add.48), channel_id=1, source_target_pairs={{0,2},{1,3},{2,0},{3,1},{4,6},{5,7},{6,4},{7,5},{8,10},{9,11},{10,... | collective-permute-start | bytes 491528 | tf_op jit(solution)/shard_map/ppermute | solution.py:405
  27.5 4.6 %collective-permute-done.3 = f32[40,1024]{1,0:T(8,128)S(1)} collective-permute-done((f32[40,1024]{1,0:T(8,128)S(1)}, f32[40,1024]{1,0:T(8,128)S(1)}, u32[]{:S(2)}, u32[]{:S(2)}) %collective-permute-start.3) | collective-permute-done | bytes 163872 | tf_op jit(solution)/shard_map/ppermute | solution.py:405
  32.1 0.1 collective-permute-start.4
  32.2 0.0 copy-done
  32.2 1.3 %collective-permute-done.4.other_ref = f32[40,1024]{1,0:T(8,128)S(1)} collective-permute-done((f32[40,1024]{1,0:T(8,128)S(1)}, f32[40,1024]{1,0:T(8,128)S(1)}, u32[]{:S(2)}, u32[]{:S(2)}) %collective-permute-start.4) | collective-permute-done | bytes 163872 | tf_op jit(solution)/shard_map/ppermute | solution.py:405
  33.6 1.2 %shard_map.152 = f32[32,40,128]{2,1,0:T(8,128)S(1)} custom-call(s32[32]{0:T(128)S(1)} %fusion.1.slot_ref, f32[40,1024]{1,0:T(8,128)S(1)} %add.49.mine_ref, f32[40,1024]{1,0:T(8,128)S(1)} %collective-permute-done.4.other_ref, bf16[2048,128]{1,0:T(8,128)(2,1)S(1)} %get-tuple-element.28.high_ref, bf16[2048,128]{1,0:T(8,128)(2,1)S(1)} %get-tuple-element.29.low_ref), custom_call_target="tpu_custom_call" | custom-call | tf_op jit(solution)/shard_map/pallas_call | solution.py:394
  34.9 4.9 %collective-permute-start.5 = (f32[4,4,40,128]{3,2,1,0:T(8,128)S(1)}, f32[4,4,40,128]{3,2,1,0:T(8,128)S(1)}, u32[]{:S(2)}, u32[]{:S(2)}) collective-permute-start(f32[4,4,40,128]{3,2,1,0:T(8,128)S(1)} %bitcast.11), channel_id=1, source_target_pairs={{0,4},{1,9},{2,6},{3,11},{4,0},{5,13},{6,2},{7,15},{8,12},{9,1},{1... | collective-permute-start | bytes 983048 | tf_op jit(solution)/shard_map/ppermute | solution.py:431
  39.7 5.1 %collective-permute-done.5 = f32[4,4,40,128]{3,2,1,0:T(8,128)S(1)} collective-permute-done((f32[4,4,40,128]{3,2,1,0:T(8,128)S(1)}, f32[4,4,40,128]{3,2,1,0:T(8,128)S(1)}, u32[]{:S(2)}, u32[]{:S(2)}) %collective-permute-start.5) | collective-permute-done | bytes 327712 | tf_op jit(solution)/shard_map/ppermute | solution.py:431
  44.9 3.0 %collective-permute-start.6 = (f32[2,4,40,128]{3,2,1,0:T(8,128)S(1)}, f32[2,4,40,128]{3,2,1,0:T(8,128)S(1)}, u32[]{:S(2)}, u32[]{:S(2)}) collective-permute-start(f32[2,4,40,128]{3,2,1,0:T(8,128)S(1)} %slice.35), channel_id=1, source_target_pairs={{0,8},{1,5},{2,10},{3,7},{4,12},{5,1},{6,14},{7,3},{8,0},{9,13},{1... | collective-permute-start | bytes 491528 | tf_op jit(solution)/shard_map/ppermute | solution.py:431
  47.9 3.3 %collective-permute-done.6 = f32[2,4,40,128]{3,2,1,0:T(8,128)S(1)} collective-permute-done((f32[2,4,40,128]{3,2,1,0:T(8,128)S(1)}, f32[2,4,40,128]{3,2,1,0:T(8,128)S(1)}, u32[]{:S(2)}, u32[]{:S(2)}) %collective-permute-start.6) | collective-permute-done | bytes 163872 | tf_op jit(solution)/shard_map/ppermute | solution.py:431
  51.2 3.0 %collective-permute-start.7 = (f32[1,4,40,128]{3,2,1,0:T(8,128)S(1)}, f32[1,4,40,128]{3,2,1,0:T(8,128)S(1)}, u32[]{:S(2)}, u32[]{:S(2)}) collective-permute-start(f32[1,4,40,128]{3,2,1,0:T(8,128)S(1)} %slice.37), channel_id=1, source_target_pairs={{0,16},{1,17},{2,18},{3,19},{4,20},{5,21},{6,22},{7,23},{8,24},{9,... | collective-permute-start | bytes 245768 | tf_op jit(solution)/shard_map/ppermute | solution.py:431
  54.3 2.4 %collective-permute-done.7 = f32[1,4,40,128]{3,2,1,0:T(8,128)S(1)} collective-permute-done((f32[1,4,40,128]{3,2,1,0:T(8,128)S(1)}, f32[1,4,40,128]{3,2,1,0:T(8,128)S(1)}, u32[]{:S(2)}, u32[]{:S(2)}) %collective-permute-start.7) | collective-permute-done | bytes 81952 | tf_op jit(solution)/shard_map/ppermute | solution.py:431
  56.7 0.6 %fusion = f32[4,40,128]{2,1,0:T(8,128)} fusion(f32[1,4,40,128]{3,2,1,0:T(8,128)S(1)} %collective-permute-done.7, f32[2,4,40,128]{3,2,1,0:T(8,128)S(1)} %slice_add_fusion), kind=kLoop, calls=%fused_computation.2 | loop fusion | flops 20480 | bytes 245760 | tf_op jit(solution)/shard_map/squeeze | solution.py:438
  (8 shorter events, 0.2 us)
Async XLA Ops:
  3.1 6.9 %collective-permute-start = (f32[288,128]{1,0:T(8,128)S(1)}, f32[288,128]{1,0:T(8,128)S(1)}, u32[]{:S(2)}, u32[]{:S(2)}) collective-permute-start(f32[288,128]{1,0:T(8,128)S(1)} %get-tuple-element.23), channel_id=1, source_target_pairs={{0,4},{4,0},{8,12},{12,8},{16,20},{20,16},{24,28},{28,24},{1,5},{5... | collective-permute-start | bytes 442376 | tf_op jit(solution)/shard_map/ppermute | solution.py:405
  6.1 3.9 %collective-permute-start.1 = (f32[288,128]{1,0:T(8,128)S(1)}, f32[288,128]{1,0:T(8,128)S(1)}, u32[]{:S(2)}, u32[]{:S(2)}) collective-permute-start(f32[288,128]{1,0:T(8,128)S(1)} %get-tuple-element.24), channel_id=1, source_target_pairs={{4,8},{8,4},{12,16},{16,12},{20,24},{24,20},{5,9},{9,5},{13,17},{1... | collective-permute-start | bytes 442376 | tf_op jit(solution)/shard_map/ppermute | solution.py:445
  10.0 22.2 %copy-start = (s32[32]{0:T(128)S(1)}, s32[32]{0:T(128)}, u32[]{:S(2)}) copy-start(s32[32]{0:T(128)} %param.24) | copy-start | bytes 388
  24.3 1.5 %collective-permute-start.2 = (f32[40,1024]{1,0:T(8,128)S(1)}, f32[40,1024]{1,0:T(8,128)S(1)}, u32[]{:S(2)}, u32[]{:S(2)}) collective-permute-start(f32[40,1024]{1,0:T(8,128)S(1)} %get-tuple-element.27), channel_id=1, source_target_pairs={{0,1},{1,0},{2,3},{3,2},{4,5},{5,4},{6,7},{7,6},{8,9},{9,8},{10,11... | collective-permute-start | bytes 491528 | tf_op jit(solution)/shard_map/ppermute | solution.py:405
  25.8 6.3 %collective-permute-start.3 = (f32[40,1024]{1,0:T(8,128)S(1)}, f32[40,1024]{1,0:T(8,128)S(1)}, u32[]{:S(2)}, u32[]{:S(2)}) collective-permute-start(f32[40,1024]{1,0:T(8,128)S(1)} %add.48), channel_id=1, source_target_pairs={{0,2},{1,3},{2,0},{3,1},{4,6},{5,7},{6,4},{7,5},{8,10},{9,11},{10,... | collective-permute-start | bytes 491528 | tf_op jit(solution)/shard_map/ppermute | solution.py:405
  32.1 1.5 %collective-permute-start.4 = (f32[40,1024]{1,0:T(8,128)S(1)}, f32[40,1024]{1,0:T(8,128)S(1)}, u32[]{:S(2)}, u32[]{:S(2)}) collective-permute-start(f32[40,1024]{1,0:T(8,128)S(1)} %add.49.mine_ref), channel_id=1, source_target_pairs={{0,1},{1,0},{2,3},{3,2},{4,5},{5,4},{6,7},{7,6},{8,9},{9,8},{10,11... | collective-permute-start | bytes 491528 | tf_op jit(solution)/shard_map/ppermute | solution.py:405
  34.9 9.9 %collective-permute-start.5 = (f32[4,4,40,128]{3,2,1,0:T(8,128)S(1)}, f32[4,4,40,128]{3,2,1,0:T(8,128)S(1)}, u32[]{:S(2)}, u32[]{:S(2)}) collective-permute-start(f32[4,4,40,128]{3,2,1,0:T(8,128)S(1)} %bitcast.11), channel_id=1, source_target_pairs={{0,4},{1,9},{2,6},{3,11},{4,0},{5,13},{6,2},{7,15},{8,12},{9,1},{1... | collective-permute-start | bytes 983048 | tf_op jit(solution)/shard_map/ppermute | solution.py:431
  44.9 6.3 %collective-permute-start.6 = (f32[2,4,40,128]{3,2,1,0:T(8,128)S(1)}, f32[2,4,40,128]{3,2,1,0:T(8,128)S(1)}, u32[]{:S(2)}, u32[]{:S(2)}) collective-permute-start(f32[2,4,40,128]{3,2,1,0:T(8,128)S(1)} %slice.35), channel_id=1, source_target_pairs={{0,8},{1,5},{2,10},{3,7},{4,12},{5,1},{6,14},{7,3},{8,0},{9,13},{1... | collective-permute-start | bytes 491528 | tf_op jit(solution)/shard_map/ppermute | solution.py:431
  51.2 5.5 %collective-permute-start.7 = (f32[1,4,40,128]{3,2,1,0:T(8,128)S(1)}, f32[1,4,40,128]{3,2,1,0:T(8,128)S(1)}, u32[]{:S(2)}, u32[]{:S(2)}) collective-permute-start(f32[1,4,40,128]{3,2,1,0:T(8,128)S(1)} %slice.37), channel_id=1, source_target_pairs={{0,16},{1,17},{2,18},{3,19},{4,20},{5,21},{6,22},{7,23},{8,24},{9,... | collective-permute-start | bytes 245768 | tf_op jit(solution)/shard_map/ppermute | solution.py:431

commit v5 on v4

--- a/solution.py
+++ b/solution.py
@@ -127,8 +127,8 @@
 
 def prepare_kernel(*refs):
     spec_ref, operands, blocks_hbm = refs[0], refs[1:11], refs[11]
-    table, inflow, gain, index_ref, speed_rows, kernel_both, high_ref, low_ref = refs[12:20]
-    scratch, (weights_ref, turn, sems, weights_sem) = refs[20:29], refs[29:]
+    table, inflow, gain, index_out, speed_rows, kernel_both, high_ref, low_ref = refs[12:20]
+    scratch, (index_ref, weights_ref, turn, sems, weights_sem, index_sem) = refs[20:29], refs[29:]
     copies = start_all(operands, (*scratch, index_ref), sems)
     cells = high_ref.shape[1]
     mine = pl.ds(pl.multiple_of(lax.axis_index("grp") * cells, LANES), cells)
@@ -152,6 +152,8 @@
     for copy in copies:
         copy.wait()
     index_ref[...] = index_ref[...] * groups
+    index_copy = pltpu.make_async_copy(index_ref, index_out, index_sem)
+    index_copy.start()
     kernel_high, kernel_low = split2(kernel_ref[...])
     kernel_both[...] = jnp.concatenate([kernel_high, kernel_low], 0)
     lower = lax.broadcasted_iota(jnp.int32, (PAIR, LANES), 0) < ND
@@ -196,6 +198,8 @@
         high_ref[rows, :] = high
         low_ref[rows, :] = low
 
+    index_copy.wait()
+
 
 def prepare(spectrum, coef, loss, speed, edges, wind, friction, kernel, index, blocks, rows):
     bins, points = spectrum.shape
@@ -209,12 +213,12 @@
     return pl.pallas_call(
         prepare_kernel,
         in_specs=[VMEM] + [ANY] * 11,
-        out_specs=[VMEM] * 8,
+        out_specs=[VMEM] * 3 + [SMEM] + [VMEM] * 4,
         out_shape=[
             vmem((rows, LANES)),
             vmem((slots, points + 8, LANES)),
             vmem((bins, points)),
-            vmem(index.shape, jnp.int32),
+            pltpu.SMEM(index.shape, jnp.int32),
             vmem((bins, LANES)),
             vmem((2 * kernel.shape[0], bins), BF),
             vmem((count * block_rows, cells), BF),
@@ -223,17 +227,19 @@
         scratch_shapes=[
             *[pltpu.SMEM(operand.shape, F32) for operand in (coef, loss, speed)],
             *[pltpu.VMEM(operand.shape, operand.dtype) for operand in operands],
+            pltpu.VMEM(index.shape, jnp.int32),
             pltpu.VMEM((count, block_rows, cells), F32),
             pltpu.VMEM((2, *shape), F32),
             pltpu.SemaphoreType.DMA((10,)),
             pltpu.SemaphoreType.DMA(()),
+            pltpu.SemaphoreType.DMA(()),
         ],
         compiler_params=params(8),
     )(spectrum, *in_hbm(coef, loss, speed, *operands, index, blocks))
 
 
 def advance_kernel(
-    index_vmem,
+    index_ref,
     table_in,
     inflow,
     spec_ref,
@@ -246,11 +252,9 @@
     keep_ref,
     send_ref,
     table,
-    index_ref,
     gathered,
     result,
     sems,
-    index_sems,
     *,
     unroll,
 ):
@@ -262,15 +266,6 @@
     depth = keep_ref.shape[0]
     filler = jnp.zeros((LANES - PAIR, LANES), F32)
 
-    def fetch(block):
-        return pltpu.make_async_copy(
-            index_vmem.at[block], index_ref.at[block], index_sems.at[block]
-        )
-
-    @pl.loop(0, blocks)
-    def _(block):
-        fetch(block).start()
-
     right = lax.axis_index("wave") % 2
     for number, ref in ((1 - right, first_ref), (right, second_ref)):
         for group in range(groups):
@@ -289,7 +284,6 @@
         )
 
     def gather(block, start):
-        fetch(block).wait()
         base = pl.multiple_of(block * LANES, LANES)
 
         @pl.loop(0, LANES // unroll)
@@ -354,16 +348,14 @@
     half = jax.ShapeDtypeStruct((kernel_both.shape[0] // 2, points // 2), F32)
     return pl.pallas_call(
         functools.partial(advance_kernel, unroll=UNROLL),
-        in_specs=[VMEM] * 9,
+        in_specs=[SMEM] + [VMEM] * 8,
         out_specs=[ANY, VMEM, VMEM, VMEM],
         out_shape=[jax.ShapeDtypeStruct((bins, points), F32), half, half, vmem(table.shape)],
         input_output_aliases={1: 3},
         scratch_shapes=[
-            pltpu.SMEM(index.shape, jnp.int32),
             pltpu.VMEM((WIDTH * groups, LANES), F32),
             pltpu.VMEM((points // WIDTH, bins, WIDTH), F32),
             pltpu.SemaphoreType.DMA((points // WIDTH, groups)),
-            pltpu.SemaphoreType.DMA((blocks,)),
         ],
         compiler_params=params(12),
     )(index, table, inflow, spectrum, gain, speed_rows, kernel_both, first, second)

time: 57.5 us -> 56.9 us (0.990)
  Pallas kernels: 21.2 us -> 20.5 us
    pallas_call x1, Pallas kernels: 14.3 us -> 13.6 us  [advance(): pl.pallas_call(functools.partial(advance_kernel, unroll=UNROLL), in_specs...]
where the time goes in v5:
time: 56.9 us; the launch traced here: 56.7 us
  Pallas kernels  20.5 us (36%)
  waiting for transfers between devices  18.1 us (32%)
  starting transfers between devices  16.5 us (29%)
  other arithmetic  0.77 us (1%)
  between operations  0.76 us (1%)
    pallas_call x1, Pallas kernels, advance(): pl.pallas_call(functools.partial(advance_kernel, unroll=UNROLL), in_specs...  13.6 us
    ppermute x3, starting transfers between devices, exchange(): return lax.ppermute(value, ('wave', 'grp'), pairs)  11 us
    ppermute x3, waiting for transfers between devices, exchange(): return lax.ppermute(value, ('wave', 'grp'), pairs)  10.8 us
    ppermute x4, waiting for transfers between devices, swap(): return lax.ppermute(value, axis, [(i, i ^ bit) for i in range(count)])  7.32 us
    ppermute x4, starting transfers between devices, swap(): return lax.ppermute(value, axis, [(i, i ^ bit) for i in range(count)])  4.87 us
    pallas_call x1, Pallas kernels, prepare(): pl.pallas_call(prepare_kernel, in_specs=[VMEM] + [ANY] * 11, out_specs=[V...  3.25 us
    pallas_call x1, Pallas kernels, pick_halo(): pl.pallas_call(pick_kernel, in_specs=[ANY, ANY], out_specs=[VMEM] * 3, ou...  2.43 us
    pallas_call x1, Pallas kernels, regrid(): pl.pallas_call(functools.partial(regrid_kernel, block_rows=block_rows), i...  1.22 us
  transfers between devices with their start and end apart: 8, of which 6 were waited for; matrix products, arithmetic and copies ran while one was open for 0% of the time, Pallas kernels for 6%

profile of v5, /device:TPU:0, one launch (start us, length us, event | category | flops | bytes accessed | tf_op | source)
XLA Modules:
  0.0 56.7 jit_solution(11964550589369142877)
XLA Ops:
  0.6 2.4 %shard_map.149 = (f32[288,2048]{1,0:T(8,128)S(1)}, f32[288,128]{1,0:T(8,128)S(1)}, f32[288,128]{1,0:T(8,128)S(1)}) custom-call(s32[2,1,128]{2,1,0:T(1,128)} %lists_hbm.1, f32[288,2048]{1,0:T(8,128)} %spec_hbm.1), custom_call_target="tpu_custom_call" | custom-call | tf_op jit(solution)/shard_map/pallas_call | solution.py:113
  3.1 3.0 %collective-permute-start = (f32[288,128]{1,0:T(8,128)S(1)}, f32[288,128]{1,0:T(8,128)S(1)}, u32[]{:S(2)}, u32[]{:S(2)}) collective-permute-start(f32[288,128]{1,0:T(8,128)S(1)} %get-tuple-element.23), channel_id=1, source_target_pairs={{0,4},{4,0},{8,12},{12,8},{16,20},{20,16},{24,28},{28,24},{1,5},{5... | collective-permute-start | bytes 442376 | tf_op jit(solution)/shard_map/ppermute | solution.py:397
  6.1 0.7 %collective-permute-start.1 = (f32[288,128]{1,0:T(8,128)S(1)}, f32[288,128]{1,0:T(8,128)S(1)}, u32[]{:S(2)}, u32[]{:S(2)}) collective-permute-start(f32[288,128]{1,0:T(8,128)S(1)} %get-tuple-element.24), channel_id=1, source_target_pairs={{4,8},{8,4},{12,16},{16,12},{20,24},{24,20},{5,9},{9,5},{13,17},{1... | collective-permute-start | bytes 442376 | tf_op jit(solution)/shard_map/ppermute | solution.py:437
  6.7 3.3 %shard_map.150 = (f32[9216,128]{1,0:T(8,128)S(1)}, f32[8,2056,128]{2,1,0:T(8,128)S(1)}, f32[288,2048]{1,0:T(8,128)S(1)}, s32[16,8,128]{2,1,0:T(8,128)S(4)}, f32[...) custom-call(f32[288,2048]{1,0:T(8,128)S(1)} %get-tuple-element.16.re, ...), custom_call_target="tpu_custom_call" | custom-call | tf_op jit(solution)/shard_map/pallas_call | solution.py:213
  10.0 0.0 collective-permute-done.first_ref
  10.0 0.0 collective-permute-done.1.second_ref
  10.0 0.0 copy-start
  10.0 13.6 %shard_map.151 = (f32[288,2048]{1,0:T(8,128)}, f32[40,1024]{1,0:T(8,128)S(1)}, f32[40,1024]{1,0:T(8,128)S(1)}, f32[9216,128]{1,0:T(8,128)S(1)}) custom-call(s32[16,8,128]{2,1,0:T(8,128)S(4)} %get-tuple-element.17.index_ref, f32[9216,128]{1,0:T(8,128)S(1)} %get-tuple-element.18.table_in, ...), custom_call_target="tpu_custom_call", output_to_operand_aliasing={{3}: (1, {})} | custom-call | tf_op jit(solution)/shard_map/pallas_call | solution.py:349
  23.7 0.1 collective-permute-start.2
  23.7 1.4 %collective-permute-done.2 = f32[40,1024]{1,0:T(8,128)S(1)} collective-permute-done((f32[40,1024]{1,0:T(8,128)S(1)}, f32[40,1024]{1,0:T(8,128)S(1)}, u32[]{:S(2)}, u32[]{:S(2)}) %collective-permute-start.2) | collective-permute-done | bytes 163872 | tf_op jit(solution)/shard_map/ppermute | solution.py:397
  25.1 1.7 %collective-permute-start.3 = (f32[40,1024]{1,0:T(8,128)S(1)}, f32[40,1024]{1,0:T(8,128)S(1)}, u32[]{:S(2)}, u32[]{:S(2)}) collective-permute-start(f32[40,1024]{1,0:T(8,128)S(1)} %add.48), channel_id=1, source_target_pairs={{0,2},{1,3},{2,0},{3,1},{4,6},{5,7},{6,4},{7,5},{8,10},{9,11},{10,... | collective-permute-start | bytes 491528 | tf_op jit(solution)/shard_map/ppermute | solution.py:397
  26.9 4.6 %collective-permute-done.3 = f32[40,1024]{1,0:T(8,128)S(1)} collective-permute-done((f32[40,1024]{1,0:T(8,128)S(1)}, f32[40,1024]{1,0:T(8,128)S(1)}, u32[]{:S(2)}, u32[]{:S(2)}) %collective-permute-start.3) | collective-permute-done | bytes 163872 | tf_op jit(solution)/shard_map/ppermute | solution.py:397
  31.5 0.1 collective-permute-start.4
  31.6 0.0 copy-done
  31.6 1.3 %collective-permute-done.4.other_ref = f32[40,1024]{1,0:T(8,128)S(1)} collective-permute-done((f32[40,1024]{1,0:T(8,128)S(1)}, f32[40,1024]{1,0:T(8,128)S(1)}, u32[]{:S(2)}, u32[]{:S(2)}) %collective-permute-start.4) | collective-permute-done | bytes 163872 | tf_op jit(solution)/shard_map/ppermute | solution.py:397
  32.9 1.2 %shard_map.152 = f32[32,40,128]{2,1,0:T(8,128)S(1)} custom-call(s32[32]{0:T(128)S(1)} %fusion.1.slot_ref, f32[40,1024]{1,0:T(8,128)S(1)} %add.49.mine_ref, f32[40,1024]{1,0:T(8,128)S(1)} %collective-permute-done.4.other_ref, bf16[2048,128]{1,0:T(8,128)(2,1)S(1)} %get-tuple-element.28.high_ref, bf16[2048,128]{1,0:T(8,128)(2,1)S(1)} %get-tuple-element.29.low_ref), custom_call_target="tpu_custom_call" | custom-call | tf_op jit(solution)/shard_map/pallas_call | solution.py:386
  34.2 4.9 %collective-permute-start.5 = (f32[4,4,40,128]{3,2,1,0:T(8,128)S(1)}, f32[4,4,40,128]{3,2,1,0:T(8,128)S(1)}, u32[]{:S(2)}, u32[]{:S(2)}) collective-permute-start(f32[4,4,40,128]{3,2,1,0:T(8,128)S(1)} %bitcast.11), channel_id=1, source_target_pairs={{0,4},{1,9},{2,6},{3,11},{4,0},{5,13},{6,2},{7,15},{8,12},{9,1},{1... | collective-permute-start | bytes 983048 | tf_op jit(solution)/shard_map/ppermute | solution.py:423
  39.1 5.1 %collective-permute-done.5 = f32[4,4,40,128]{3,2,1,0:T(8,128)S(1)} collective-permute-done((f32[4,4,40,128]{3,2,1,0:T(8,128)S(1)}, f32[4,4,40,128]{3,2,1,0:T(8,128)S(1)}, u32[]{:S(2)}, u32[]{:S(2)}) %collective-permute-start.5) | collective-permute-done | bytes 327712 | tf_op jit(solution)/shard_map/ppermute | solution.py:423
  44.2 3.0 %collective-permute-start.6 = (f32[2,4,40,128]{3,2,1,0:T(8,128)S(1)}, f32[2,4,40,128]{3,2,1,0:T(8,128)S(1)}, u32[]{:S(2)}, u32[]{:S(2)}) collective-permute-start(f32[2,4,40,128]{3,2,1,0:T(8,128)S(1)} %slice.35), channel_id=1, source_target_pairs={{0,8},{1,5},{2,10},{3,7},{4,12},{5,1},{6,14},{7,3},{8,0},{9,13},{1... | collective-permute-start | bytes 491528 | tf_op jit(solution)/shard_map/ppermute | solution.py:423
  47.2 3.3 %collective-permute-done.6 = f32[2,4,40,128]{3,2,1,0:T(8,128)S(1)} collective-permute-done((f32[2,4,40,128]{3,2,1,0:T(8,128)S(1)}, f32[2,4,40,128]{3,2,1,0:T(8,128)S(1)}, u32[]{:S(2)}, u32[]{:S(2)}) %collective-permute-start.6) | collective-permute-done | bytes 163872 | tf_op jit(solution)/shard_map/ppermute | solution.py:423
  50.6 3.1 %collective-permute-start.7 = (f32[1,4,40,128]{3,2,1,0:T(8,128)S(1)}, f32[1,4,40,128]{3,2,1,0:T(8,128)S(1)}, u32[]{:S(2)}, u32[]{:S(2)}) collective-permute-start(f32[1,4,40,128]{3,2,1,0:T(8,128)S(1)} %slice.37), channel_id=1, source_target_pairs={{0,16},{1,17},{2,18},{3,19},{4,20},{5,21},{6,22},{7,23},{8,24},{9,... | collective-permute-start | bytes 245768 | tf_op jit(solution)/shard_map/ppermute | solution.py:423
  53.6 2.4 %collective-permute-done.7 = f32[1,4,40,128]{3,2,1,0:T(8,128)S(1)} collective-permute-done((f32[1,4,40,128]{3,2,1,0:T(8,128)S(1)}, f32[1,4,40,128]{3,2,1,0:T(8,128)S(1)}, u32[]{:S(2)}, u32[]{:S(2)}) %collective-permute-start.7) | collective-permute-done | bytes 81952 | tf_op jit(solution)/shard_map/ppermute | solution.py:423
  56.0 0.6 %fusion = f32[4,40,128]{2,1,0:T(8,128)} fusion(f32[1,4,40,128]{3,2,1,0:T(8,128)S(1)} %collective-permute-done.7, f32[2,4,40,128]{3,2,1,0:T(8,128)S(1)} %slice_add_fusion), kind=kLoop, calls=%fused_computation.2 | loop fusion | flops 20480 | bytes 245760 | tf_op jit(solution)/shard_map/squeeze | solution.py:430
  (8 shorter events, 0.2 us)
Async XLA Ops:
  3.1 6.9 %collective-permute-start = (f32[288,128]{1,0:T(8,128)S(1)}, f32[288,128]{1,0:T(8,128)S(1)}, u32[]{:S(2)}, u32[]{:S(2)}) collective-permute-start(f32[288,128]{1,0:T(8,128)S(1)} %get-tuple-element.23), channel_id=1, source_target_pairs={{0,4},{4,0},{8,12},{12,8},{16,20},{20,16},{24,28},{28,24},{1,5},{5... | collective-permute-start | bytes 442376 | tf_op jit(solution)/shard_map/ppermute | solution.py:397
  6.1 3.9 %collective-permute-start.1 = (f32[288,128]{1,0:T(8,128)S(1)}, f32[288,128]{1,0:T(8,128)S(1)}, u32[]{:S(2)}, u32[]{:S(2)}) collective-permute-start(f32[288,128]{1,0:T(8,128)S(1)} %get-tuple-element.24), channel_id=1, source_target_pairs={{4,8},{8,4},{12,16},{16,12},{20,24},{24,20},{5,9},{9,5},{13,17},{1... | collective-permute-start | bytes 442376 | tf_op jit(solution)/shard_map/ppermute | solution.py:437
  10.0 21.5 %copy-start = (s32[32]{0:T(128)S(1)}, s32[32]{0:T(128)}, u32[]{:S(2)}) copy-start(s32[32]{0:T(128)} %param.24) | copy-start | bytes 388
  23.7 1.5 %collective-permute-start.2 = (f32[40,1024]{1,0:T(8,128)S(1)}, f32[40,1024]{1,0:T(8,128)S(1)}, u32[]{:S(2)}, u32[]{:S(2)}) collective-permute-start(f32[40,1024]{1,0:T(8,128)S(1)} %get-tuple-element.27), channel_id=1, source_target_pairs={{0,1},{1,0},{2,3},{3,2},{4,5},{5,4},{6,7},{7,6},{8,9},{9,8},{10,11... | collective-permute-start | bytes 491528 | tf_op jit(solution)/shard_map/ppermute | solution.py:397
  25.1 6.3 %collective-permute-start.3 = (f32[40,1024]{1,0:T(8,128)S(1)}, f32[40,1024]{1,0:T(8,128)S(1)}, u32[]{:S(2)}, u32[]{:S(2)}) collective-permute-start(f32[40,1024]{1,0:T(8,128)S(1)} %add.48), channel_id=1, source_target_pairs={{0,2},{1,3},{2,0},{3,1},{4,6},{5,7},{6,4},{7,5},{8,10},{9,11},{10,... | collective-permute-start | bytes 491528 | tf_op jit(solution)/shard_map/ppermute | solution.py:397
  31.5 1.5 %collective-permute-start.4 = (f32[40,1024]{1,0:T(8,128)S(1)}, f32[40,1024]{1,0:T(8,128)S(1)}, u32[]{:S(2)}, u32[]{:S(2)}) collective-permute-start(f32[40,1024]{1,0:T(8,128)S(1)} %add.49.mine_ref), channel_id=1, source_target_pairs={{0,1},{1,0},{2,3},{3,2},{4,5},{5,4},{6,7},{7,6},{8,9},{9,8},{10,11... | collective-permute-start | bytes 491528 | tf_op jit(solution)/shard_map/ppermute | solution.py:397
  34.2 9.9 %collective-permute-start.5 = (f32[4,4,40,128]{3,2,1,0:T(8,128)S(1)}, f32[4,4,40,128]{3,2,1,0:T(8,128)S(1)}, u32[]{:S(2)}, u32[]{:S(2)}) collective-permute-start(f32[4,4,40,128]{3,2,1,0:T(8,128)S(1)} %bitcast.11), channel_id=1, source_target_pairs={{0,4},{1,9},{2,6},{3,11},{4,0},{5,13},{6,2},{7,15},{8,12},{9,1},{1... | collective-permute-start | bytes 983048 | tf_op jit(solution)/shard_map/ppermute | solution.py:423
  44.2 6.3 %collective-permute-start.6 = (f32[2,4,40,128]{3,2,1,0:T(8,128)S(1)}, f32[2,4,40,128]{3,2,1,0:T(8,128)S(1)}, u32[]{:S(2)}, u32[]{:S(2)}) collective-permute-start(f32[2,4,40,128]{3,2,1,0:T(8,128)S(1)} %slice.35), channel_id=1, source_target_pairs={{0,8},{1,5},{2,10},{3,7},{4,12},{5,1},{6,14},{7,3},{8,0},{9,13},{1... | collective-permute-start | bytes 491528 | tf_op jit(solution)/shard_map/ppermute | solution.py:423
  50.6 5.5 %collective-permute-start.7 = (f32[1,4,40,128]{3,2,1,0:T(8,128)S(1)}, f32[1,4,40,128]{3,2,1,0:T(8,128)S(1)}, u32[]{:S(2)}, u32[]{:S(2)}) collective-permute-start(f32[1,4,40,128]{3,2,1,0:T(8,128)S(1)} %slice.37), channel_id=1, source_target_pairs={{0,16},{1,17},{2,18},{3,19},{4,20},{5,21},{6,22},{7,23},{8,24},{9,... | collective-permute-start | bytes 245768 | tf_op jit(solution)/shard_map/ppermute | solution.py:423

commit v6 on v5

--- a/solution.py
+++ b/solution.py
@@ -125,11 +125,21 @@
     )(*in_hbm(lists, spectrum))
 
 
-def prepare_kernel(*refs):
-    spec_ref, operands, blocks_hbm = refs[0], refs[1:11], refs[11]
-    table, inflow, gain, index_out, speed_rows, kernel_both, high_ref, low_ref = refs[12:20]
-    scratch, (index_ref, weights_ref, turn, sems, weights_sem, index_sem) = refs[20:29], refs[29:]
-    copies = start_all(operands, (*scratch, index_ref), sems)
+def places(relative, bits):
+    total = 0
+    for bit in bits:
+        total = 2 * total + jnp.where((relative & bit) != 0, 1, 0)
+    return total
+
+
+def prepare_kernel(*refs, orders):
+    spec_ref, operands, blocks_hbm, tile_hbm = refs[0], refs[1:11], refs[11], refs[12]
+    table, inflow, gain, index_out, speed_rows, kernel_both, high_ref, low_ref, slot_ref = refs[13:22]
+    scratch, (tile_ref, index_ref, weights_ref, turn, sems, weights_sem, index_sem) = (
+        refs[22:31],
+        refs[31:],
+    )
+    copies = start_all((*operands, tile_hbm), (*scratch, index_ref, tile_ref), sems)
     cells = high_ref.shape[1]
     mine = pl.ds(pl.multiple_of(lax.axis_index("grp") * cells, LANES), cells)
     weights_copy = pltpu.make_async_copy(blocks_hbm.at[:, :, mine], weights_ref, weights_sem)
@@ -154,6 +164,16 @@
     index_ref[...] = index_ref[...] * groups
     index_copy = pltpu.make_async_copy(index_ref, index_out, index_sem)
     index_copy.start()
+    wave = lax.axis_index("wave")
+    odd = lax.axis_index("grp") % 2 == 1
+
+    @pl.loop(0, tile_ref.shape[0])
+    def _(block):
+        tile = tile_ref[block]
+        relative = lax.div(tile, TPW) ^ wave
+        place = jnp.where(odd, places(relative, orders[1]), places(relative, orders[0]))
+        slot_ref[block] = place * TPW + lax.rem(tile, TPW)
+
     kernel_high, kernel_low = split2(kernel_ref[...])
     kernel_both[...] = jnp.concatenate([kernel_high, kernel_low], 0)
     lower = lax.broadcasted_iota(jnp.int32, (PAIR, LANES), 0) < ND
@@ -201,7 +221,9 @@
     index_copy.wait()
 
 
-def prepare(spectrum, coef, loss, speed, edges, wind, friction, kernel, index, blocks, rows):
+def prepare(
+    spectrum, coef, loss, speed, edges, wind, friction, kernel, index, blocks, tiles, rows, orders
+):
     bins, points = spectrum.shape
     slots = edges.shape[0] // 2
     weight, facing = direction_constants(slots)
@@ -211,9 +233,9 @@
     count, block_rows, tile_cells = blocks.shape
     cells = tile_cells // lax.axis_size("grp")
     return pl.pallas_call(
-        prepare_kernel,
-        in_specs=[VMEM] + [ANY] * 11,
-        out_specs=[VMEM] * 3 + [SMEM] + [VMEM] * 4,
+        functools.partial(prepare_kernel, orders=orders),
+        in_specs=[VMEM] + [ANY] * 12,
+        out_specs=[VMEM] * 3 + [SMEM] + [VMEM] * 4 + [SMEM],
         out_shape=[
             vmem((rows, LANES)),
             vmem((slots, points + 8, LANES)),
@@ -223,19 +245,21 @@
             vmem((2 * kernel.shape[0], bins), BF),
             vmem((count * block_rows, cells), BF),
             vmem((count * block_rows, cells), BF),
+            pltpu.SMEM(tiles.shape, jnp.int32),
         ],
         scratch_shapes=[
             *[pltpu.SMEM(operand.shape, F32) for operand in (coef, loss, speed)],
             *[pltpu.VMEM(operand.shape, operand.dtype) for operand in operands],
+            pltpu.SMEM(tiles.shape, jnp.int32),
             pltpu.VMEM(index.shape, jnp.int32),
             pltpu.VMEM((count, block_rows, cells), F32),
             pltpu.VMEM((2, *shape), F32),
-            pltpu.SemaphoreType.DMA((10,)),
+            pltpu.SemaphoreType.DMA((11,)),
             pltpu.SemaphoreType.DMA(()),
             pltpu.SemaphoreType.DMA(()),
         ],
         compiler_params=params(8),
-    )(spectrum, *in_hbm(coef, loss, speed, *operands, index, blocks))
+    )(spectrum, *in_hbm(coef, loss, speed, *operands, index, blocks, tiles))
 
 
 def advance_kernel(
@@ -361,35 +385,41 @@
     )(index, table, inflow, spectrum, gain, speed_rows, kernel_both, first, second)
 
 
-def regrid_kernel(slot_ref, mine_ref, other_ref, high_ref, low_ref, out_ref, *, block_rows):
-    depth, points = mine_ref.shape
+def regrid_kernel(slot_ref, high_ref, low_ref, stokes_ref, *refs, block_rows, own):
+    out_ref = refs[-1]
+    depth, points = stokes_ref.shape
     pairs = points // LANES
     odd = lax.axis_index("grp") % 2
-    out_ref[...] = jnp.zeros(out_ref.shape, F32)
+    half = odd if own else 1 - odd
+    if own:
+        out_ref[...] = jnp.zeros(out_ref.shape, F32)
     lower = lax.broadcasted_iota(jnp.int32, (depth, LANES), 1) < block_rows
-    for ref, half in ((mine_ref, odd), (other_ref, 1 - odd)):
-        for pair in range(pairs):
-            part = ref[:, pair * LANES : (pair + 1) * LANES]
-            both = jnp.concatenate([jnp.where(lower, part, 0.0), jnp.where(lower, 0.0, part)], 0)
-            high, low = split2(both)
-            place = half * pairs + pair
-            rows = pl.ds(pl.multiple_of(place * LANES, LANES), LANES)
-            terms = (
-                dot(high, high_ref[rows, :]) + dot(low, high_ref[rows, :]) + dot(high, low_ref[rows, :])
-            )
-            for side in range(2):
-                slot = slot_ref[2 * place + side]
-                out_ref[slot] = out_ref[slot] + terms[side * depth : (side + 1) * depth]
+    for pair in range(pairs):
+        part = stokes_ref[:, pair * LANES : (pair + 1) * LANES]
+        both = jnp.concatenate([jnp.where(lower, part, 0.0), jnp.where(lower, 0.0, part)], 0)
+        high, low = split2(both)
+        place = half * pairs + pair
+        rows = pl.ds(pl.multiple_of(place * LANES, LANES), LANES)
+        terms = dot(high, high_ref[rows, :]) + dot(low, high_ref[rows, :]) + dot(high, low_ref[rows, :])
+        for side in range(2):
+            slot = slot_ref[2 * place + side]
+            out_ref[slot] = out_ref[slot] + terms[side * depth : (side + 1) * depth]
 
 
 def regrid(slots, mine, other, high, low, count, block_rows):
-    return pl.pallas_call(
-        functools.partial(regrid_kernel, block_rows=block_rows),
-        in_specs=[SMEM] + [VMEM] * 4,
-        out_specs=VMEM,
-        out_shape=jax.ShapeDtypeStruct((count, mine.shape[0], LANES), F32),
-        compiler_params=params(4),
-    )(slots, mine, other, high, low)
+    total = []
+    for stokes in (mine, other):
+        total = [
+            pl.pallas_call(
+                functools.partial(regrid_kernel, block_rows=block_rows, own=not total),
+                in_specs=[SMEM] + [VMEM] * (3 + len(total)),
+                out_specs=VMEM,
+                out_shape=jax.ShapeDtypeStruct((count, mine.shape[0], LANES), F32),
+                input_output_aliases={4: 0} if total else {},
+                compiler_params=params(4),
+            )(slots, high, low, stokes, *total)
+        ]
+    return total[0]
 
 
 def swap(value, axis, bit):
@@ -404,13 +434,6 @@
         mine = mine + swap(mine, axis, bit)
         bit *= 2
     return mine, swap(mine, axis, 1)
-
-
-def places(relative, bits):
-    total = jnp.zeros_like(relative)
-    for bit in bits:
-        total = 2 * total + jnp.where((relative & bit) != 0, 1, 0)
-    return total
 
 
 def exchange(value, even_bit, odd_bit):
@@ -456,11 +479,13 @@
     groups = bins // PAIR
     slots = neighbours.shape[0]
     rows = (points + 2 * halo_lists.shape[-1]) * groups
+    bits = [1 << b for b in range(n_wave.bit_length() - 1)]
+    other_bits = bits[1::-1] + bits[2:]
     spectrum, first, second = pick_halo(spectrum, halo_lists)
     first, second = swap_halo(first, second)
     index = neighbours.reshape(slots, points // LANES, LANES).transpose(1, 0, 2)
     edges = edge_vectors.reshape(2 * slots, points)
-    table, inflow, gain, index, speed_rows, kernel_both, high, low = prepare(
+    table, inflow, gain, index, speed_rows, kernel_both, high, low, slot = prepare(
         spectrum,
         input_coef,
         dissipation,
@@ -471,20 +496,16 @@
         drift_kernel,
         index,
         block_weights,
+        block_tile,
         rows,
+        (bits, other_bits),
     )
     updated, keep, send, _ = advance(
         index, table, inflow, spectrum, gain, speed_rows, kernel_both, first, second
     )
     mine, other = sum_over(keep, send, "grp")
-    relative = (block_tile // TPW) ^ lax.axis_index("wave")
-    tile = block_tile % TPW
-    bits = [1 << b for b in range(n_wave.bit_length() - 1)]
-    other_bits = bits[1::-1] + bits[2:]
-    odd = lax.axis_index("grp") % 2 == 1
-    place = jnp.where(odd, places(relative, other_bits), places(relative, bits))
     block_rows = block_weights.shape[1]
-    parts = regrid(place * TPW + tile, mine, other, high, low, n_wave * TPW, block_rows)
+    parts = regrid(slot, mine, other, high, low, n_wave * TPW, block_rows)
     parts = parts.reshape(n_wave, TPW, *parts.shape[1:])
     drift = scatter_sum(parts, bits, other_bits)
     return updated, drift

time: 56.9 us -> 56.1 us (0.986)
  starting transfers between devices: 16.5 us -> 15.9 us
    pallas_call x2 -> x3, Pallas kernels: 4.47 us -> 4.56 us  [the longest x1 3.72 us: prepare(): pl.pallas_call(functools.partial(prepare_kernel, orders=orders), in_specs...]
  transfers between devices with their start and end apart: 8 -> 8, of which waited for: 6 -> 6; matrix products, arithmetic and copies ran while one was open for 0% -> 0% of each run, Pallas kernels for 6% -> 7%
where the time goes in v6:
time: 56.1 us; the launch traced here: 55.9 us
  Pallas kernels  20.6 us (37%)
  waiting for transfers between devices  17.8 us (32%)
  starting transfers between devices  15.9 us (28%)
  between operations  0.75 us (1%)
  other arithmetic  0.74 us (1%)
    pallas_call x1, Pallas kernels, advance(): pl.pallas_call(functools.partial(advance_kernel, unroll=UNROLL), in_specs...  13.6 us
    ppermute x3, waiting for transfers between devices, exchange(): return lax.ppermute(value, ('wave', 'grp'), pairs)  10.8 us
    ppermute x3, starting transfers between devices, exchange(): return lax.ppermute(value, ('wave', 'grp'), pairs)  10.5 us
    ppermute x4, waiting for transfers between devices, swap(): return lax.ppermute(value, axis, [(i, i ^ bit) for i in range(count)])  7.07 us
    ppermute x4, starting transfers between devices, swap(): return lax.ppermute(value, axis, [(i, i ^ bit) for i in range(count)])  4.72 us
    pallas_call x1, Pallas kernels, prepare(): pl.pallas_call(functools.partial(prepare_kernel, orders=orders), in_specs...  3.72 us
    pallas_call x1, Pallas kernels, pick_halo(): pl.pallas_call(pick_kernel, in_specs=[ANY, ANY], out_specs=[VMEM] * 3, ou...  2.43 us
  transfers between devices with their start and end apart: 8, of which 6 were waited for; matrix products, arithmetic and copies ran while one was open for 0% of the time, Pallas kernels for 7%

profile of v6, /device:TPU:0, one launch (start us, length us, event | category | flops | bytes accessed | tf_op | source)
XLA Modules:
  0.0 55.9 jit_solution(9932386480760694396)
XLA Ops:
  0.6 2.4 %shard_map.149 = (f32[288,2048]{1,0:T(8,128)S(1)}, f32[288,128]{1,0:T(8,128)S(1)}, f32[288,128]{1,0:T(8,128)S(1)}) custom-call(s32[2,1,128]{2,1,0:T(1,128)} %lists_hbm.1, f32[288,2048]{1,0:T(8,128)} %spec_hbm.1), custom_call_target="tpu_custom_call" | custom-call | tf_op jit(solution)/shard_map/pallas_call | solution.py:113
  3.1 3.0 %collective-permute-start = (f32[288,128]{1,0:T(8,128)S(1)}, f32[288,128]{1,0:T(8,128)S(1)}, u32[]{:S(2)}, u32[]{:S(2)}) collective-permute-start(f32[288,128]{1,0:T(8,128)S(1)} %get-tuple-element.24), channel_id=1, source_target_pairs={{0,4},{4,0},{8,12},{12,8},{16,20},{20,16},{24,28},{28,24},{1,5},{5... | collective-permute-start | bytes 442376 | tf_op jit(solution)/shard_map/ppermute | solution.py:427
  6.1 0.7 %collective-permute-start.1 = (f32[288,128]{1,0:T(8,128)S(1)}, f32[288,128]{1,0:T(8,128)S(1)}, u32[]{:S(2)}, u32[]{:S(2)}) collective-permute-start(f32[288,128]{1,0:T(8,128)S(1)} %get-tuple-element.25), channel_id=1, source_target_pairs={{4,8},{8,4},{12,16},{16,12},{20,24},{24,20},{5,9},{9,5},{13,17},{1... | collective-permute-start | bytes 442376 | tf_op jit(solution)/shard_map/ppermute | solution.py:460
  6.7 3.7 %shard_map.150 = (f32[9216,128]{1,0:T(8,128)S(1)}, f32[8,2056,128]{2,1,0:T(8,128)S(1)}, f32[288,2048]{1,0:T(8,128)S(1)}, s32[16,8,128]{2,1,0:T(8,128)S(4)}, f32[...) custom-call(f32[288,2048]{1,0:T(8,128)S(1)} %get-tuple-element.17.re, ...), custom_call_target="tpu_custom_call" | custom-call | tf_op jit(solution)/shard_map/pallas_call | solution.py:235
  10.5 0.0 collective-permute-done.first_ref
  10.5 0.0 collective-permute-done.1.second_ref
  10.5 13.6 %shard_map.151 = (f32[288,2048]{1,0:T(8,128)}, f32[40,1024]{1,0:T(8,128)S(1)}, f32[40,1024]{1,0:T(8,128)S(1)}, f32[9216,128]{1,0:T(8,128)S(1)}) custom-call(s32[16,8,128]{2,1,0:T(8,128)S(4)} %get-tuple-element.18.index_ref, f32[9216,128]{1,0:T(8,128)S(1)} %get-tuple-element.19.table_in, ...), custom_call_target="tpu_custom_call", output_to_operand_aliasing={{3}: (1, {})} | custom-call | tf_op jit(solution)/shard_map/pallas_call | solution.py:373
  24.1 0.1 collective-permute-start.2
  24.2 1.4 %collective-permute-done.2 = f32[40,1024]{1,0:T(8,128)S(1)} collective-permute-done((f32[40,1024]{1,0:T(8,128)S(1)}, f32[40,1024]{1,0:T(8,128)S(1)}, u32[]{:S(2)}, u32[]{:S(2)}) %collective-permute-start.2) | collective-permute-done | bytes 163872 | tf_op jit(solution)/shard_map/ppermute | solution.py:427
  25.6 1.6 %collective-permute-start.3 = (f32[40,1024]{1,0:T(8,128)S(1)}, f32[40,1024]{1,0:T(8,128)S(1)}, u32[]{:S(2)}, u32[]{:S(2)}) collective-permute-start(f32[40,1024]{1,0:T(8,128)S(1)} %add.15), channel_id=1, source_target_pairs={{0,2},{1,3},{2,0},{3,1},{4,6},{5,7},{6,4},{7,5},{8,10},{9,11},{10,... | collective-permute-start | bytes 491528 | tf_op jit(solution)/shard_map/ppermute | solution.py:427
  27.2 4.7 %collective-permute-done.3 = f32[40,1024]{1,0:T(8,128)S(1)} collective-permute-done((f32[40,1024]{1,0:T(8,128)S(1)}, f32[40,1024]{1,0:T(8,128)S(1)}, u32[]{:S(2)}, u32[]{:S(2)}) %collective-permute-start.3) | collective-permute-done | bytes 163872 | tf_op jit(solution)/shard_map/ppermute | solution.py:427
  32.0 0.1 collective-permute-start.4
  32.0 0.4 shard_map.152.refs_0_
  32.5 1.0 %collective-permute-done.4.stokes_ref = f32[40,1024]{1,0:T(8,128)S(1)} collective-permute-done((f32[40,1024]{1,0:T(8,128)S(1)}, f32[40,1024]{1,0:T(8,128)S(1)}, u32[]{:S(2)}, u32[]{:S(2)}) %collective-permute-start.4) | collective-permute-done | bytes 163872 | tf_op jit(solution)/shard_map/ppermute | solution.py:427
  33.4 0.4 shard_map.153
  33.9 4.4 %collective-permute-start.5 = (f32[4,4,40,128]{3,2,1,0:T(8,128)S(1)}, f32[4,4,40,128]{3,2,1,0:T(8,128)S(1)}, u32[]{:S(2)}, u32[]{:S(2)}) collective-permute-start(f32[4,4,40,128]{3,2,1,0:T(8,128)S(1)} %bitcast.11), channel_id=1, source_target_pairs={{0,4},{1,9},{2,6},{3,11},{4,0},{5,13},{6,2},{7,15},{8,12},{9,1},{1... | collective-permute-start | bytes 983048 | tf_op jit(solution)/shard_map/ppermute | solution.py:446
  38.3 5.1 %collective-permute-done.5 = f32[4,4,40,128]{3,2,1,0:T(8,128)S(1)} collective-permute-done((f32[4,4,40,128]{3,2,1,0:T(8,128)S(1)}, f32[4,4,40,128]{3,2,1,0:T(8,128)S(1)}, u32[]{:S(2)}, u32[]{:S(2)}) %collective-permute-start.5) | collective-permute-done | bytes 327712 | tf_op jit(solution)/shard_map/ppermute | solution.py:446
  43.4 3.0 %collective-permute-start.6 = (f32[2,4,40,128]{3,2,1,0:T(8,128)S(1)}, f32[2,4,40,128]{3,2,1,0:T(8,128)S(1)}, u32[]{:S(2)}, u32[]{:S(2)}) collective-permute-start(f32[2,4,40,128]{3,2,1,0:T(8,128)S(1)} %slice.35), channel_id=1, source_target_pairs={{0,8},{1,5},{2,10},{3,7},{4,12},{5,1},{6,14},{7,3},{8,0},{9,13},{1... | collective-permute-start | bytes 491528 | tf_op jit(solution)/shard_map/ppermute | solution.py:446
  46.5 3.3 %collective-permute-done.6 = f32[2,4,40,128]{3,2,1,0:T(8,128)S(1)} collective-permute-done((f32[2,4,40,128]{3,2,1,0:T(8,128)S(1)}, f32[2,4,40,128]{3,2,1,0:T(8,128)S(1)}, u32[]{:S(2)}, u32[]{:S(2)}) %collective-permute-start.6) | collective-permute-done | bytes 163872 | tf_op jit(solution)/shard_map/ppermute | solution.py:446
  49.8 3.0 %collective-permute-start.7 = (f32[1,4,40,128]{3,2,1,0:T(8,128)S(1)}, f32[1,4,40,128]{3,2,1,0:T(8,128)S(1)}, u32[]{:S(2)}, u32[]{:S(2)}) collective-permute-start(f32[1,4,40,128]{3,2,1,0:T(8,128)S(1)} %slice.37), channel_id=1, source_target_pairs={{0,16},{1,17},{2,18},{3,19},{4,20},{5,21},{6,22},{7,23},{8,24},{9,... | collective-permute-start | bytes 245768 | tf_op jit(solution)/shard_map/ppermute | solution.py:446
  52.8 2.4 %collective-permute-done.7 = f32[1,4,40,128]{3,2,1,0:T(8,128)S(1)} collective-permute-done((f32[1,4,40,128]{3,2,1,0:T(8,128)S(1)}, f32[1,4,40,128]{3,2,1,0:T(8,128)S(1)}, u32[]{:S(2)}, u32[]{:S(2)}) %collective-permute-start.7) | collective-permute-done | bytes 81952 | tf_op jit(solution)/shard_map/ppermute | solution.py:446
  55.3 0.6 %fusion = f32[4,40,128]{2,1,0:T(8,128)} fusion(f32[1,4,40,128]{3,2,1,0:T(8,128)S(1)} %collective-permute-done.7, f32[2,4,40,128]{3,2,1,0:T(8,128)S(1)} %slice_add_fusion), kind=kLoop, calls=%fused_computation.2 | loop fusion | flops 20480 | bytes 245760 | tf_op jit(solution)/shard_map/squeeze | solution.py:453
  (7 shorter events, 0.2 us)
Async XLA Ops:
  3.1 7.4 %collective-permute-start = (f32[288,128]{1,0:T(8,128)S(1)}, f32[288,128]{1,0:T(8,128)S(1)}, u32[]{:S(2)}, u32[]{:S(2)}) collective-permute-start(f32[288,128]{1,0:T(8,128)S(1)} %get-tuple-element.24), channel_id=1, source_target_pairs={{0,4},{4,0},{8,12},{12,8},{16,20},{20,16},{24,28},{28,24},{1,5},{5... | collective-permute-start | bytes 442376 | tf_op jit(solution)/shard_map/ppermute | solution.py:427
  6.1 4.4 %collective-permute-start.1 = (f32[288,128]{1,0:T(8,128)S(1)}, f32[288,128]{1,0:T(8,128)S(1)}, u32[]{:S(2)}, u32[]{:S(2)}) collective-permute-start(f32[288,128]{1,0:T(8,128)S(1)} %get-tuple-element.25), channel_id=1, source_target_pairs={{4,8},{8,4},{12,16},{16,12},{20,24},{24,20},{5,9},{9,5},{13,17},{1... | collective-permute-start | bytes 442376 | tf_op jit(solution)/shard_map/ppermute | solution.py:460
  24.1 1.5 %collective-permute-start.2 = (f32[40,1024]{1,0:T(8,128)S(1)}, f32[40,1024]{1,0:T(8,128)S(1)}, u32[]{:S(2)}, u32[]{:S(2)}) collective-permute-start(f32[40,1024]{1,0:T(8,128)S(1)} %get-tuple-element.31), channel_id=1, source_target_pairs={{0,1},{1,0},{2,3},{3,2},{4,5},{5,4},{6,7},{7,6},{8,9},{9,8},{10,11... | collective-permute-start | bytes 491528 | tf_op jit(solution)/shard_map/ppermute | solution.py:427
  25.6 6.3 %collective-permute-start.3 = (f32[40,1024]{1,0:T(8,128)S(1)}, f32[40,1024]{1,0:T(8,128)S(1)}, u32[]{:S(2)}, u32[]{:S(2)}) collective-permute-start(f32[40,1024]{1,0:T(8,128)S(1)} %add.15), channel_id=1, source_target_pairs={{0,2},{1,3},{2,0},{3,1},{4,6},{5,7},{6,4},{7,5},{8,10},{9,11},{10,... | collective-permute-start | bytes 491528 | tf_op jit(solution)/shard_map/ppermute | solution.py:427
  32.0 1.5 %collective-permute-start.4 = (f32[40,1024]{1,0:T(8,128)S(1)}, f32[40,1024]{1,0:T(8,128)S(1)}, u32[]{:S(2)}, u32[]{:S(2)}) collective-permute-start(f32[40,1024]{1,0:T(8,128)S(1)} %add.16.stokes_ref), channel_id=1, source_target_pairs={{0,1},{1,0},{2,3},{3,2},{4,5},{5,4},{6,7},{7,6},{8,9},{9,8},{10,11... | collective-permute-start | bytes 491528 | tf_op jit(solution)/shard_map/ppermute | solution.py:427
  33.9 9.5 %collective-permute-start.5 = (f32[4,4,40,128]{3,2,1,0:T(8,128)S(1)}, f32[4,4,40,128]{3,2,1,0:T(8,128)S(1)}, u32[]{:S(2)}, u32[]{:S(2)}) collective-permute-start(f32[4,4,40,128]{3,2,1,0:T(8,128)S(1)} %bitcast.11), channel_id=1, source_target_pairs={{0,4},{1,9},{2,6},{3,11},{4,0},{5,13},{6,2},{7,15},{8,12},{9,1},{1... | collective-permute-start | bytes 983048 | tf_op jit(solution)/shard_map/ppermute | solution.py:446
  43.4 6.3 %collective-permute-start.6 = (f32[2,4,40,128]{3,2,1,0:T(8,128)S(1)}, f32[2,4,40,128]{3,2,1,0:T(8,128)S(1)}, u32[]{:S(2)}, u32[]{:S(2)}) collective-permute-start(f32[2,4,40,128]{3,2,1,0:T(8,128)S(1)} %slice.35), channel_id=1, source_target_pairs={{0,8},{1,5},{2,10},{3,7},{4,12},{5,1},{6,14},{7,3},{8,0},{9,13},{1... | collective-permute-start | bytes 491528 | tf_op jit(solution)/shard_map/ppermute | solution.py:446
  49.8 5.5 %collective-permute-start.7 = (f32[1,4,40,128]{3,2,1,0:T(8,128)S(1)}, f32[1,4,40,128]{3,2,1,0:T(8,128)S(1)}, u32[]{:S(2)}, u32[]{:S(2)}) collective-permute-start(f32[1,4,40,128]{3,2,1,0:T(8,128)S(1)} %slice.37), channel_id=1, source_target_pairs={{0,16},{1,17},{2,18},{3,19},{4,20},{5,21},{6,22},{7,23},{8,24},{9,... | collective-permute-start | bytes 245768 | tf_op jit(solution)/shard_map/ppermute | solution.py:446

commit v7 on v6

--- a/solution.py
+++ b/solution.py
@@ -151,7 +151,7 @@
     slots = inflow.shape[0]
     filler = jnp.zeros((LANES - PAIR, LANES), F32)
 
-    @pl.loop(0, points // LANES, unroll=8)
+    @pl.loop(0, points // LANES, unroll=4)
     def _(block):
         columns = pl.ds(pl.multiple_of(block * LANES, LANES), LANES)
         for group in range(groups):
@@ -188,7 +188,7 @@
     turn[0] = jnp.cos(wind_ref[...])
     turn[1] = jnp.sin(wind_ref[...])
 
-    @pl.loop(0, points // LANES, unroll=8)
+    @pl.loop(0, points // LANES, unroll=4)
     def _(block):
         base = pl.multiple_of(block * LANES, LANES)
         columns = pl.ds(base, LANES)

time: 56.1 us -> 56.1 us (level)
  starting transfers between devices: 15.9 us -> 15.2 us
  Pallas kernels: 20.6 us -> 21.3 us
    pallas_call x1, Pallas kernels: 3.72 us -> 4.37 us  [prepare(): pl.pallas_call(functools.partial(prepare_kernel, orders=orders), in_specs...]
    ppermute x3, starting transfers between devices: 10.5 us -> 9.85 us  [exchange(): return lax.ppermute(value, ('wave', 'grp'), pairs)]
  transfers between devices with their start and end apart: 8 -> 8, of which waited for: 6 -> 6; matrix products, arithmetic and copies ran while one was open for 0% -> 0% of each run, Pallas kernels for 7% -> 9%
where the time goes in v7:
time: 56.1 us; the launch traced here: 55.9 us
  Pallas kernels  21.3 us (38%)
  waiting for transfers between devices  17.8 us (32%)
  starting transfers between devices  15.2 us (27%)
  between operations  0.75 us (1%)
  other arithmetic  0.74 us (1%)
    pallas_call x1, Pallas kernels, advance(): pl.pallas_call(functools.partial(advance_kernel, unroll=UNROLL), in_specs...  13.6 us
    ppermute x3, waiting for transfers between devices, exchange(): return lax.ppermute(value, ('wave', 'grp'), pairs)  10.8 us
    ppermute x3, starting transfers between devices, exchange(): return lax.ppermute(value, ('wave', 'grp'), pairs)  9.85 us
    ppermute x4, waiting for transfers between devices, swap(): return lax.ppermute(value, axis, [(i, i ^ bit) for i in range(count)])  7.06 us
    ppermute x4, starting transfers between devices, swap(): return lax.ppermute(value, axis, [(i, i ^ bit) for i in range(count)])  4.73 us
    pallas_call x1, Pallas kernels, prepare(): pl.pallas_call(functools.partial(prepare_kernel, orders=orders), in_specs...  4.37 us
    pallas_call x1, Pallas kernels, pick_halo(): pl.pallas_call(pick_kernel, in_specs=[ANY, ANY], out_specs=[VMEM] * 3, ou...  2.43 us
  transfers between devices with their start and end apart: 8, of which 6 were waited for; matrix products, arithmetic and copies ran while one was open for 0% of the time, Pallas kernels for 9%

profile of v7, /device:TPU:0, one launch (start us, length us, event | category | flops | bytes accessed | tf_op | source)
XLA Modules:
  0.0 55.9 jit_solution(8254682644956366266)
XLA Ops:
  0.6 2.4 %shard_map.149 = (f32[288,2048]{1,0:T(8,128)S(1)}, f32[288,128]{1,0:T(8,128)S(1)}, f32[288,128]{1,0:T(8,128)S(1)}) custom-call(s32[2,1,128]{2,1,0:T(1,128)} %lists_hbm.1, f32[288,2048]{1,0:T(8,128)} %spec_hbm.1), custom_call_target="tpu_custom_call" | custom-call | tf_op jit(solution)/shard_map/pallas_call | solution.py:113
  3.1 3.0 %collective-permute-start = (f32[288,128]{1,0:T(8,128)S(1)}, f32[288,128]{1,0:T(8,128)S(1)}, u32[]{:S(2)}, u32[]{:S(2)}) collective-permute-start(f32[288,128]{1,0:T(8,128)S(1)} %get-tuple-element.24), channel_id=1, source_target_pairs={{0,4},{4,0},{8,12},{12,8},{16,20},{20,16},{24,28},{28,24},{1,5},{5... | collective-permute-start | bytes 442376 | tf_op jit(solution)/shard_map/ppermute | solution.py:427
  6.1 0.7 %collective-permute-start.1 = (f32[288,128]{1,0:T(8,128)S(1)}, f32[288,128]{1,0:T(8,128)S(1)}, u32[]{:S(2)}, u32[]{:S(2)}) collective-permute-start(f32[288,128]{1,0:T(8,128)S(1)} %get-tuple-element.25), channel_id=1, source_target_pairs={{4,8},{8,4},{12,16},{16,12},{20,24},{24,20},{5,9},{9,5},{13,17},{1... | collective-permute-start | bytes 442376 | tf_op jit(solution)/shard_map/ppermute | solution.py:460
  6.7 4.4 %shard_map.150 = (f32[9216,128]{1,0:T(8,128)S(1)}, f32[8,2056,128]{2,1,0:T(8,128)S(1)}, f32[288,2048]{1,0:T(8,128)S(1)}, s32[16,8,128]{2,1,0:T(8,128)S(4)}, f32[...) custom-call(f32[288,2048]{1,0:T(8,128)S(1)} %get-tuple-element.17.re, ...), custom_call_target="tpu_custom_call" | custom-call | tf_op jit(solution)/shard_map/pallas_call | solution.py:235
  11.1 0.0 collective-permute-done.first_ref
  11.1 0.0 collective-permute-done.1.second_ref
  11.1 13.6 %shard_map.151 = (f32[288,2048]{1,0:T(8,128)}, f32[40,1024]{1,0:T(8,128)S(1)}, f32[40,1024]{1,0:T(8,128)S(1)}, f32[9216,128]{1,0:T(8,128)S(1)}) custom-call(s32[16,8,128]{2,1,0:T(8,128)S(4)} %get-tuple-element.18.index_ref, f32[9216,128]{1,0:T(8,128)S(1)} %get-tuple-element.19.table_in, ...), custom_call_target="tpu_custom_call", output_to_operand_aliasing={{3}: (1, {})} | custom-call | tf_op jit(solution)/shard_map/pallas_call | solution.py:373
  24.8 0.1 collective-permute-start.2
  24.9 1.4 %collective-permute-done.2 = f32[40,1024]{1,0:T(8,128)S(1)} collective-permute-done((f32[40,1024]{1,0:T(8,128)S(1)}, f32[40,1024]{1,0:T(8,128)S(1)}, u32[]{:S(2)}, u32[]{:S(2)}) %collective-permute-start.2) | collective-permute-done | bytes 163872 | tf_op jit(solution)/shard_map/ppermute | solution.py:427
  26.3 1.6 %collective-permute-start.3 = (f32[40,1024]{1,0:T(8,128)S(1)}, f32[40,1024]{1,0:T(8,128)S(1)}, u32[]{:S(2)}, u32[]{:S(2)}) collective-permute-start(f32[40,1024]{1,0:T(8,128)S(1)} %add.15), channel_id=1, source_target_pairs={{0,2},{1,3},{2,0},{3,1},{4,6},{5,7},{6,4},{7,5},{8,10},{9,11},{10,... | collective-permute-start | bytes 491528 | tf_op jit(solution)/shard_map/ppermute | solution.py:427
  27.8 4.7 %collective-permute-done.3 = f32[40,1024]{1,0:T(8,128)S(1)} collective-permute-done((f32[40,1024]{1,0:T(8,128)S(1)}, f32[40,1024]{1,0:T(8,128)S(1)}, u32[]{:S(2)}, u32[]{:S(2)}) %collective-permute-start.3) | collective-permute-done | bytes 163872 | tf_op jit(solution)/shard_map/ppermute | solution.py:427
  32.6 0.1 collective-permute-start.4
  32.7 0.4 shard_map.152.refs_0_
  33.1 0.9 %collective-permute-done.4.stokes_ref = f32[40,1024]{1,0:T(8,128)S(1)} collective-permute-done((f32[40,1024]{1,0:T(8,128)S(1)}, f32[40,1024]{1,0:T(8,128)S(1)}, u32[]{:S(2)}, u32[]{:S(2)}) %collective-permute-start.4) | collective-permute-done | bytes 163872 | tf_op jit(solution)/shard_map/ppermute | solution.py:427
  34.1 0.4 shard_map.153
  34.5 4.4 %collective-permute-start.5 = (f32[4,4,40,128]{3,2,1,0:T(8,128)S(1)}, f32[4,4,40,128]{3,2,1,0:T(8,128)S(1)}, u32[]{:S(2)}, u32[]{:S(2)}) collective-permute-start(f32[4,4,40,128]{3,2,1,0:T(8,128)S(1)} %bitcast.11), channel_id=1, source_target_pairs={{0,4},{1,9},{2,6},{3,11},{4,0},{5,13},{6,2},{7,15},{8,12},{9,1},{1... | collective-permute-start | bytes 983048 | tf_op jit(solution)/shard_map/ppermute | solution.py:446
  38.9 5.1 %collective-permute-done.5 = f32[4,4,40,128]{3,2,1,0:T(8,128)S(1)} collective-permute-done((f32[4,4,40,128]{3,2,1,0:T(8,128)S(1)}, f32[4,4,40,128]{3,2,1,0:T(8,128)S(1)}, u32[]{:S(2)}, u32[]{:S(2)}) %collective-permute-start.5) | collective-permute-done | bytes 327712 | tf_op jit(solution)/shard_map/ppermute | solution.py:446
  44.0 2.4 %collective-permute-start.6 = (f32[2,4,40,128]{3,2,1,0:T(8,128)S(1)}, f32[2,4,40,128]{3,2,1,0:T(8,128)S(1)}, u32[]{:S(2)}, u32[]{:S(2)}) collective-permute-start(f32[2,4,40,128]{3,2,1,0:T(8,128)S(1)} %slice.35), channel_id=1, source_target_pairs={{0,8},{1,5},{2,10},{3,7},{4,12},{5,1},{6,14},{7,3},{8,0},{9,13},{1... | collective-permute-start | bytes 491528 | tf_op jit(solution)/shard_map/ppermute | solution.py:446
  46.4 3.3 %collective-permute-done.6 = f32[2,4,40,128]{3,2,1,0:T(8,128)S(1)} collective-permute-done((f32[2,4,40,128]{3,2,1,0:T(8,128)S(1)}, f32[2,4,40,128]{3,2,1,0:T(8,128)S(1)}, u32[]{:S(2)}, u32[]{:S(2)}) %collective-permute-start.6) | collective-permute-done | bytes 163872 | tf_op jit(solution)/shard_map/ppermute | solution.py:446
  49.8 3.1 %collective-permute-start.7 = (f32[1,4,40,128]{3,2,1,0:T(8,128)S(1)}, f32[1,4,40,128]{3,2,1,0:T(8,128)S(1)}, u32[]{:S(2)}, u32[]{:S(2)}) collective-permute-start(f32[1,4,40,128]{3,2,1,0:T(8,128)S(1)} %slice.37), channel_id=1, source_target_pairs={{0,16},{1,17},{2,18},{3,19},{4,20},{5,21},{6,22},{7,23},{8,24},{9,... | collective-permute-start | bytes 245768 | tf_op jit(solution)/shard_map/ppermute | solution.py:446
  52.8 2.4 %collective-permute-done.7 = f32[1,4,40,128]{3,2,1,0:T(8,128)S(1)} collective-permute-done((f32[1,4,40,128]{3,2,1,0:T(8,128)S(1)}, f32[1,4,40,128]{3,2,1,0:T(8,128)S(1)}, u32[]{:S(2)}, u32[]{:S(2)}) %collective-permute-start.7) | collective-permute-done | bytes 81952 | tf_op jit(solution)/shard_map/ppermute | solution.py:446
  55.3 0.6 %fusion = f32[4,40,128]{2,1,0:T(8,128)} fusion(f32[1,4,40,128]{3,2,1,0:T(8,128)S(1)} %collective-permute-done.7, f32[2,4,40,128]{3,2,1,0:T(8,128)S(1)} %slice_add_fusion), kind=kLoop, calls=%fused_computation.2 | loop fusion | flops 20480 | bytes 245760 | tf_op jit(solution)/shard_map/squeeze | solution.py:453
  (7 shorter events, 0.2 us)
Async XLA Ops:
  3.1 8.0 %collective-permute-start = (f32[288,128]{1,0:T(8,128)S(1)}, f32[288,128]{1,0:T(8,128)S(1)}, u32[]{:S(2)}, u32[]{:S(2)}) collective-permute-start(f32[288,128]{1,0:T(8,128)S(1)} %get-tuple-element.24), channel_id=1, source_target_pairs={{0,4},{4,0},{8,12},{12,8},{16,20},{20,16},{24,28},{28,24},{1,5},{5... | collective-permute-start | bytes 442376 | tf_op jit(solution)/shard_map/ppermute | solution.py:427
  6.1 5.1 %collective-permute-start.1 = (f32[288,128]{1,0:T(8,128)S(1)}, f32[288,128]{1,0:T(8,128)S(1)}, u32[]{:S(2)}, u32[]{:S(2)}) collective-permute-start(f32[288,128]{1,0:T(8,128)S(1)} %get-tuple-element.25), channel_id=1, source_target_pairs={{4,8},{8,4},{12,16},{16,12},{20,24},{24,20},{5,9},{9,5},{13,17},{1... | collective-permute-start | bytes 442376 | tf_op jit(solution)/shard_map/ppermute | solution.py:460
  24.8 1.5 %collective-permute-start.2 = (f32[40,1024]{1,0:T(8,128)S(1)}, f32[40,1024]{1,0:T(8,128)S(1)}, u32[]{:S(2)}, u32[]{:S(2)}) collective-permute-start(f32[40,1024]{1,0:T(8,128)S(1)} %get-tuple-element.31), channel_id=1, source_target_pairs={{0,1},{1,0},{2,3},{3,2},{4,5},{5,4},{6,7},{7,6},{8,9},{9,8},{10,11... | collective-permute-start | bytes 491528 | tf_op jit(solution)/shard_map/ppermute | solution.py:427
  26.3 6.3 %collective-permute-start.3 = (f32[40,1024]{1,0:T(8,128)S(1)}, f32[40,1024]{1,0:T(8,128)S(1)}, u32[]{:S(2)}, u32[]{:S(2)}) collective-permute-start(f32[40,1024]{1,0:T(8,128)S(1)} %add.15), channel_id=1, source_target_pairs={{0,2},{1,3},{2,0},{3,1},{4,6},{5,7},{6,4},{7,5},{8,10},{9,11},{10,... | collective-permute-start | bytes 491528 | tf_op jit(solution)/shard_map/ppermute | solution.py:427
  32.6 1.5 %collective-permute-start.4 = (f32[40,1024]{1,0:T(8,128)S(1)}, f32[40,1024]{1,0:T(8,128)S(1)}, u32[]{:S(2)}, u32[]{:S(2)}) collective-permute-start(f32[40,1024]{1,0:T(8,128)S(1)} %add.16.stokes_ref), channel_id=1, source_target_pairs={{0,1},{1,0},{2,3},{3,2},{4,5},{5,4},{6,7},{7,6},{8,9},{9,8},{10,11... | collective-permute-start | bytes 491528 | tf_op jit(solution)/shard_map/ppermute | solution.py:427
  34.5 9.4 %collective-permute-start.5 = (f32[4,4,40,128]{3,2,1,0:T(8,128)S(1)}, f32[4,4,40,128]{3,2,1,0:T(8,128)S(1)}, u32[]{:S(2)}, u32[]{:S(2)}) collective-permute-start(f32[4,4,40,128]{3,2,1,0:T(8,128)S(1)} %bitcast.11), channel_id=1, source_target_pairs={{0,4},{1,9},{2,6},{3,11},{4,0},{5,13},{6,2},{7,15},{8,12},{9,1},{1... | collective-permute-start | bytes 983048 | tf_op jit(solution)/shard_map/ppermute | solution.py:446
  44.0 5.7 %collective-permute-start.6 = (f32[2,4,40,128]{3,2,1,0:T(8,128)S(1)}, f32[2,4,40,128]{3,2,1,0:T(8,128)S(1)}, u32[]{:S(2)}, u32[]{:S(2)}) collective-permute-start(f32[2,4,40,128]{3,2,1,0:T(8,128)S(1)} %slice.35), channel_id=1, source_target_pairs={{0,8},{1,5},{2,10},{3,7},{4,12},{5,1},{6,14},{7,3},{8,0},{9,13},{1... | collective-permute-start | bytes 491528 | tf_op jit(solution)/shard_map/ppermute | solution.py:446
  49.8 5.5 %collective-permute-start.7 = (f32[1,4,40,128]{3,2,1,0:T(8,128)S(1)}, f32[1,4,40,128]{3,2,1,0:T(8,128)S(1)}, u32[]{:S(2)}, u32[]{:S(2)}) collective-permute-start(f32[1,4,40,128]{3,2,1,0:T(8,128)S(1)} %slice.37), channel_id=1, source_target_pairs={{0,16},{1,17},{2,18},{3,19},{4,20},{5,21},{6,22},{7,23},{8,24},{9,... | collective-permute-start | bytes 245768 | tf_op jit(solution)/shard_map/ppermute | solution.py:446
